TPU v7x, 32 devices: a whole 2x2x4 slice. The times are simulated.
32 devices in a mesh: row: 8 (over y, x, core), col: 4 (over z).
Axes of the slice: x: 2, y: 2, z: 4, core: 2. Of those that a mesh axis runs over, the one named last changes fastest.
Arguments:
- columns: float32 [16384, 1024], P('row', 'col'), as said below
Outputs:
- factored: float32 [16384, 1024], P('row', 'col')
- projected: float32 [256, 1024], P(None, 'col')
Inputs may be any that keep to these rules, and one draw needn't show every extreme that they name: `columns`: the panel has full column rank and a condition number of at most about 40.
All inputs are finite; a program needn't handle non-finite values.
Results may differ from a plain program's by a relative error of at most 0.0003.
Values sent between devices are 32-bit elements; how exact they have to be, the bound alone decides.
No kernel may reach another device: no remote copies, remote signals or barrier semaphores. Data moves between devices by JAX's collectives and lax.ppermute only.
A program may use at most 64 MiB of HBM per device.

v0:
```python
import jax
import jax.numpy as jnp
from jax import lax
from jax.sharding import PartitionSpec as P


def spread(value, axis, source):
    kept = jnp.where(lax.axis_index(axis) == source, value, 0).astype(value.dtype)
    return lax.psum(kept, axis)


def cross_product(left, right):
    return lax.dot_general(
        left,
        right,
        (((0,), (0,)), ((), ())),
        precision=lax.Precision.HIGHEST,
        preferred_element_type=jnp.float32,
    )


def invert_lower(gram_sum):
    lower = jnp.linalg.cholesky(gram_sum)
    ident = jnp.eye(gram_sum.shape[0], dtype=jnp.float32)
    return jax.scipy.linalg.solve_triangular(lower, ident, lower=True)


def times_inverse(block, inverse):
    return jnp.dot(
        block, inverse.T, precision=lax.Precision.HIGHEST, preferred_element_type=jnp.float32
    )


def per_device(columns):
    at_root = lax.axis_index("col") == 0
    panel_rows = spread(columns, "col", 0)
    gram_sum, raw_proj = lax.psum(
        (cross_product(panel_rows, panel_rows), cross_product(panel_rows, columns)), "row"
    )
    inverse_low = invert_lower(gram_sum)
    sent_basis = times_inverse(panel_rows, inverse_low)
    projected = jnp.dot(
        inverse_low, raw_proj, precision=lax.Precision.HIGHEST, preferred_element_type=jnp.float32
    )
    remainder = columns - jnp.dot(
        sent_basis, projected, precision=lax.Precision.HIGHEST, preferred_element_type=jnp.float32
    )
    factored = jnp.where(at_root, sent_basis, remainder)
    return (factored, projected)


def solution(mesh):
    return jax.shard_map(
        per_device,
        mesh=mesh,
        in_specs=(P("row", "col"),),
        out_specs=(P("row", "col"), P(None, "col")),
        check_vma=False,
    )
```

profile of v0, /device:TPU:0, one launch (start us, length us, event | category | flops | bytes accessed | tf_op | source)
XLA Modules:
  0.0 239.8 jit_solution(14196477842423527275)
XLA Ops:
  7.2 0.0 all-reduce.5.cloned.1.call-start
  7.2 3.1 %broadcast_select_fusion = f32[2048,256]{1,0:T(8,128)} fusion(f32[2048,256]{1,0:T(8,128)} %param.1, pred[]{:T(512)S(6)} %eq.9), kind=kLoop, calls=%fused_computation.6 | loop fusion | flops 524288 | bytes 4194305 | tf_op jit(solution)/shard_map/jit(_where)/select_n | solution.py:8
  10.3 0.0 all-reduce.5.cloned.1.call-update
  10.3 0.0 all-reduce.7.cloned.1.call-start
  10.3 89.4 %all-reduce.5.cloned.1.call-done = f32[2048,256]{1,0:T(8,128)} async-done(((f32[2048,256]{1,0:T(8,128)}), f32[2048,256]{1,0:T(8,128)}) %all-reduce.5.cloned.1.call-update) | async-done | bytes 2097168 | tf_op jit(solution)/shard_map/psum | solution.py:9
  99.8 6.5 %fusion.15 = f32[256,256]{1,0:T(8,128)} fusion(f32[2048,256]{1,0:T(8,128)} %all-reduce.5.cloned.1.call-done, f32[2048,256]{1,0:T(8,128)} %param.1), kind=kOutput, calls=%fused_computation.38 | convolution fusion | flops 1610612736 | bytes 4456448 | tf_op jit(solution)/shard_map/dot_general | solution.py:13
  106.3 4.2 %fusion.14 = f32[256,256]{0,1:T(8,128)} fusion(f32[2048,256]{1,0:T(8,128)S(1)} %copy-done), kind=kOutput, calls=%fused_computation.37 | convolution fusion | flops 1610612736 | bytes 2359296 | tf_op jit(solution)/shard_map/dot_general | solution.py:13
  110.5 0.0 all-reduce.7.cloned.1.call-update
  110.6 54.0 %all-reduce.7.cloned.1.call-done = (f32[256,256]{0,1:T(8,128)}, f32[256,256]{1,0:T(8,128)}) async-done(((f32[256,256]{0,1:T(8,128)}, f32[256,256]{1,0:T(8,128)}), (f32[256,256]{0,1:T(8,128)}, f32[256,256]{1,0:T(8,128)})) %all-reduce.7.cloned.1.call-update) | async-done | bytes 524304 | tf_op jit(solution)/shard_map/psum | solution.py:37
  164.6 1.1 copy.4
  165.7 1.0 fusion.1
  166.7 11.7 %cholesky.50 = f32[128,128]{1,0:T(8,128)S(1)} custom-call(f32[128,128]{1,0:T(8,128)S(1)} %cholesky.118), custom_call_target="Cholesky" | custom-call | tf_op jit(solution)/shard_map/jit(cholesky)/cholesky | solution.py:23
  178.5 10.0 %custom-call.15 = f32[1,128,128]{1,2,0:T(8,128)S(1)} custom-call(f32[1,128,128]{2,1,0:T(8,128)S(1)} %get-tuple-element.25), custom_call_target="InvertDiagBlocksLowerTriangular" | custom-call | tf_op jit(solution)/shard_map/jit(cholesky)/cholesky | solution.py:23
  188.4 0.2 constant_dynamic-update-slice_fusion.1
  188.6 0.3 convolution_subtract_fusion.2
  188.9 11.7 %cholesky.105 = f32[128,128]{1,0:T(8,128)S(1)} custom-call(f32[128,128]{1,0:T(8,128)S(1)} %convolution_subtract_fusion.2), custom_call_target="Cholesky" | custom-call | tf_op jit(solution)/shard_map/jit(cholesky)/cholesky | solution.py:23
  200.7 0.6 compare_reduce_fusion
  202.7 0.1 triangular_solve.63
  202.7 4.0 %while.1 = (s32[]{:T(128)}, f32[256,256]{1,0:T(8,128)S(1)}, s32[2,2]{1,0:T(2,128)S(1)}, f32[2,128,128]{2,1,0:T(8,128)S(1)}, s32[]{:T(128)}) while((s32[]{:T(128)}, f32[256,256]{1,0:T(8,128)S(1)}, s32[2,2]{1,0:T(2,128)S(1)}, f32[2,128,128]{2,1,0:T(8,128)S(1)}, s32[]{:T(128)}) %tuple.27), condition=%wide.while_cond, body=%wide.while_body.sunk | while | flops 2 | bytes 131189 | solution.py:25
  202.7 0.6 fusion.29
  203.3 1.4 bitcast_dynamic-update-slice_fusion.2
  204.7 0.6 fusion.29
  205.3 1.4 bitcast_dynamic-update-slice_fusion.2
  206.7 19.7 %custom-call.16 = f32[2,128,128]{1,2,0:T(8,128)S(1)} custom-call(f32[2,128,128]{2,1,0:T(8,128)S(1)} %get-tuple-element.9), custom_call_target="InvertDiagBlocksLowerTriangular" | custom-call | tf_op jit(solution)/shard_map/jit(_solve_triangular)/triangular_solve | solution.py:25
  226.4 0.3 fusion.4
  226.7 0.3 convolution_subtract_fusion.1
  226.9 0.3 fusion.7
  227.3 0.4 fusion.2
  227.7 0.0 copy-start.2
  227.7 0.0 copy-start.1
  227.7 1.9 fusion.3
  229.7 3.3 %fusion = f32[2048,256]{1,0:T(8,128)} fusion(f32[2048,256]{1,0:T(8,128)S(1)} %fusion.3, f32[2048,256]{1,0:T(8,128)S(1)} %copy-done.1, f32[256,256]{1,0:T(8,128)S(1)} %fusion.2, pred[]{:T(512)S(6)} %eq.9), kind=kOutput, calls=%fused_computation.3 | convolution fusion | flops 1611661312 | bytes 6553601 | tf_op jit(solution)/shard_map/dot_general | solution.py:45
  (16 shorter events, 0.2 us)
Async XLA Ops:
  7.2 92.6 %all-reduce.5.cloned.1.call-start = ((), (), s32[]{:S(2)}) async-start(), calls=%async_computation | async-start | bytes 4194304 | tf_op jit(solution)/shard_map/psum | solution.py:9
  10.3 154.3 %all-reduce.7.cloned.1.call-start = ((), (), s32[]{:S(2)}) async-start(), calls=%async_computation.1 | async-start | bytes 1048576 | tf_op jit(solution)/shard_map/psum | solution.py:37
  99.8 6.5 %copy-start = (f32[2048,256]{1,0:T(8,128)S(1)}, f32[2048,256]{1,0:T(8,128)}, u32[]{:S(2)}) copy-start(f32[2048,256]{1,0:T(8,128)} %all-reduce.5.cloned.1.call-done) | copy-start | bytes 6291460
  165.7 61.6 %copy-start.3 = (f32[256,256]{1,0:T(8,128)S(1)}, f32[256,256]{1,0:T(8,128)}, u32[]{:S(2)}) copy-start(f32[256,256]{1,0:T(8,128)} %get-tuple-element.19) | copy-start | bytes 786436
  227.7 2.0 copy-start.2
  227.7 2.0 copy-start.1
Sparse Core Ops, SparseCore 0:
  10.9 88.8 all-reduce.4
  110.6 53.8 all-reduce.6
where the time goes:
time: 240 us
  waiting for transfers between devices  143 us (60%)
  other arithmetic  57.9 us (24%)
  matrix products  17.6 us (7%)
  between operations  15.5 us (6%)
  local copies, waits for them, and re-layouts  5.15 us (2%)
    psum x1, waiting for transfers between devices, spread(): return lax.psum(kept, axis)  89.4 us
    psum x1, waiting for transfers between devices, per_device(): lax.psum((cross_product(panel_rows, panel_rows), cross_product(panel_rows...  54 us
    another operation x6, other arithmetic, invert_lower(): lower = jnp.linalg.cholesky(gram_sum)  34.1 us
    another operation x3, other arithmetic, invert_lower(): return jax.scipy.linalg.solve_triangular(lower, ident, lower=True)  19.7 us
    dot_general x2, matrix products, cross_product(): lax.dot_general(left, right, (((0,), (0,)), ((), ())), precision=lax.Prec...  10.7 us
  transfers between devices with their start and end apart: 2, of which 2 were waited for; matrix products, arithmetic and copies ran while one was open for 0% of the time, Pallas kernels for 0%

commit v1 on v0

v1 whole, which is shorter than its diff:
```python
import jax
import jax.numpy as jnp
from jax import lax
from jax.experimental import pallas as pl
from jax.experimental.pallas import tpu as pltpu
from jax.sharding import PartitionSpec as P


CHUNKS = 8
GROUPS = ((0, 1, 2, 3), (4, 5, 6), (7,))
TILE = 64
F32 = jnp.float32
BF16 = jnp.bfloat16
VMEM = pl.BlockSpec(memory_space=pltpu.VMEM)
SMEM = pl.BlockSpec(memory_space=pltpu.SMEM)
ANY = pl.BlockSpec(memory_space=pl.ANY)
NN = ((1,), (0,))
TN = ((0,), (0,))


def fine(left, right, dims=NN):
    return lax.dot_general(left, right, (dims, ((), ())), precision=lax.Precision.HIGHEST, preferred_element_type=F32)


def split(value):
    high = value.astype(BF16)
    return high, (value - high.astype(F32)).astype(BF16)


def three(left, right, dims=NN):
    one = lambda a, b: lax.dot_general(a, b, (dims, ((), ())), preferred_element_type=F32)
    return one(left[0], right[0]) + (one(left[0], right[1]) + one(left[1], right[0]))


def gram_kernel(block_ref, out_ref):
    pair = split(block_ref[...])
    part = three(pair, pair, TN)

    @pl.when(pl.program_id(0) == 0)
    def _():
        out_ref[...] = part

    @pl.when(pl.program_id(0) > 0)
    def _():
        out_ref[...] += part


def gram_of(columns):
    rows, width = columns.shape
    step = rows // CHUNKS
    return pl.pallas_call(
        gram_kernel,
        out_shape=jax.ShapeDtypeStruct((width, width), F32),
        grid=(CHUNKS,),
        in_specs=[pl.BlockSpec((step, width), lambda k: (k, 0))],
        out_specs=pl.BlockSpec((width, width), lambda k: (0, 0)),
        name="gram",
    )(columns)


def eliminate(tile, size):
    lanes = tile.shape[1]
    row = lax.broadcasted_iota(jnp.int32, (size, 1), 0)
    for j in range(0, size, 2):
        low = j // 8 * 8
        tail, at = tile[low:], row[low:]
        k, count = j - low, size - low
        c0 = jnp.broadcast_to(tail[:, j : j + 1], (count, lanes))
        c1 = jnp.broadcast_to(tail[:, j + 1 : j + 2], (count, lanes))
        p00, p01, p11 = c0[k : k + 1], c1[k : k + 1], c1[k + 1 : k + 2]
        r0, r1 = tail[k : k + 1], tail[k + 1 : k + 2]
        scale = 1.0 / (p00 * p11 - p01 * p01)
        q0 = (p11 * r0 - p01 * r1) * scale
        q1 = (p00 * r1 - p01 * r0) * scale
        inner = r0 * (p01 * (1.0 / p00))
        tail = tail - jnp.where(at > j + 1, c0 * q0 + c1 * q1, jnp.where(at == j + 1, inner, 0.0))
        tile = tail if low == 0 else jnp.concatenate([tile[:low], tail], axis=0)
    return tile


def identity(size):
    shape = (size, size)
    same = lax.broadcasted_iota(jnp.int32, shape, 0) == lax.broadcasted_iota(jnp.int32, shape, 1)
    return jnp.where(same, 1.0, 0.0).astype(F32)


def factor_kernel(flag_ref, gram_ref, out_ref, work_ref):
    width = gram_ref.shape[0]

    @pl.when(flag_ref[0] == 1)
    def _():
        work_ref[:, :width] = gram_ref[...]
        work_ref[:, width:] = identity(width)
        eye = identity(TILE)
        for start in range(0, width, TILE):
            end = start + TILE
            tile = jnp.concatenate([work_ref[start:end, start:end], eye], axis=1)
            tile = eliminate(tile, TILE)
            pivots = jnp.sum(tile[:, :TILE] * eye, axis=1, keepdims=True)
            block = fine(tile[:, TILE:] * lax.rsqrt(pivots), work_ref[start:end, :])
            work_ref[start:end, :] = block
            if end < width:
                work_ref[end:, :] = work_ref[end:, :] - fine(block[:, end:width], block, TN)
        out_ref[...] = work_ref[:, width:]


def inverse_of(flag, gram):
    width = gram.shape[0]
    return pl.pallas_call(
        factor_kernel,
        out_shape=jax.ShapeDtypeStruct((width, width), F32),
        in_specs=[SMEM, VMEM],
        out_specs=VMEM,
        scratch_shapes=[pltpu.VMEM((width, 2 * width), F32)],
        name="factor",
    )(flag, gram)


def gather_kernel(first, count, hops, step, flag_ref, *refs):
    columns_ref, before_ref = refs[:2]
    moved = refs[2 : 2 + count * hops]
    sum_ref, high_ref, low_ref = refs[2 + count * hops :]
    total = before_ref[...] if first > 0 else None
    for c in range(count):
        block = columns_ref[(first + c) * step : (first + c + 1) * step, :]
        parts = [ref[...] for ref in moved[c * hops : (c + 1) * hops]]
        got = sum(parts[1:], parts[0]) if parts else block
        pair = split(jnp.where(flag_ref[0] == 1, block, got))
        high_ref[c * step : (c + 1) * step, :] = pair[0]
        low_ref[c * step : (c + 1) * step, :] = pair[1]
        part = three(pair, split(block), TN)
        total = part if total is None else total + part
    sum_ref[...] = total


def gather(flag, columns, before, moved, first):
    count, hops, step = len(moved), len(moved[0]), columns.shape[0] // CHUNKS
    width = columns.shape[1]
    flat = [m for ms in moved for m in ms]
    return pl.pallas_call(
        lambda *refs: gather_kernel(first, count, hops, step, *refs),
        out_shape=(
            jax.ShapeDtypeStruct((width, width), F32),
            jax.ShapeDtypeStruct((count * step, width), BF16),
            jax.ShapeDtypeStruct((count * step, width), BF16),
        ),
        in_specs=[SMEM] + [VMEM] * (2 + len(flat)),
        out_specs=(VMEM, VMEM, VMEM),
    )(flag, columns, before, *flat)


def finish_kernel(groups, hops, flag_ref, own_ref, gram_ref, total_ref, columns_ref, *refs):
    moved = refs[:hops]
    pairs = refs[hops : hops + 2 * len(groups)]
    out_ref, projected_ref, buffer_ref, sem = refs[hops + 2 * len(groups) :]
    root = flag_ref[0] == 1
    got = own_ref[...]
    if hops:
        parts = [ref[...] for ref in moved]
        got = jnp.where(root, got, sum(parts[1:], parts[0]))
    projected = fine(got, jnp.where(root, gram_ref[...], total_ref[...]))
    projected_ref[...] = projected
    weight = split(jnp.where(root, -got.T, fine(got, projected, TN)))
    step = columns_ref.shape[0] // CHUNKS
    copies = []
    for g, group in enumerate(groups):
        for c, chunk in enumerate(group):
            here = pl.ds(c * step, step)
            there = pl.ds(chunk * step, step)
            pair = (pairs[2 * g][here, :], pairs[2 * g + 1][here, :])
            base = jnp.where(root, 0.0, columns_ref[there, :])
            buffer_ref[there, :] = base - three(pair, weight)
            copies.append(pltpu.make_async_copy(buffer_ref.at[there, :], out_ref.at[there, :], sem.at[chunk]))
            copies[-1].start()
    for copy in copies:
        copy.wait()


def finish(flag, own, gram, total, columns, moved, pairs):
    rows, width = columns.shape
    return pl.pallas_call(
        lambda *refs: finish_kernel(GROUPS, len(moved), *refs),
        out_shape=(jax.ShapeDtypeStruct((rows, width), F32), jax.ShapeDtypeStruct((width, width), F32)),
        in_specs=[SMEM] + [VMEM] * (4 + len(moved) + len(pairs)),
        out_specs=(ANY, VMEM),
        scratch_shapes=[pltpu.VMEM((rows, width), F32), pltpu.SemaphoreType.DMA((CHUNKS,))],
        name="finish",
    )(flag, own, gram, total, columns, *moved, *pairs)


def exchange_sum(value, rows, cols, members):
    axes = ("row", "col")
    odd = lax.axis_index("row") % 2 == 1

    def swap(part, bit):
        pairs = [(r * cols + c, (r ^ bit) * cols + c) for r in range(rows) for c in members]
        return lax.ppermute(part, axes, pairs)

    half = value.shape[0] // 2
    low, high = value[:half], value[half:]
    mine = jnp.where(odd, high, low) + swap(jnp.where(odd, low, high), 1)
    bit = 2
    while bit < rows:
        mine = mine + swap(mine, bit)
        bit *= 2
    other = swap(mine, 1)
    return jnp.concatenate([jnp.where(odd, other, mine), jnp.where(odd, mine, other)], axis=0)


def spread(value, cols):
    mid = cols // 2
    held = lax.ppermute(value, "col", [(0, mid)])
    parts = [held]
    for step in range(1, mid + 1):
        pairs = [(mid + step - 1, mid + step), (mid - step + 1, mid - step)]
        pairs = [p for p in pairs if 0 < p[1] < cols]
        if not pairs:
            break
        if step == 1:
            sent = []
            for pair in pairs:
                sent.append(lax.ppermute(held, "col", [pair]))
            parts += sent
            held = sum(sent[1:], sent[0])
        else:
            held = lax.ppermute(held, "col", pairs)
            parts.append(held)
    return parts


def solution(mesh):
    rows, cols = mesh.shape["row"], mesh.shape["col"]

    def per_device(columns):
        step = columns.shape[0] // CHUNKS
        flag = (lax.axis_index("col") == 0).astype(jnp.int32).reshape(1)
        moved = [spread(columns[c * step : (c + 1) * step], cols) for c in range(CHUNKS)]
        gram = gram_of(columns)
        gram = exchange_sum(gram, rows, cols, (0,))
        inverse = inverse_of(flag, gram)
        sent = []
        for c in range(1, cols):
            sent.append(lax.ppermute(inverse, "col", [(0, c)]))
        total, pairs = gram, []
        for group in GROUPS:
            total, *pair = gather(flag, columns, total, [moved[c] for c in group], group[0])
            pairs += pair
        total = exchange_sum(total, rows, cols, tuple(range(1, cols)))
        return tuple(finish(flag, inverse, gram, total, columns, sent, pairs))

    return jax.shard_map(
        per_device, mesh=mesh, in_specs=(P("row", "col"),), out_specs=(P("row", "col"), P(None, "col")), check_vma=False
    )
```

time: 240 us -> 158 us (0.66)
  waiting for transfers between devices: 143 us -> 28.5 us
  starting transfers between devices: 0.08 us -> 81.2 us
  other arithmetic: 57.9 us -> 5.45 us
  Pallas kernels: 0 us -> 39.9 us
  matrix products: 17.6 us -> 0 us
  between operations: 15.5 us -> 1.18 us
  local copies, waits for them, and re-layouts: 5.15 us -> 0.89 us
    psum x2 -> x0, waiting for transfers between devices: 143 us -> none  [the longest x1 89.4 us: spread(): return lax.psum(kept, axis)]
    ppermute x0 -> x35, starting transfers between devices: none -> 81.2 us  [the longest x3 25.6 us: per_device(): sent.append(lax.ppermute(inverse, 'col', [(0, c)]))]
    another operation x9 -> x0, other arithmetic: 53.8 us -> none  [the longest x6 34.1 us: invert_lower(): lower = jnp.linalg.cholesky(gram_sum)]
    pallas_call x0 -> x6, Pallas kernels: none -> 39.9 us  [the longest x1 16.5 us: inverse_of(): pl.pallas_call(factor_kernel, out_shape=jax.ShapeDtypeStruct((width, widt...]
    ppermute x0 -> x35, waiting for transfers between devices: none -> 28.5 us  [the longest x3 14.4 us: per_device(): sent.append(lax.ppermute(inverse, 'col', [(0, c)]))]
    dot_general x5 -> x0, matrix products: 16.3 us -> none  [the longest x2 10.7 us: cross_product(): lax.dot_general(left, right, (((0,), (0,)), ((), ())), precision=lax.Prec...]
    another operation x9 -> x0, local copies, waits for them, and re-layouts: 4.05 us -> none
  transfers between devices with their start and end apart: 2 -> 35, of which waited for: 2 -> 9; matrix products, arithmetic and copies ran while one was open for 0% -> 2% of each run, Pallas kernels for 0% -> 15%
where the time goes in v1:
time: 158 us; the launch traced here: 157 us
  starting transfers between devices  81.2 us (51%)
  Pallas kernels  39.9 us (25%)
  waiting for transfers between devices  28.5 us (18%)
  other arithmetic  5.45 us (3%)
    ppermute x3, starting transfers between devices, per_device(): sent.append(lax.ppermute(inverse, 'col', [(0, c)]))  25.6 us
    ppermute x8, starting transfers between devices, spread(): held = lax.ppermute(value, 'col', [(0, mid)])  23.9 us
    ppermute x16, starting transfers between devices, spread(): sent.append(lax.ppermute(held, 'col', [pair]))  17.7 us
    pallas_call x1, Pallas kernels, inverse_of(): pl.pallas_call(factor_kernel, out_shape=jax.ShapeDtypeStruct((width, widt...  16.5 us
    ppermute x3, waiting for transfers between devices, per_device(): sent.append(lax.ppermute(inverse, 'col', [(0, c)]))  14.4 us
    ppermute x8, starting transfers between devices, swap(): return lax.ppermute(part, axes, pairs)  14 us
    ppermute x8, waiting for transfers between devices, spread(): held = lax.ppermute(value, 'col', [(0, mid)])  12 us
    pallas_call x3, Pallas kernels, gather(): pl.pallas_call(lambda *refs: gather_kernel(first, count, hops, step, *ref...  10.6 us
  transfers between devices with their start and end apart: 35, of which 9 were waited for; matrix products, arithmetic and copies ran while one was open for 2% of the time, Pallas kernels for 15%

profile of v1, /device:TPU:0, one launch (start us, length us, event | category | flops | bytes accessed | tf_op | source)
XLA Modules:
  0.0 157.2 jit_solution(17337865894306689192)
XLA Ops:
  0.7 6.4 %gram.1 = f32[256,256]{1,0:T(8,128)} custom-call(f32[2048,256]{1,0:T(8,128)} %refs_4_.1), custom_call_target="tpu_custom_call" | custom-call | tf_op jit(solution)/shard_map/gram/pallas_call | solution.py:51
  8.1 2.5 %collective-permute-start = (f32[128,256]{1,0:T(8,128)S(1)}, f32[128,256]{1,0:T(8,128)S(1)}, u32[]{:S(2)}, u32[]{:S(2)}) collective-permute-start(f32[128,256]{1,0:T(8,128)S(1)} %slice_select_fusion), channel_id=1, source_target_pairs={{0,4},{4,0},{8,12},{12,8},{16,20},{20,16},{24,28},{28,24}} | collective-permute-start | bytes 393224 | tf_op jit(solution)/shard_map/ppermute | solution.py:197
  10.8 4.3 %collective-permute-start.10 = (f32[256,256]{1,0:T(8,128)S(1)}, f32[256,256]{1,0:T(8,128)S(1)}, u32[]{:S(2)}, u32[]{:S(2)}) collective-permute-start(f32[256,256]{1,0:T(8,128)S(1)} %get-tuple-element.25), channel_id=1, source_target_pairs={{0,2},{4,6},{8,10},{12,14},{16,18},{20,22},{24,26},{28,30}} | collective-permute-start | bytes 786440 | tf_op jit(solution)/shard_map/ppermute | solution.py:212
  17.7 3.4 %collective-permute-start.1 = (f32[128,256]{1,0:T(8,128)S(1)}, f32[128,256]{1,0:T(8,128)S(1)}, u32[]{:S(2)}, u32[]{:S(2)}) collective-permute-start(f32[128,256]{1,0:T(8,128)S(1)} %select_add_fusion.1), channel_id=1, source_target_pairs={{0,8},{4,12},{8,0},{12,4},{16,24},{20,28},{24,16},{28,20}} | collective-permute-start | bytes 393224 | tf_op jit(solution)/shard_map/ppermute | solution.py:197
  22.4 2.1 %collective-permute-done.1 = f32[128,256]{1,0:T(8,128)S(1)} collective-permute-done((f32[128,256]{1,0:T(8,128)S(1)}, f32[128,256]{1,0:T(8,128)S(1)}, u32[]{:S(2)}, u32[]{:S(2)}) %collective-permute-start.1) | collective-permute-done | bytes 131104 | tf_op jit(solution)/shard_map/ppermute | solution.py:197
  25.9 3.4 %collective-permute-start.2 = (f32[128,256]{1,0:T(8,128)S(1)}, f32[128,256]{1,0:T(8,128)S(1)}, u32[]{:S(2)}, u32[]{:S(2)}) collective-permute-start(f32[128,256]{1,0:T(8,128)S(1)} %add.25), channel_id=1, source_target_pairs={{0,16},{4,20},{8,24},{12,28},{16,0},{20,4},{24,8},{28,12}} | collective-permute-start | bytes 393224 | tf_op jit(solution)/shard_map/ppermute | solution.py:197
  29.4 3.2 %collective-permute-start.19 = (f32[256,256]{1,0:T(8,128)S(1)}, f32[256,256]{1,0:T(8,128)S(1)}, u32[]{:S(2)}, u32[]{:S(2)}) collective-permute-start(f32[256,256]{1,0:T(8,128)S(1)} %get-tuple-element.22), channel_id=1, source_target_pairs={{0,2},{4,6},{8,10},{12,14},{16,18},{20,22},{24,26},{28,30}} | collective-permute-start | bytes 786440 | tf_op jit(solution)/shard_map/ppermute | solution.py:212
  32.9 5.3 %collective-permute-start.22 = (f32[256,256]{1,0:T(8,128)S(1)}, f32[256,256]{1,0:T(8,128)S(1)}, u32[]{:S(2)}, u32[]{:S(2)}) collective-permute-start(f32[256,256]{1,0:T(8,128)S(1)} %get-tuple-element.21), channel_id=1, source_target_pairs={{0,2},{4,6},{8,10},{12,14},{16,18},{20,22},{24,26},{28,30}} | collective-permute-start | bytes 786440 | tf_op jit(solution)/shard_map/ppermute | solution.py:212
  38.5 6.0 %collective-permute-start.25 = (f32[256,256]{1,0:T(8,128)S(1)}, f32[256,256]{1,0:T(8,128)}, u32[]{:S(2)}, u32[]{:S(2)}) collective-permute-start(f32[256,256]{1,0:T(8,128)S(1)} %get-tuple-element.20), channel_id=1, source_target_pairs={{0,2},{4,6},{8,10},{12,14},{16,18},{20,22},{24,26},{28,30}} | collective-permute-start | bytes 786440 | tf_op jit(solution)/shard_map/ppermute | solution.py:212
  45.3 1.9 %collective-permute-start.3 = (f32[128,256]{1,0:T(8,128)S(1)}, f32[128,256]{1,0:T(8,128)}, u32[]{:S(2)}, u32[]{:S(2)}) collective-permute-start(f32[128,256]{1,0:T(8,128)S(1)} %add.26), channel_id=1, source_target_pairs={{0,4},{4,0},{8,12},{12,8},{16,20},{20,16},{24,28},{28,24}} | collective-permute-start | bytes 393224 | tf_op jit(solution)/shard_map/ppermute | solution.py:197
  47.2 2.6 %collective-permute-done.19.refs_6_ = f32[256,256]{1,0:T(8,128)S(1)} collective-permute-done((f32[256,256]{1,0:T(8,128)S(1)}, f32[256,256]{1,0:T(8,128)S(1)}, u32[]{:S(2)}, u32[]{:S(2)}) %collective-permute-start.19) | collective-permute-done | bytes 262176 | tf_op jit(solution)/shard_map/ppermute | solution.py:212
  50.5 4.9 %collective-permute-done.22.refs_9_ = f32[256,256]{1,0:T(8,128)S(1)} collective-permute-done((f32[256,256]{1,0:T(8,128)S(1)}, f32[256,256]{1,0:T(8,128)S(1)}, u32[]{:S(2)}, u32[]{:S(2)}) %collective-permute-start.22) | collective-permute-done | bytes 262176 | tf_op jit(solution)/shard_map/ppermute | solution.py:212
  56.1 3.8 %collective-permute-done.25.refs_3_ = f32[256,256]{1,0:T(8,128)} collective-permute-done((f32[256,256]{1,0:T(8,128)S(1)}, f32[256,256]{1,0:T(8,128)}, u32[]{:S(2)}, u32[]{:S(2)}) %collective-permute-start.25) | collective-permute-done | bytes 262176 | tf_op jit(solution)/shard_map/ppermute | solution.py:212
  62.0 1.4 collective-permute-start.8
  63.4 1.4 collective-permute-start.9
  64.7 1.4 collective-permute-start.17
  66.1 1.4 collective-permute-start.18
  67.5 1.4 collective-permute-start.20
  68.8 1.4 collective-permute-start.21
  70.2 1.4 collective-permute-start.23
  71.6 1.4 collective-permute-start.24
  73.0 1.3 collective-permute-start.26
  74.3 1.4 collective-permute-start.27
  77.4 4.2 %shard_map.30 = (f32[256,256]{1,0:T(8,128)}, bf16[1024,256]{1,0:T(8,128)(2,1)}, bf16[1024,256]{1,0:T(8,128)(2,1)}) custom-call(s32[1]{0:T(128)} %bitcast.flag_ref.refs_0_, f32[2048,256]{1,0:T(8,128)} %refs_4_.1, f32[256,256]{1,0:T(8,128)} %pad_maximum_fusion.gram_ref.refs_2_, f32[256,256]{1,0:T(8,128)} %copy-done.5, f32[256,256]{1,0:T(8,128)} %copy-done.13, ...), custom_call_target="tpu_custom_call" | custom-call | tf_op jit(solution)/shard_map/pallas_call | solution.py:140
  81.6 3.6 %shard_map.31 = (f32[256,256]{1,0:T(8,128)}, bf16[768,256]{1,0:T(8,128)(2,1)}, bf16[768,256]{1,0:T(8,128)(2,1)}) custom-call(s32[1]{0:T(128)} %bitcast.flag_ref.refs_0_, f32[2048,256]{1,0:T(8,128)} %refs_4_.1, f32[256,256]{1,0:T(8,128)} %get-tuple-element.11.refs_2_, f32[256,256]{1,0:T(8,128)} %copy-done.4, f32[256,256]{1,0:T(8,128)} %collective-permute-done.17.refs_4_, ...), custom_call_target="tpu_custom_call" | custom-call | tf_op jit(solution)/shard_map/pallas_call | solution.py:140
  85.3 2.9 %shard_map.32 = (f32[256,256]{1,0:T(8,128)}, bf16[256,256]{1,0:T(8,128)(2,1)}, bf16[256,256]{1,0:T(8,128)(2,1)}) custom-call(s32[1]{0:T(128)} %bitcast.flag_ref.refs_0_, f32[2048,256]{1,0:T(8,128)} %refs_4_.1, f32[256,256]{1,0:T(8,128)} %get-tuple-element.12.refs_2_, f32[256,256]{1,0:T(8,128)} %collective-permute-done.25.refs_3_, ...), custom_call_target="tpu_custom_call" | custom-call | tf_op jit(solution)/shard_map/pallas_call | solution.py:140
  92.9 16.5 %factor.1.refs_1_ = f32[256,256]{1,0:T(8,128)} custom-call(s32[1]{0:T(128)} %bitcast.flag_ref.refs_0_, f32[256,256]{1,0:T(8,128)} %pad_maximum_fusion.gram_ref.refs_2_), custom_call_target="tpu_custom_call" | custom-call | tf_op jit(solution)/shard_map/factor/pallas_call | solution.py:109
  109.4 23.0 %collective-permute-start.32 = (f32[256,256]{1,0:T(8,128)}, f32[256,256]{1,0:T(8,128)S(1)}, u32[]{:S(2)}, u32[]{:S(2)}) collective-permute-start(f32[256,256]{1,0:T(8,128)} %factor.1.refs_1_), channel_id=1, source_target_pairs={{0,1},{4,5},{8,9},{12,13},{16,17},{20,21},{24,25},{28,29}} | collective-permute-start | bytes 786440 | tf_op jit(solution)/shard_map/ppermute | solution.py:243
  135.8 3.6 %collective-permute-done.32.refs_5_ = f32[256,256]{1,0:T(8,128)S(1)} collective-permute-done((f32[256,256]{1,0:T(8,128)}, f32[256,256]{1,0:T(8,128)S(1)}, u32[]{:S(2)}, u32[]{:S(2)}) %collective-permute-start.32) | collective-permute-done | bytes 262176 | tf_op jit(solution)/shard_map/ppermute | solution.py:243
  139.4 5.6 %collective-permute-done.33.refs_6_ = f32[256,256]{1,0:T(8,128)S(1)} collective-permute-done((f32[256,256]{1,0:T(8,128)}, f32[256,256]{1,0:T(8,128)S(1)}, u32[]{:S(2)}, u32[]{:S(2)}) %collective-permute-start.33) | collective-permute-done | bytes 262176 | tf_op jit(solution)/shard_map/ppermute | solution.py:243
  145.0 5.1 %collective-permute-done.34.refs_7_ = f32[256,256]{1,0:T(8,128)S(1)} collective-permute-done((f32[256,256]{1,0:T(8,128)}, f32[256,256]{1,0:T(8,128)S(1)}, u32[]{:S(2)}, u32[]{:S(2)}) %collective-permute-start.34) | collective-permute-done | bytes 262176 | tf_op jit(solution)/shard_map/ppermute | solution.py:243
  150.8 6.3 %finish.1 = (f32[2048,256]{1,0:T(8,128)}, f32[256,256]{1,0:T(8,128)}) custom-call(s32[1]{0:T(128)} %bitcast.flag_ref.refs_0_, f32[256,256]{1,0:T(8,128)} %factor.1.refs_1_, f32[256,256]{1,0:T(8,128)} %pad_maximum_fusion.gram_ref.refs_2_, f32[256,256]{1,0:T(8,128)} %pad_maximum_fusion.1.refs_3_, f32[2048,256]{1,0:T(8,128)} %refs_4_.1, f32[256,256]{1,0:T(8,128)} %copy-done.15, ...), custom_call_target="tpu_custom_call" | custom-call | tf_op jit(solution)/shard_map/finish/pallas_call | solution.py:181
  (93 shorter events, 21.6 us)
Async XLA Ops:
  8.1 9.6 %collective-permute-start = (f32[128,256]{1,0:T(8,128)S(1)}, f32[128,256]{1,0:T(8,128)S(1)}, u32[]{:S(2)}, u32[]{:S(2)}) collective-permute-start(f32[128,256]{1,0:T(8,128)S(1)} %slice_select_fusion), channel_id=1, source_target_pairs={{0,4},{4,0},{8,12},{12,8},{16,20},{20,16},{24,28},{28,24}} | collective-permute-start | bytes 393224 | tf_op jit(solution)/shard_map/ppermute | solution.py:197
  10.8 15.1 %collective-permute-start.10 = (f32[256,256]{1,0:T(8,128)S(1)}, f32[256,256]{1,0:T(8,128)S(1)}, u32[]{:S(2)}, u32[]{:S(2)}) collective-permute-start(f32[256,256]{1,0:T(8,128)S(1)} %get-tuple-element.25), channel_id=1, source_target_pairs={{0,2},{4,6},{8,10},{12,14},{16,18},{20,22},{24,26},{28,30}} | collective-permute-start | bytes 786440 | tf_op jit(solution)/shard_map/ppermute | solution.py:212
  15.0 14.3 %collective-permute-start.13 = (f32[256,256]{1,0:T(8,128)S(1)}, f32[256,256]{1,0:T(8,128)S(1)}, u32[]{:S(2)}, u32[]{:S(2)}) collective-permute-start(f32[256,256]{1,0:T(8,128)S(1)} %get-tuple-element.24), channel_id=1, source_target_pairs={{0,2},{4,6},{8,10},{12,14},{16,18},{20,22},{24,26},{28,30}} | collective-permute-start | bytes 786440 | tf_op jit(solution)/shard_map/ppermute | solution.py:212
  16.3 16.6 %collective-permute-start.4 = (f32[256,256]{1,0:T(8,128)S(1)}, f32[256,256]{1,0:T(8,128)S(1)}, u32[]{:S(2)}, u32[]{:S(2)}) collective-permute-start(f32[256,256]{1,0:T(8,128)S(1)} %get-tuple-element.27), channel_id=1, source_target_pairs={{0,2},{4,6},{8,10},{12,14},{16,18},{20,22},{24,26},{28,30}} | collective-permute-start | bytes 786440 | tf_op jit(solution)/shard_map/ppermute | solution.py:212
  17.7 6.9 %collective-permute-start.1 = (f32[128,256]{1,0:T(8,128)S(1)}, f32[128,256]{1,0:T(8,128)S(1)}, u32[]{:S(2)}, u32[]{:S(2)}) collective-permute-start(f32[128,256]{1,0:T(8,128)S(1)} %select_add_fusion.1), channel_id=1, source_target_pairs={{0,8},{4,12},{8,0},{12,4},{16,24},{20,28},{24,16},{28,20}} | collective-permute-start | bytes 393224 | tf_op jit(solution)/shard_map/ppermute | solution.py:197
  21.1 17.4 %collective-permute-start.7 = (f32[256,256]{1,0:T(8,128)S(1)}, f32[256,256]{1,0:T(8,128)S(1)}, u32[]{:S(2)}, u32[]{:S(2)}) collective-permute-start(f32[256,256]{1,0:T(8,128)S(1)} %get-tuple-element.26), channel_id=1, source_target_pairs={{0,2},{4,6},{8,10},{12,14},{16,18},{20,22},{24,26},{28,30}} | collective-permute-start | bytes 786440 | tf_op jit(solution)/shard_map/ppermute | solution.py:212
  24.6 20.7 %collective-permute-start.16 = (f32[256,256]{1,0:T(8,128)S(1)}, f32[256,256]{1,0:T(8,128)S(1)}, u32[]{:S(2)}, u32[]{:S(2)}) collective-permute-start(f32[256,256]{1,0:T(8,128)S(1)} %get-tuple-element.23), channel_id=1, source_target_pairs={{0,2},{4,6},{8,10},{12,14},{16,18},{20,22},{24,26},{28,30}} | collective-permute-start | bytes 786440 | tf_op jit(solution)/shard_map/ppermute | solution.py:212
  25.9 18.6 %collective-permute-start.2 = (f32[128,256]{1,0:T(8,128)S(1)}, f32[128,256]{1,0:T(8,128)S(1)}, u32[]{:S(2)}, u32[]{:S(2)}) collective-permute-start(f32[128,256]{1,0:T(8,128)S(1)} %add.25), channel_id=1, source_target_pairs={{0,16},{4,20},{8,24},{12,28},{16,0},{20,4},{24,8},{28,12}} | collective-permute-start | bytes 393224 | tf_op jit(solution)/shard_map/ppermute | solution.py:197
  29.4 20.4 %collective-permute-start.19 = (f32[256,256]{1,0:T(8,128)S(1)}, f32[256,256]{1,0:T(8,128)S(1)}, u32[]{:S(2)}, u32[]{:S(2)}) collective-permute-start(f32[256,256]{1,0:T(8,128)S(1)} %get-tuple-element.22), channel_id=1, source_target_pairs={{0,2},{4,6},{8,10},{12,14},{16,18},{20,22},{24,26},{28,30}} | collective-permute-start | bytes 786440 | tf_op jit(solution)/shard_map/ppermute | solution.py:212
  32.9 22.5 %collective-permute-start.22 = (f32[256,256]{1,0:T(8,128)S(1)}, f32[256,256]{1,0:T(8,128)S(1)}, u32[]{:S(2)}, u32[]{:S(2)}) collective-permute-start(f32[256,256]{1,0:T(8,128)S(1)} %get-tuple-element.21), channel_id=1, source_target_pairs={{0,2},{4,6},{8,10},{12,14},{16,18},{20,22},{24,26},{28,30}} | collective-permute-start | bytes 786440 | tf_op jit(solution)/shard_map/ppermute | solution.py:212
  38.5 21.3 %collective-permute-start.25 = (f32[256,256]{1,0:T(8,128)S(1)}, f32[256,256]{1,0:T(8,128)}, u32[]{:S(2)}, u32[]{:S(2)}) collective-permute-start(f32[256,256]{1,0:T(8,128)S(1)} %get-tuple-element.20), channel_id=1, source_target_pairs={{0,2},{4,6},{8,10},{12,14},{16,18},{20,22},{24,26},{28,30}} | collective-permute-start | bytes 786440 | tf_op jit(solution)/shard_map/ppermute | solution.py:212
  44.5 16.7 %collective-permute-start.11 = (f32[256,256]{1,0:T(8,128)S(1)}, f32[256,256]{1,0:T(8,128)S(1)}, u32[]{:S(2)}, u32[]{:S(2)}) collective-permute-start(f32[256,256]{1,0:T(8,128)S(1)} %collective-permute-done.10.refs_9_), channel_id=1, source_target_pairs={{2,3},{6,7},{10,11},{14,15},{18,19},{22,23},{26,27},{30,31}} | collective-permute-start | bytes 786440 | tf_op jit(solution)/shard_map/ppermute | solution.py:222
  45.3 15.3 %collective-permute-start.3 = (f32[128,256]{1,0:T(8,128)S(1)}, f32[128,256]{1,0:T(8,128)}, u32[]{:S(2)}, u32[]{:S(2)}) collective-permute-start(f32[128,256]{1,0:T(8,128)S(1)} %add.26), channel_id=1, source_target_pairs={{0,4},{4,0},{8,12},{12,8},{16,20},{20,16},{24,28},{28,24}} | collective-permute-start | bytes 393224 | tf_op jit(solution)/shard_map/ppermute | solution.py:197
  49.8 12.2 %collective-permute-start.12 = (f32[256,256]{1,0:T(8,128)S(1)}, f32[256,256]{1,0:T(8,128)S(1)}, u32[]{:S(2)}, u32[]{:S(2)}) collective-permute-start(f32[256,256]{1,0:T(8,128)S(1)} %collective-permute-done.10.refs_9_), channel_id=1, source_target_pairs={{2,1},{6,5},{10,9},{14,13},{18,17},{22,21},{26,25},{30,29}} | collective-permute-start | bytes 786440 | tf_op jit(solution)/shard_map/ppermute | solution.py:222
  55.4 7.9 %collective-permute-start.14 = (f32[256,256]{1,0:T(8,128)S(1)}, f32[256,256]{1,0:T(8,128)S(1)}, u32[]{:S(2)}, u32[]{:S(2)}) collective-permute-start(f32[256,256]{1,0:T(8,128)S(1)} %collective-permute-done.13.refs_12_), channel_id=1, source_target_pairs={{2,3},{6,7},{10,11},{14,15},{18,19},{22,23},{26,27},{30,31}} | collective-permute-start | bytes 786440 | tf_op jit(solution)/shard_map/ppermute | solution.py:222
  59.9 4.8 %collective-permute-start.15 = (f32[256,256]{1,0:T(8,128)S(1)}, f32[256,256]{1,0:T(8,128)S(1)}, u32[]{:S(2)}, u32[]{:S(2)}) collective-permute-start(f32[256,256]{1,0:T(8,128)S(1)} %collective-permute-done.13.refs_12_), channel_id=1, source_target_pairs={{2,1},{6,5},{10,9},{14,13},{18,17},{22,21},{26,25},{30,29}} | collective-permute-start | bytes 786440 | tf_op jit(solution)/shard_map/ppermute | solution.py:222
  60.6 5.5 %collective-permute-start.5 = (f32[256,256]{1,0:T(8,128)S(1)}, f32[256,256]{1,0:T(8,128)S(1)}, u32[]{:S(2)}, u32[]{:S(2)}) collective-permute-start(f32[256,256]{1,0:T(8,128)S(1)} %collective-permute-done.4.refs_3_), channel_id=1, source_target_pairs={{2,3},{6,7},{10,11},{14,15},{18,19},{22,23},{26,27},{30,31}} | collective-permute-start | bytes 786440 | tf_op jit(solution)/shard_map/ppermute | solution.py:222
  61.3 6.2 %collective-permute-start.6 = (f32[256,256]{1,0:T(8,128)S(1)}, f32[256,256]{1,0:T(8,128)S(1)}, u32[]{:S(2)}, u32[]{:S(2)}) collective-permute-start(f32[256,256]{1,0:T(8,128)S(1)} %collective-permute-done.4.refs_3_), channel_id=1, source_target_pairs={{2,1},{6,5},{10,9},{14,13},{18,17},{22,21},{26,25},{30,29}} | collective-permute-start | bytes 786440 | tf_op jit(solution)/shard_map/ppermute | solution.py:222
  62.0 6.9 %collective-permute-start.8 = (f32[256,256]{1,0:T(8,128)S(1)}, f32[256,256]{1,0:T(8,128)}, u32[]{:S(2)}, u32[]{:S(2)}) collective-permute-start(f32[256,256]{1,0:T(8,128)S(1)} %collective-permute-done.7.refs_6_), channel_id=1, source_target_pairs={{2,3},{6,7},{10,11},{14,15},{18,19},{22,23},{26,27},{30,31}} | collective-permute-start | bytes 786440 | tf_op jit(solution)/shard_map/ppermute | solution.py:222
  63.4 6.9 %collective-permute-start.9 = (f32[256,256]{1,0:T(8,128)S(1)}, f32[256,256]{1,0:T(8,128)}, u32[]{:S(2)}, u32[]{:S(2)}) collective-permute-start(f32[256,256]{1,0:T(8,128)S(1)} %collective-permute-done.7.refs_6_), channel_id=1, source_target_pairs={{2,1},{6,5},{10,9},{14,13},{18,17},{22,21},{26,25},{30,29}} | collective-permute-start | bytes 786440 | tf_op jit(solution)/shard_map/ppermute | solution.py:222
  64.7 6.9 %collective-permute-start.17 = (f32[256,256]{1,0:T(8,128)S(1)}, f32[256,256]{1,0:T(8,128)}, u32[]{:S(2)}, u32[]{:S(2)}) collective-permute-start(f32[256,256]{1,0:T(8,128)S(1)} %collective-permute-done.16.refs_3_), channel_id=1, source_target_pairs={{2,3},{6,7},{10,11},{14,15},{18,19},{22,23},{26,27},{30,31}} | collective-permute-start | bytes 786440 | tf_op jit(solution)/shard_map/ppermute | solution.py:222
  66.1 6.9 %collective-permute-start.18 = (f32[256,256]{1,0:T(8,128)S(1)}, f32[256,256]{1,0:T(8,128)}, u32[]{:S(2)}, u32[]{:S(2)}) collective-permute-start(f32[256,256]{1,0:T(8,128)S(1)} %collective-permute-done.16.refs_3_), channel_id=1, source_target_pairs={{2,1},{6,5},{10,9},{14,13},{18,17},{22,21},{26,25},{30,29}} | collective-permute-start | bytes 786440 | tf_op jit(solution)/shard_map/ppermute | solution.py:222
  67.5 6.9 %collective-permute-start.20 = (f32[256,256]{1,0:T(8,128)S(1)}, f32[256,256]{1,0:T(8,128)}, u32[]{:S(2)}, u32[]{:S(2)}) collective-permute-start(f32[256,256]{1,0:T(8,128)S(1)} %collective-permute-done.19.refs_6_), channel_id=1, source_target_pairs={{2,3},{6,7},{10,11},{14,15},{18,19},{22,23},{26,27},{30,31}} | collective-permute-start | bytes 786440 | tf_op jit(solution)/shard_map/ppermute | solution.py:222
  68.8 12.8 %collective-permute-start.21 = (f32[256,256]{1,0:T(8,128)S(1)}, f32[256,256]{1,0:T(8,128)}, u32[]{:S(2)}, u32[]{:S(2)}) collective-permute-start(f32[256,256]{1,0:T(8,128)S(1)} %collective-permute-done.19.refs_6_), channel_id=1, source_target_pairs={{2,1},{6,5},{10,9},{14,13},{18,17},{22,21},{26,25},{30,29}} | collective-permute-start | bytes 786440 | tf_op jit(solution)/shard_map/ppermute | solution.py:222
  70.2 11.4 %collective-permute-start.23 = (f32[256,256]{1,0:T(8,128)S(1)}, f32[256,256]{1,0:T(8,128)}, u32[]{:S(2)}, u32[]{:S(2)}) collective-permute-start(f32[256,256]{1,0:T(8,128)S(1)} %collective-permute-done.22.refs_9_), channel_id=1, source_target_pairs={{2,3},{6,7},{10,11},{14,15},{18,19},{22,23},{26,27},{30,31}} | collective-permute-start | bytes 786440 | tf_op jit(solution)/shard_map/ppermute | solution.py:222
  71.6 10.0 %collective-permute-start.24 = (f32[256,256]{1,0:T(8,128)S(1)}, f32[256,256]{1,0:T(8,128)}, u32[]{:S(2)}, u32[]{:S(2)}) collective-permute-start(f32[256,256]{1,0:T(8,128)S(1)} %collective-permute-done.22.refs_9_), channel_id=1, source_target_pairs={{2,1},{6,5},{10,9},{14,13},{18,17},{22,21},{26,25},{30,29}} | collective-permute-start | bytes 786440 | tf_op jit(solution)/shard_map/ppermute | solution.py:222
  73.0 12.3 %collective-permute-start.26 = (f32[256,256]{1,0:T(8,128)}, f32[256,256]{1,0:T(8,128)}, u32[]{:S(2)}, u32[]{:S(2)}) collective-permute-start(f32[256,256]{1,0:T(8,128)} %collective-permute-done.25.refs_3_), channel_id=1, source_target_pairs={{2,3},{6,7},{10,11},{14,15},{18,19},{22,23},{26,27},{30,31}} | collective-permute-start | bytes 786440 | tf_op jit(solution)/shard_map/ppermute | solution.py:222
  74.3 10.9 %collective-permute-start.27 = (f32[256,256]{1,0:T(8,128)}, f32[256,256]{1,0:T(8,128)}, u32[]{:S(2)}, u32[]{:S(2)}) collective-permute-start(f32[256,256]{1,0:T(8,128)} %collective-permute-done.25.refs_3_), channel_id=1, source_target_pairs={{2,1},{6,5},{10,9},{14,13},{18,17},{22,21},{26,25},{30,29}} | collective-permute-start | bytes 786440 | tf_op jit(solution)/shard_map/ppermute | solution.py:222
  92.2 42.8 %collective-permute-start.31 = (f32[128,256]{1,0:T(8,128)S(1)}, f32[128,256]{1,0:T(8,128)S(1)}, u32[]{:S(2)}, u32[]{:S(2)}) collective-permute-start(f32[128,256]{1,0:T(8,128)S(1)} %add.29), channel_id=1, source_target_pairs={{1,5},{2,6},{3,7},{5,1},{6,2},{7,3},{9,13},{10,14},{11,15},{13,9},... | collective-permute-start | bytes 393224 | tf_op jit(solution)/shard_map/ppermute | solution.py:197
  109.4 30.0 %collective-permute-start.32 = (f32[256,256]{1,0:T(8,128)}, f32[256,256]{1,0:T(8,128)S(1)}, u32[]{:S(2)}, u32[]{:S(2)}) collective-permute-start(f32[256,256]{1,0:T(8,128)} %factor.1.refs_1_), channel_id=1, source_target_pairs={{0,1},{4,5},{8,9},{12,13},{16,17},{20,21},{24,25},{28,29}} | collective-permute-start | bytes 786440 | tf_op jit(solution)/shard_map/ppermute | solution.py:243
  132.4 12.6 %collective-permute-start.33 = (f32[256,256]{1,0:T(8,128)}, f32[256,256]{1,0:T(8,128)S(1)}, u32[]{:S(2)}, u32[]{:S(2)}) collective-permute-start(f32[256,256]{1,0:T(8,128)} %factor.1.refs_1_), channel_id=1, source_target_pairs={{0,2},{4,6},{8,10},{12,14},{16,18},{20,22},{24,26},{28,30}} | collective-permute-start | bytes 786440 | tf_op jit(solution)/shard_map/ppermute | solution.py:243
  133.7 16.4 %collective-permute-start.34 = (f32[256,256]{1,0:T(8,128)}, f32[256,256]{1,0:T(8,128)S(1)}, u32[]{:S(2)}, u32[]{:S(2)}) collective-permute-start(f32[256,256]{1,0:T(8,128)} %factor.1.refs_1_), channel_id=1, source_target_pairs={{0,3},{4,7},{8,11},{12,15},{16,19},{20,23},{24,27},{28,31}} | collective-permute-start | bytes 786440 | tf_op jit(solution)/shard_map/ppermute | solution.py:243
  (21 other events, 394.6 us)

commit v2 on v0

v2 whole, which is shorter than its diff:
```python
import jax
import jax.numpy as jnp
from jax import lax
from jax.experimental import pallas as pl
from jax.experimental.pallas import tpu as pltpu
from jax.sharding import PartitionSpec as P


PAIRS = 4
CHUNKS = 2 * PAIRS
TILE = 64
F32 = jnp.float32
BF16 = jnp.bfloat16
VMEM = pl.BlockSpec(memory_space=pltpu.VMEM)
SMEM = pl.BlockSpec(memory_space=pltpu.SMEM)
ANY = pl.BlockSpec(memory_space=pl.ANY)
NN = ((1,), (0,))
TN = ((0,), (0,))
ROOT, LOWER, _, ODD = range(4)


def kernel_call(body, ctrl, operands, outputs, scratch=(), hbm_in=0, hbm_out=0, room=8):
    held = [pltpu.with_memory_space_constraint(o, pltpu.VMEM) for o in operands[hbm_in:]]
    shapes = [jax.ShapeDtypeStruct(s, d) for s, d in outputs[:hbm_out]]
    shapes += [pltpu.VMEM(s, d) for s, d in outputs[hbm_out:]]
    return pl.pallas_call(
        body,
        out_shape=tuple(shapes),
        in_specs=[SMEM] + [ANY] * hbm_in + [VMEM] * len(held),
        out_specs=tuple([ANY] * hbm_out + [VMEM] * (len(outputs) - hbm_out)),
        scratch_shapes=scratch,
        compiler_params=pltpu.CompilerParams(vmem_limit_bytes=room << 20),
    )(ctrl, *[pltpu.with_memory_space_constraint(o, pltpu.HBM) for o in operands[:hbm_in]], *held)


def fine(left, right, dims=NN):
    return lax.dot_general(left, right, (dims, ((), ())), precision=lax.Precision.HIGHEST, preferred_element_type=F32)


def split(value):
    high = value.astype(BF16)
    return high, (value - high.astype(F32)).astype(BF16)


def three(left, right, dims=NN):
    one = lambda a, b: lax.dot_general(a, b, (dims, ((), ())), preferred_element_type=F32)
    return one(left[0], right[0]) + (one(left[0], right[1]) + one(left[1], right[0]))


def halves(value, ctrl_ref, keep_ref, send_ref):
    half = value.shape[0] // 2
    odd = ctrl_ref[ODD] == 1
    keep_ref[...] = jnp.where(odd, value[half:], value[:half])
    send_ref[...] = jnp.where(odd, value[:half], value[half:])


def joined(ctrl_ref, mine, other):
    odd = ctrl_ref[ODD] == 1
    return jnp.concatenate([jnp.where(odd, other, mine), jnp.where(odd, mine, other)], axis=0)


def load(ctrl, columns):
    rows, width = columns.shape
    step = rows // CHUNKS

    def body(ctrl_ref, columns_ref, *refs):
        outs, sem = refs[:CHUNKS], refs[CHUNKS]
        copies = [
            pltpu.make_async_copy(columns_ref.at[pl.ds(c * step, step), :], outs[c], sem.at[c]) for c in range(CHUNKS)
        ]
        for copy in copies:
            copy.start()
        for copy in copies:
            copy.wait()

    shape = [((step, width), F32)] * CHUNKS
    return kernel_call(body, ctrl, [columns], shape, [pltpu.SemaphoreType.DMA((CHUNKS,))], hbm_in=1)


def gram_halves(ctrl, chunks):
    width = chunks[0].shape[1]

    def body(ctrl_ref, *refs):
        ins, (keep_ref, send_ref) = refs[:CHUNKS], refs[CHUNKS:]

        @pl.when(ctrl_ref[ROOT] == 1)
        def _():
            total = None
            for ref in ins:
                pair = split(ref[...])
                part = three(pair, pair, TN)
                total = part if total is None else total + part
            halves(total, ctrl_ref, keep_ref, send_ref)

    return kernel_call(body, ctrl, chunks, [((width // 2, width), F32)] * 2)


def eliminate(tile, size):
    lanes = tile.shape[1]
    row = lax.broadcasted_iota(jnp.int32, (size, 1), 0)
    for j in range(0, size, 2):
        low = j // 8 * 8
        tail, at = tile[low:], row[low:]
        k, count = j - low, size - low
        c0 = jnp.broadcast_to(tail[:, j : j + 1], (count, lanes))
        c1 = jnp.broadcast_to(tail[:, j + 1 : j + 2], (count, lanes))
        p00, p01, p11 = c0[k : k + 1], c1[k : k + 1], c1[k + 1 : k + 2]
        r0, r1 = tail[k : k + 1], tail[k + 1 : k + 2]
        scale = 1.0 / (p00 * p11 - p01 * p01)
        q0 = (p11 * r0 - p01 * r1) * scale
        q1 = (p00 * r1 - p01 * r0) * scale
        inner = r0 * (p01 * (1.0 / p00))
        tail = tail - jnp.where(at > j + 1, c0 * q0 + c1 * q1, jnp.where(at == j + 1, inner, 0.0))
        tile = tail if low == 0 else jnp.concatenate([tile[:low], tail], axis=0)
    return tile


def identity(size):
    shape = (size, size)
    same = lax.broadcasted_iota(jnp.int32, shape, 0) == lax.broadcasted_iota(jnp.int32, shape, 1)
    return jnp.where(same, 1.0, 0.0).astype(F32)


def factor(ctrl, mine, other):
    width = mine.shape[1]

    def body(ctrl_ref, mine_ref, other_ref, gram_ref, inverse_ref, work_ref):
        @pl.when(ctrl_ref[ROOT] == 1)
        def _():
            gram = joined(ctrl_ref, mine_ref[...], other_ref[...])
            gram_ref[...] = gram
            work_ref[:, :width] = gram
            work_ref[:, width:] = identity(width)
            eye = identity(TILE)
            for start in range(0, width, TILE):
                end = start + TILE
                tile = jnp.concatenate([work_ref[start:end, start:end], eye], axis=1)
                tile = eliminate(tile, TILE)
                pivots = jnp.sum(tile[:, :TILE] * eye, axis=1, keepdims=True)
                block = fine(tile[:, TILE:] * lax.rsqrt(pivots), work_ref[start:end, :])
                work_ref[start:end, :] = block
                if end < width:
                    work_ref[end:, :] = work_ref[end:, :] - fine(block[:, end:width], block, TN)
            inverse_ref[...] = work_ref[:, width:]

    shape = [((width, width), F32)] * 2
    return kernel_call(body, ctrl, [mine, other], shape, [pltpu.VMEM((width, 2 * width), F32)])


def gather(ctrl, total, chunks, moved, last):
    step, width = chunks[0].shape
    first = total is None
    counts = [len(m) for m in moved[1:]]

    def body(ctrl_ref, *refs):
        refs = list(refs)
        sum_ref = None if first else refs.pop(0)
        blocks = [refs.pop(0)[...] for _ in range(2)]
        swapped = refs.pop(0)[...] if moved[0] else None
        parts = []
        for n in counts:
            got = [refs.pop(0)[...] for _ in range(n)]
            parts.append(sum(got[1:], got[0]) if got else None)
        outs = refs[:4]
        acc = None if first else sum_ref[...]
        for k in range(2):
            got = blocks[k]
            if parts[k] is not None:
                got = parts[k]
                if swapped is not None:
                    got = jnp.where(ctrl_ref[LOWER + k] == 1, swapped, got)
                got = jnp.where(ctrl_ref[ROOT] == 1, blocks[k], got)
            pair = split(got)
            outs[2 * k][...], outs[2 * k + 1][...] = pair
            part = three(pair, split(blocks[k]), TN)
            acc = part if acc is None else acc + part
        if last:
            halves(acc, ctrl_ref, *refs[4:])
        else:
            refs[4][...] = acc

    flat = ([] if first else [total]) + list(chunks) + [m for ms in moved for m in ms]
    shape = [((step, width), BF16)] * 4
    shape += [((width // 2, width), F32)] * 2 if last else [((width, width), F32)]
    return kernel_call(body, ctrl, flat, shape)


def finish(ctrl, inverse, gram, mine, other, chunks, sent, pairs):
    step, width = chunks[0].shape

    def body(ctrl_ref, own_ref, gram_ref, mine_ref, other_ref, *refs):
        blocks, refs = refs[:CHUNKS], refs[CHUNKS:]
        moved, refs = refs[: len(sent)], refs[len(sent) :]
        held, refs = refs[: 2 * CHUNKS], refs[2 * CHUNKS :]
        out_ref, projected_ref, buffer_ref, small_ref, sem = refs
        root = ctrl_ref[ROOT] == 1
        got = own_ref[...]
        if moved:
            parts = [ref[...] for ref in moved]
            got = jnp.where(root, got, sum(parts[1:], parts[0]))
        projected = fine(got, jnp.where(root, gram_ref[...], joined(ctrl_ref, mine_ref[...], other_ref[...])))
        small_ref[...] = projected
        copies = [pltpu.make_async_copy(small_ref, projected_ref, sem.at[CHUNKS])]
        copies[0].start()
        weight = split(jnp.where(root, -got.T, fine(got, projected, TN)))
        for c in range(CHUNKS):
            there = pl.ds(c * step, step)
            base = jnp.where(root, 0.0, blocks[c][...])
            buffer_ref[there, :] = base - three((held[2 * c][...], held[2 * c + 1][...]), weight)
            copies.append(pltpu.make_async_copy(buffer_ref.at[there, :], out_ref.at[there, :], sem.at[c]))
            copies[-1].start()
        for copy in copies:
            copy.wait()

    return kernel_call(
        body,
        ctrl,
        [inverse, gram, mine, other, *chunks, *sent, *pairs],
        [((CHUNKS * step, width), F32), ((width, width), F32)],
        [
            pltpu.VMEM((CHUNKS * step, width), F32),
            pltpu.VMEM((width, width), F32),
            pltpu.SemaphoreType.DMA((CHUNKS + 1,)),
        ],
        hbm_out=2,
        room=16,
    )


def added(ctrl, left, right):
    def body(ctrl_ref, left_ref, right_ref, out_ref):
        out_ref[...] = left_ref[...] + right_ref[...]

    return kernel_call(body, ctrl, [left, right], [(left.shape, F32)])[0]


def exchange(ctrl, mine, send, rows, cols, members):
    def swap(part, bit):
        pairs = [(r * cols + c, (r ^ bit) * cols + c) for r in range(rows) for c in members]
        return lax.ppermute(part, ("row", "col"), pairs)

    mine = added(ctrl, mine, swap(send, 1))
    bit = 2
    while bit < rows:
        mine = added(ctrl, mine, swap(mine, bit))
        bit *= 2
    return mine, swap(mine, 1)


def hop(value, pairs):
    return lax.ppermute(value, "col", pairs)


def spread(ctrl, chunks, cols):
    lower, upper = cols // 2, cols // 2 + 1
    two = cols > 3
    if not two:
        parts = [[hop(v, [(0, c)]) for c in range(1, cols)] for v in chunks]
        return [[], *parts]
    first = hop(chunks[0], [(0, upper)])
    second = hop(chunks[1], [(0, lower)])
    own = [(lower, lower - 1)] if lower > 1 else []
    far = [(upper, lower - 1)] if lower > 1 else []
    firsts, seconds = [first], [second]
    both = added(ctrl, first, second)
    swapped = hop(both, [(lower, upper), (upper, lower)])
    if upper + 1 < cols:
        near = hop(both, own + [(upper, upper + 1)])
        away = hop(both, far + [(lower, upper + 1)])
        above = lax.axis_index("col") > upper
        firsts.append(jnp.where(above, near, away))
        seconds.append(jnp.where(above, away, near))
        for tail, into in ((firsts[-1], firsts), (seconds[-1], seconds)):
            down, up = lower - 1, upper + 1
            while down > 1 or up + 1 < cols:
                pairs = ([(down, down - 1)] if down > 1 else []) + ([(up, up + 1)] if up + 1 < cols else [])
                tail = hop(tail, pairs)
                into.append(tail)
                down, up = down - 1, up + 1
    else:
        firsts.append(hop(first, far))
        seconds.append(hop(second, own))
    return [[swapped], firsts, seconds]


def solution(mesh):
    rows, cols = mesh.shape["row"], mesh.shape["col"]

    def per_device(columns):
        at = lax.axis_index("col")
        odd = lax.axis_index("row") % 2 == 1
        ctrl = jnp.stack([at == 0, at == cols // 2, at == cols // 2 + 1, odd]).astype(jnp.int32)
        chunks = load(ctrl, columns)
        moved = [spread(ctrl, chunks[2 * p : 2 * p + 2], cols) for p in range(PAIRS)]
        gram, inverse = factor(ctrl, *exchange(ctrl, *gram_halves(ctrl, chunks), rows, cols, (0,)))
        sent = [hop(inverse, [(0, c)]) for c in range(1, cols)]
        total, pairs = None, []
        for p in range(PAIRS):
            *held, total = gather(ctrl, total, chunks[2 * p : 2 * p + 2], moved[p], False) if (
                p + 1 < PAIRS
            ) else (*gather(ctrl, total, chunks[2 * p : 2 * p + 2], moved[p], True), None)
            pairs += held
        mine, send = pairs[2 * CHUNKS :]
        total = exchange(ctrl, mine, send, rows, cols, tuple(range(cols)))
        return tuple(finish(ctrl, inverse, gram, *total, chunks, sent, pairs[: 2 * CHUNKS]))

    return jax.shard_map(
        per_device, mesh=mesh, in_specs=(P("row", "col"),), out_specs=(P("row", "col"), P(None, "col")), check_vma=False
    )
```

time: 240 us -> 118 us (0.49)
  waiting for transfers between devices: 143 us -> 32.7 us
  other arithmetic: 57.9 us -> 0.08 us
  starting transfers between devices: 0.08 us -> 51 us
  Pallas kernels: 0 us -> 32.5 us
  matrix products: 17.6 us -> 0 us
  between operations: 15.5 us -> 1.17 us
  local copies, waits for them, and re-layouts: 5.15 us -> 0 us
    psum x2 -> x0, waiting for transfers between devices: 143 us -> none  [the longest x1 89.4 us: spread(): return lax.psum(kept, axis)]
    another operation x9 -> x0, other arithmetic: 53.8 us -> none  [the longest x6 34.1 us: invert_lower(): lower = jnp.linalg.cholesky(gram_sum)]
    ppermute x0 -> x31, starting transfers between devices: none -> 51 us  [the longest x23 37.1 us: hop(): return lax.ppermute(value, 'col', pairs)]
    ppermute x0 -> x31, waiting for transfers between devices: none -> 32.7 us  [the longest x23 31 us: hop(): return lax.ppermute(value, 'col', pairs)]
    pallas_call x0 -> x18, Pallas kernels: none -> 32.5 us  [kernel_call(): pl.pallas_call(body, out_shape=tuple(shapes), in_specs=[SMEM] + [ANY] * h...]
    dot_general x5 -> x0, matrix products: 16.3 us -> none  [the longest x2 10.7 us: cross_product(): lax.dot_general(left, right, (((0,), (0,)), ((), ())), precision=lax.Prec...]
    another operation x9 -> x0, local copies, waits for them, and re-layouts: 4.05 us -> none
    select_n x1 -> x0, other arithmetic: 3.05 us -> none  [spread(): jnp.where(lax.axis_index(axis) == source, value, 0).astype(value.dtype)]
  transfers between devices with their start and end apart: 2 -> 31, of which waited for: 2 -> 9; matrix products, arithmetic and copies ran while one was open for 0% -> 0% of each run, Pallas kernels for 0% -> 23%
where the time goes in v2:
time: 118 us
  starting transfers between devices  51 us (43%)
  waiting for transfers between devices  32.7 us (28%)
  Pallas kernels  32.5 us (28%)
    ppermute x23, starting transfers between devices, hop(): return lax.ppermute(value, 'col', pairs)  37.1 us
    pallas_call x18, Pallas kernels, kernel_call(): pl.pallas_call(body, out_shape=tuple(shapes), in_specs=[SMEM] + [ANY] * h...  32.5 us
    ppermute x23, waiting for transfers between devices, hop(): return lax.ppermute(value, 'col', pairs)  31 us
    ppermute x8, starting transfers between devices, swap(): return lax.ppermute(part, ('row', 'col'), pairs)  14 us
  transfers between devices with their start and end apart: 31, of which 9 were waited for; matrix products, arithmetic and copies ran while one was open for 0% of the time, Pallas kernels for 23%

profile of v2, /device:TPU:0, one launch (start us, length us, event | category | flops | bytes accessed | tf_op | source)
XLA Modules:
  0.0 117.5 jit_solution(3380308213848284864)
XLA Ops:
  0.7 2.1 %shard_map.30 = (f32[256,256]{1,0:T(8,128)S(1)}, f32[256,256]{1,0:T(8,128)S(1)}, f32[256,256]{1,0:T(8,128)S(1)}, f32[256,256]{1,0:T(8,128)S(1)}, f32[256,256]{1,...) custom-call(s32[4]{0:T(128)S(1)} %add_convert_fusion.ctrl_ref, ...), custom_call_target="tpu_custom_call" | custom-call | tf_op jit(solution)/shard_map/pallas_call | solution.py:26
  2.8 7.0 %collective-permute-start.4 = (f32[256,256]{1,0:T(8,128)S(1)}, f32[256,256]{1,0:T(8,128)S(1)}, u32[]{:S(2)}, u32[]{:S(2)}) collective-permute-start(f32[256,256]{1,0:T(8,128)S(1)} %get-tuple-element.35.refs_0_), channel_id=1, source_target_pairs={{0,3},{4,7},{8,11},{12,15},{16,19},{20,23},{24,27},{28,31}} | collective-permute-start | bytes 786440 | tf_op jit(solution)/shard_map/ppermute | solution.py:251
  9.8 1.6 %shard_map.31 = (f32[128,256]{1,0:T(8,128)S(1)}, f32[128,256]{1,0:T(8,128)S(1)}) custom-call(s32[4]{0:T(128)S(1)} %add_convert_fusion.ctrl_ref, f32[256,256]{1,0:T(8,128)S(1)} %get-tuple-element.35.refs_0_, f32[256,256]{1,0:T(8,128)S(1)} %get-tuple-element.36.refs_1_, f32[256,256]{1,0:T(8,128)S(1)} %get-tuple-element.37.refs_2_.refs_1_, ...), custom_call_target="tpu_custom_call" | custom-call | tf_op jit(solution)/shard_map/pallas_call | solution.py:26
  11.4 1.9 %collective-permute-start = (f32[128,256]{1,0:T(8,128)S(1)}, f32[128,256]{1,0:T(8,128)S(1)}, u32[]{:S(2)}, u32[]{:S(2)}) collective-permute-start(f32[128,256]{1,0:T(8,128)S(1)} %get-tuple-element.44), channel_id=1, source_target_pairs={{0,4},{4,0},{8,12},{12,8},{16,20},{20,16},{24,28},{28,24}} | collective-permute-start | bytes 393224 | tf_op jit(solution)/shard_map/ppermute | solution.py:240
  13.4 1.3 %collective-permute-start.5 = (f32[256,256]{1,0:T(8,128)S(1)}, f32[256,256]{1,0:T(8,128)S(1)}, u32[]{:S(2)}, u32[]{:S(2)}) collective-permute-start(f32[256,256]{1,0:T(8,128)S(1)} %get-tuple-element.36.refs_1_), channel_id=1, source_target_pairs={{0,2},{4,6},{8,10},{12,14},{16,18},{20,22},{24,26},{28,30}} | collective-permute-start | bytes 786440 | tf_op jit(solution)/shard_map/ppermute | solution.py:251
  14.7 1.3 %collective-permute-start.9 = (f32[256,256]{1,0:T(8,128)S(1)}, f32[256,256]{1,0:T(8,128)S(1)}, u32[]{:S(2)}, u32[]{:S(2)}) collective-permute-start(f32[256,256]{1,0:T(8,128)S(1)} %get-tuple-element.37.refs_2_.refs_1_), channel_id=1, source_target_pairs={{0,3},{4,7},{8,11},{12,15},{16,19},{20,23},{24,27},{28,31}} | collective-permute-start | bytes 786440 | tf_op jit(solution)/shard_map/ppermute | solution.py:251
  16.0 1.3 %collective-permute-start.10 = (f32[256,256]{1,0:T(8,128)S(1)}, f32[256,256]{1,0:T(8,128)S(1)}, u32[]{:S(2)}, u32[]{:S(2)}) collective-permute-start(f32[256,256]{1,0:T(8,128)S(1)} %get-tuple-element.38.refs_3_.refs_2_), channel_id=1, source_target_pairs={{0,2},{4,6},{8,10},{12,14},{16,18},{20,22},{24,26},{28,30}} | collective-permute-start | bytes 786440 | tf_op jit(solution)/shard_map/ppermute | solution.py:251
  17.3 1.3 %collective-permute-start.14 = (f32[256,256]{1,0:T(8,128)S(1)}, f32[256,256]{1,0:T(8,128)S(1)}, u32[]{:S(2)}, u32[]{:S(2)}) collective-permute-start(f32[256,256]{1,0:T(8,128)S(1)} %get-tuple-element.39.refs_4_.refs_1_), channel_id=1, source_target_pairs={{0,3},{4,7},{8,11},{12,15},{16,19},{20,23},{24,27},{28,31}} | collective-permute-start | bytes 786440 | tf_op jit(solution)/shard_map/ppermute | solution.py:251
  19.2 3.4 %collective-permute-start.1 = (f32[128,256]{1,0:T(8,128)S(1)}, f32[128,256]{1,0:T(8,128)S(1)}, u32[]{:S(2)}, u32[]{:S(2)}) collective-permute-start(f32[128,256]{1,0:T(8,128)S(1)} %shard_map.32.left_ref), channel_id=1, source_target_pairs={{0,8},{4,12},{8,0},{12,4},{16,24},{20,28},{24,16},{28,20}} | collective-permute-start | bytes 393224 | tf_op jit(solution)/shard_map/ppermute | solution.py:240
  22.6 4.0 %collective-permute-start.15 = (f32[256,256]{1,0:T(8,128)S(1)}, f32[256,256]{1,0:T(8,128)S(1)}, u32[]{:S(2)}, u32[]{:S(2)}) collective-permute-start(f32[256,256]{1,0:T(8,128)S(1)} %get-tuple-element.40.refs_5_.refs_2_), channel_id=1, source_target_pairs={{0,2},{4,6},{8,10},{12,14},{16,18},{20,22},{24,26},{28,30}} | collective-permute-start | bytes 786440 | tf_op jit(solution)/shard_map/ppermute | solution.py:251
  27.2 1.3 %collective-permute-start.19 = (f32[256,256]{1,0:T(8,128)S(1)}, f32[256,256]{1,0:T(8,128)S(1)}, u32[]{:S(2)}, u32[]{:S(2)}) collective-permute-start(f32[256,256]{1,0:T(8,128)S(1)} %get-tuple-element.41.refs_6_.refs_1_), channel_id=1, source_target_pairs={{0,3},{4,7},{8,11},{12,15},{16,19},{20,23},{24,27},{28,31}} | collective-permute-start | bytes 786440 | tf_op jit(solution)/shard_map/ppermute | solution.py:251
  28.6 1.3 %collective-permute-start.20 = (f32[256,256]{1,0:T(8,128)S(1)}, f32[256,256]{1,0:T(8,128)S(1)}, u32[]{:S(2)}, u32[]{:S(2)}) collective-permute-start(f32[256,256]{1,0:T(8,128)S(1)} %get-tuple-element.42.refs_7_.refs_2_), channel_id=1, source_target_pairs={{0,2},{4,6},{8,10},{12,14},{16,18},{20,22},{24,26},{28,30}} | collective-permute-start | bytes 786440 | tf_op jit(solution)/shard_map/ppermute | solution.py:251
  29.9 2.7 %collective-permute-done.10.right_ref.refs_6_ = f32[256,256]{1,0:T(8,128)S(1)} collective-permute-done((f32[256,256]{1,0:T(8,128)S(1)}, f32[256,256]{1,0:T(8,128)S(1)}, u32[]{:S(2)}, u32[]{:S(2)}) %collective-permute-start.10) | collective-permute-done | bytes 262176 | tf_op jit(solution)/shard_map/ppermute | solution.py:251
  33.3 4.9 %collective-permute-done.14.left_ref.refs_4_ = f32[256,256]{1,0:T(8,128)S(1)} collective-permute-done((f32[256,256]{1,0:T(8,128)S(1)}, f32[256,256]{1,0:T(8,128)S(1)}, u32[]{:S(2)}, u32[]{:S(2)}) %collective-permute-start.14) | collective-permute-done | bytes 262176 | tf_op jit(solution)/shard_map/ppermute | solution.py:251
  39.5 4.4 %collective-permute-done.15.right_ref.refs_6_ = f32[256,256]{1,0:T(8,128)S(1)} collective-permute-done((f32[256,256]{1,0:T(8,128)S(1)}, f32[256,256]{1,0:T(8,128)S(1)}, u32[]{:S(2)}, u32[]{:S(2)}) %collective-permute-start.15) | collective-permute-done | bytes 262176 | tf_op jit(solution)/shard_map/ppermute | solution.py:251
  44.5 4.9 %collective-permute-done.19.left_ref.refs_4_ = f32[256,256]{1,0:T(8,128)S(1)} collective-permute-done((f32[256,256]{1,0:T(8,128)S(1)}, f32[256,256]{1,0:T(8,128)S(1)}, u32[]{:S(2)}, u32[]{:S(2)}) %collective-permute-start.19) | collective-permute-done | bytes 262176 | tf_op jit(solution)/shard_map/ppermute | solution.py:251
  50.1 4.8 %collective-permute-done.20.right_ref.refs_6_ = f32[256,256]{1,0:T(8,128)S(1)} collective-permute-done((f32[256,256]{1,0:T(8,128)S(1)}, f32[256,256]{1,0:T(8,128)S(1)}, u32[]{:S(2)}, u32[]{:S(2)}) %collective-permute-start.20) | collective-permute-done | bytes 262176 | tf_op jit(solution)/shard_map/ppermute | solution.py:251
  62.1 1.1 shard_map.37
  63.2 1.1 shard_map.39
  64.3 3.4 %collective-permute-start.2 = (f32[128,256]{1,0:T(8,128)S(1)}, f32[128,256]{1,0:T(8,128)S(1)}, u32[]{:S(2)}, u32[]{:S(2)}) collective-permute-start(f32[128,256]{1,0:T(8,128)S(1)} %shard_map.33.left_ref), channel_id=1, source_target_pairs={{0,16},{4,20},{8,24},{12,28},{16,0},{20,4},{24,8},{28,12}} | collective-permute-start | bytes 393224 | tf_op jit(solution)/shard_map/ppermute | solution.py:240
  68.8 1.1 shard_map.43
  70.0 1.5 %collective-permute-done.2.right_ref = f32[128,256]{1,0:T(8,128)S(1)} collective-permute-done((f32[128,256]{1,0:T(8,128)S(1)}, f32[128,256]{1,0:T(8,128)S(1)}, u32[]{:S(2)}, u32[]{:S(2)}) %collective-permute-start.2) | collective-permute-done | bytes 131104 | tf_op jit(solution)/shard_map/ppermute | solution.py:240
  72.1 1.9 %collective-permute-start.3 = (f32[128,256]{1,0:T(8,128)S(1)}, f32[128,256]{1,0:T(8,128)S(1)}, u32[]{:S(2)}, u32[]{:S(2)}) collective-permute-start(f32[128,256]{1,0:T(8,128)S(1)} %shard_map.34.mine_ref), channel_id=1, source_target_pairs={{0,4},{4,0},{8,12},{12,8},{16,20},{20,16},{24,28},{28,24}} | collective-permute-start | bytes 393224 | tf_op jit(solution)/shard_map/ppermute | solution.py:240
  74.6 1.6 %collective-permute-start.25 = (f32[128,256]{1,0:T(8,128)S(1)}, f32[128,256]{1,0:T(8,128)S(1)}, u32[]{:S(2)}, u32[]{:S(2)}) collective-permute-start(f32[128,256]{1,0:T(8,128)S(1)} %shard_map.44.left_ref), channel_id=1, source_target_pairs={{0,8},{1,9},{2,10},{3,11},{4,12},{5,13},{6,14},{7,15},{8,0},{9,1},... | collective-permute-start | bytes 393224 | tf_op jit(solution)/shard_map/ppermute | solution.py:240
  76.1 15.4 %shard_map.35 = (f32[256,256]{1,0:T(8,128)S(1)}, f32[256,256]{1,0:T(8,128)S(1)}) custom-call(s32[4]{0:T(128)S(1)} %add_convert_fusion.ctrl_ref, f32[128,256]{1,0:T(8,128)S(1)} %shard_map.34.mine_ref, f32[128,256]{1,0:T(8,128)S(1)} %collective-permute-done.3.other_ref), custom_call_target="tpu_custom_call" | custom-call | tf_op jit(solution)/shard_map/pallas_call | solution.py:26
  91.5 5.4 %collective-permute-start.30 = (f32[256,256]{1,0:T(8,128)S(1)}, f32[256,256]{1,0:T(8,128)S(1)}, u32[]{:S(2)}, u32[]{:S(2)}) collective-permute-start(f32[256,256]{1,0:T(8,128)S(1)} %get-tuple-element.45.own_ref), channel_id=1, source_target_pairs={{0,3},{4,7},{8,11},{12,15},{16,19},{20,23},{24,27},{28,31}} | collective-permute-start | bytes 786440 | tf_op jit(solution)/shard_map/ppermute | solution.py:251
  96.9 1.3 %collective-permute-start.29 = (f32[256,256]{1,0:T(8,128)S(1)}, f32[256,256]{1,0:T(8,128)S(1)}, u32[]{:S(2)}, u32[]{:S(2)}) collective-permute-start(f32[256,256]{1,0:T(8,128)S(1)} %get-tuple-element.45.own_ref), channel_id=1, source_target_pairs={{0,2},{4,6},{8,10},{12,14},{16,18},{20,22},{24,26},{28,30}} | collective-permute-start | bytes 786440 | tf_op jit(solution)/shard_map/ppermute | solution.py:251
  98.8 1.6 %collective-permute-start.26 = (f32[128,256]{1,0:T(8,128)S(1)}, f32[128,256]{1,0:T(8,128)S(1)}, u32[]{:S(2)}, u32[]{:S(2)}) collective-permute-start(f32[128,256]{1,0:T(8,128)S(1)} %shard_map.45.left_ref), channel_id=1, source_target_pairs={{0,16},{1,17},{2,18},{3,19},{4,20},{5,21},{6,22},{7,23},{8,24},{9,... | collective-permute-start | bytes 393224 | tf_op jit(solution)/shard_map/ppermute | solution.py:240
  100.4 3.5 %collective-permute-start.28 = (f32[256,256]{1,0:T(8,128)S(1)}, f32[256,256]{1,0:T(8,128)S(1)}, u32[]{:S(2)}, u32[]{:S(2)}) collective-permute-start(f32[256,256]{1,0:T(8,128)S(1)} %get-tuple-element.45.own_ref), channel_id=1, source_target_pairs={{0,1},{4,5},{8,9},{12,13},{16,17},{20,21},{24,25},{28,29}} | collective-permute-start | bytes 786440 | tf_op jit(solution)/shard_map/ppermute | solution.py:251
  104.8 4.4 %collective-permute-done.29.refs_9_ = f32[256,256]{1,0:T(8,128)S(1)} collective-permute-done((f32[256,256]{1,0:T(8,128)S(1)}, f32[256,256]{1,0:T(8,128)S(1)}, u32[]{:S(2)}, u32[]{:S(2)}) %collective-permute-start.29) | collective-permute-done | bytes 262176 | tf_op jit(solution)/shard_map/ppermute | solution.py:251
  109.2 4.8 %collective-permute-done.28.refs_8_ = f32[256,256]{1,0:T(8,128)S(1)} collective-permute-done((f32[256,256]{1,0:T(8,128)S(1)}, f32[256,256]{1,0:T(8,128)S(1)}, u32[]{:S(2)}, u32[]{:S(2)}) %collective-permute-start.28) | collective-permute-done | bytes 262176 | tf_op jit(solution)/shard_map/ppermute | solution.py:251
  114.0 3.6 %shard_map.47 = (f32[2048,256]{1,0:T(8,128)}, f32[256,256]{1,0:T(8,128)}) custom-call(s32[4]{0:T(128)S(1)} %add_convert_fusion.ctrl_ref, f32[256,256]{1,0:T(8,128)S(1)} %get-tuple-element.45.own_ref, f32[256,256]{1,0:T(8,128)S(1)} %get-tuple-element.46.gram_ref, f32[128,256]{1,0:T(8,128)S(1)} %shard_map.46.mine_ref, ...), custom_call_target="tpu_custom_call" | custom-call | tf_op jit(solution)/shard_map/pallas_call | solution.py:26
  (49 shorter events, 15.2 us)
Async XLA Ops:
  2.8 16.4 %collective-permute-start.4 = (f32[256,256]{1,0:T(8,128)S(1)}, f32[256,256]{1,0:T(8,128)S(1)}, u32[]{:S(2)}, u32[]{:S(2)}) collective-permute-start(f32[256,256]{1,0:T(8,128)S(1)} %get-tuple-element.35.refs_0_), channel_id=1, source_target_pairs={{0,3},{4,7},{8,11},{12,15},{16,19},{20,23},{24,27},{28,31}} | collective-permute-start | bytes 786440 | tf_op jit(solution)/shard_map/ppermute | solution.py:251
  11.4 5.9 %collective-permute-start = (f32[128,256]{1,0:T(8,128)S(1)}, f32[128,256]{1,0:T(8,128)S(1)}, u32[]{:S(2)}, u32[]{:S(2)}) collective-permute-start(f32[128,256]{1,0:T(8,128)S(1)} %get-tuple-element.44), channel_id=1, source_target_pairs={{0,4},{4,0},{8,12},{12,8},{16,20},{20,16},{24,28},{28,24}} | collective-permute-start | bytes 393224 | tf_op jit(solution)/shard_map/ppermute | solution.py:240
  13.4 9.3 %collective-permute-start.5 = (f32[256,256]{1,0:T(8,128)S(1)}, f32[256,256]{1,0:T(8,128)S(1)}, u32[]{:S(2)}, u32[]{:S(2)}) collective-permute-start(f32[256,256]{1,0:T(8,128)S(1)} %get-tuple-element.36.refs_1_), channel_id=1, source_target_pairs={{0,2},{4,6},{8,10},{12,14},{16,18},{20,22},{24,26},{28,30}} | collective-permute-start | bytes 786440 | tf_op jit(solution)/shard_map/ppermute | solution.py:251
  14.7 13.9 %collective-permute-start.9 = (f32[256,256]{1,0:T(8,128)S(1)}, f32[256,256]{1,0:T(8,128)S(1)}, u32[]{:S(2)}, u32[]{:S(2)}) collective-permute-start(f32[256,256]{1,0:T(8,128)S(1)} %get-tuple-element.37.refs_2_.refs_1_), channel_id=1, source_target_pairs={{0,3},{4,7},{8,11},{12,15},{16,19},{20,23},{24,27},{28,31}} | collective-permute-start | bytes 786440 | tf_op jit(solution)/shard_map/ppermute | solution.py:251
  16.0 16.6 %collective-permute-start.10 = (f32[256,256]{1,0:T(8,128)S(1)}, f32[256,256]{1,0:T(8,128)S(1)}, u32[]{:S(2)}, u32[]{:S(2)}) collective-permute-start(f32[256,256]{1,0:T(8,128)S(1)} %get-tuple-element.38.refs_3_.refs_2_), channel_id=1, source_target_pairs={{0,2},{4,6},{8,10},{12,14},{16,18},{20,22},{24,26},{28,30}} | collective-permute-start | bytes 786440 | tf_op jit(solution)/shard_map/ppermute | solution.py:251
  17.3 20.9 %collective-permute-start.14 = (f32[256,256]{1,0:T(8,128)S(1)}, f32[256,256]{1,0:T(8,128)S(1)}, u32[]{:S(2)}, u32[]{:S(2)}) collective-permute-start(f32[256,256]{1,0:T(8,128)S(1)} %get-tuple-element.39.refs_4_.refs_1_), channel_id=1, source_target_pairs={{0,3},{4,7},{8,11},{12,15},{16,19},{20,23},{24,27},{28,31}} | collective-permute-start | bytes 786440 | tf_op jit(solution)/shard_map/ppermute | solution.py:251
  19.2 8.0 %collective-permute-start.1 = (f32[128,256]{1,0:T(8,128)S(1)}, f32[128,256]{1,0:T(8,128)S(1)}, u32[]{:S(2)}, u32[]{:S(2)}) collective-permute-start(f32[128,256]{1,0:T(8,128)S(1)} %shard_map.32.left_ref), channel_id=1, source_target_pairs={{0,8},{4,12},{8,0},{12,4},{16,24},{20,28},{24,16},{28,20}} | collective-permute-start | bytes 393224 | tf_op jit(solution)/shard_map/ppermute | solution.py:240
  22.6 21.2 %collective-permute-start.15 = (f32[256,256]{1,0:T(8,128)S(1)}, f32[256,256]{1,0:T(8,128)S(1)}, u32[]{:S(2)}, u32[]{:S(2)}) collective-permute-start(f32[256,256]{1,0:T(8,128)S(1)} %get-tuple-element.40.refs_5_.refs_2_), channel_id=1, source_target_pairs={{0,2},{4,6},{8,10},{12,14},{16,18},{20,22},{24,26},{28,30}} | collective-permute-start | bytes 786440 | tf_op jit(solution)/shard_map/ppermute | solution.py:251
  27.2 22.2 %collective-permute-start.19 = (f32[256,256]{1,0:T(8,128)S(1)}, f32[256,256]{1,0:T(8,128)S(1)}, u32[]{:S(2)}, u32[]{:S(2)}) collective-permute-start(f32[256,256]{1,0:T(8,128)S(1)} %get-tuple-element.41.refs_6_.refs_1_), channel_id=1, source_target_pairs={{0,3},{4,7},{8,11},{12,15},{16,19},{20,23},{24,27},{28,31}} | collective-permute-start | bytes 786440 | tf_op jit(solution)/shard_map/ppermute | solution.py:251
  28.6 26.3 %collective-permute-start.20 = (f32[256,256]{1,0:T(8,128)S(1)}, f32[256,256]{1,0:T(8,128)S(1)}, u32[]{:S(2)}, u32[]{:S(2)}) collective-permute-start(f32[256,256]{1,0:T(8,128)S(1)} %get-tuple-element.42.refs_7_.refs_2_), channel_id=1, source_target_pairs={{0,2},{4,6},{8,10},{12,14},{16,18},{20,22},{24,26},{28,30}} | collective-permute-start | bytes 786440 | tf_op jit(solution)/shard_map/ppermute | solution.py:251
  32.6 23.0 %collective-permute-start.7 = (f32[256,256]{1,0:T(8,128)S(1)}, f32[256,256]{1,0:T(8,128)S(1)}, u32[]{:S(2)}, u32[]{:S(2)}) collective-permute-start(f32[256,256]{1,0:T(8,128)S(1)} %collective-permute-done.4.left_ref.refs_3_), channel_id=1, source_target_pairs={{3,1},{7,5},{11,9},{15,13},{19,17},{23,21},{27,25},{31,29}} | collective-permute-start | bytes 786440 | tf_op jit(solution)/shard_map/ppermute | solution.py:251
  38.2 18.0 %collective-permute-start.6 = (f32[256,256]{1,0:T(8,128)S(1)}, f32[256,256]{1,0:T(8,128)S(1)}, u32[]{:S(2)}, u32[]{:S(2)}) collective-permute-start(f32[256,256]{1,0:T(8,128)S(1)} %shard_map.36), channel_id=1, source_target_pairs={{2,3},{3,2},{6,7},{7,6},{10,11},{11,10},{14,15},{15,14},{18,19},{1... | collective-permute-start | bytes 786440 | tf_op jit(solution)/shard_map/ppermute | solution.py:251
  43.8 14.3 %collective-permute-start.8 = (f32[256,256]{1,0:T(8,128)S(1)}, f32[256,256]{1,0:T(8,128)S(1)}, u32[]{:S(2)}, u32[]{:S(2)}) collective-permute-start(f32[256,256]{1,0:T(8,128)S(1)} %collective-permute-done.5.right_ref.refs_5_), channel_id=1, source_target_pairs={{2,1},{6,5},{10,9},{14,13},{18,17},{22,21},{26,25},{30,29}} | collective-permute-start | bytes 786440 | tf_op jit(solution)/shard_map/ppermute | solution.py:251
  49.4 9.3 %collective-permute-start.12 = (f32[256,256]{1,0:T(8,128)S(1)}, f32[256,256]{1,0:T(8,128)S(1)}, u32[]{:S(2)}, u32[]{:S(2)}) collective-permute-start(f32[256,256]{1,0:T(8,128)S(1)} %collective-permute-done.9.left_ref.refs_4_), channel_id=1, source_target_pairs={{3,1},{7,5},{11,9},{15,13},{19,17},{23,21},{27,25},{31,29}} | collective-permute-start | bytes 786440 | tf_op jit(solution)/shard_map/ppermute | solution.py:251
  54.9 4.6 %collective-permute-start.11 = (f32[256,256]{1,0:T(8,128)S(1)}, f32[256,256]{1,0:T(8,128)S(1)}, u32[]{:S(2)}, u32[]{:S(2)}) collective-permute-start(f32[256,256]{1,0:T(8,128)S(1)} %shard_map.38), channel_id=1, source_target_pairs={{2,3},{3,2},{6,7},{7,6},{10,11},{11,10},{14,15},{15,14},{18,19},{1... | collective-permute-start | bytes 786440 | tf_op jit(solution)/shard_map/ppermute | solution.py:251
  55.6 4.6 %collective-permute-start.13 = (f32[256,256]{1,0:T(8,128)S(1)}, f32[256,256]{1,0:T(8,128)S(1)}, u32[]{:S(2)}, u32[]{:S(2)}) collective-permute-start(f32[256,256]{1,0:T(8,128)S(1)} %collective-permute-done.10.right_ref.refs_6_), channel_id=1, source_target_pairs={{2,1},{6,5},{10,9},{14,13},{18,17},{22,21},{26,25},{30,29}} | collective-permute-start | bytes 786440 | tf_op jit(solution)/shard_map/ppermute | solution.py:251
  56.2 4.6 %collective-permute-start.17 = (f32[256,256]{1,0:T(8,128)S(1)}, f32[256,256]{1,0:T(8,128)S(1)}, u32[]{:S(2)}, u32[]{:S(2)}) collective-permute-start(f32[256,256]{1,0:T(8,128)S(1)} %collective-permute-done.14.left_ref.refs_4_), channel_id=1, source_target_pairs={{3,1},{7,5},{11,9},{15,13},{19,17},{23,21},{27,25},{31,29}} | collective-permute-start | bytes 786440 | tf_op jit(solution)/shard_map/ppermute | solution.py:251
  58.1 6.2 %collective-permute-start.16 = (f32[256,256]{1,0:T(8,128)S(1)}, f32[256,256]{1,0:T(8,128)S(1)}, u32[]{:S(2)}, u32[]{:S(2)}) collective-permute-start(f32[256,256]{1,0:T(8,128)S(1)} %shard_map.40), channel_id=1, source_target_pairs={{2,3},{3,2},{6,7},{7,6},{10,11},{11,10},{14,15},{15,14},{18,19},{1... | collective-permute-start | bytes 786440 | tf_op jit(solution)/shard_map/ppermute | solution.py:251
  58.8 8.9 %collective-permute-start.18 = (f32[256,256]{1,0:T(8,128)S(1)}, f32[256,256]{1,0:T(8,128)S(1)}, u32[]{:S(2)}, u32[]{:S(2)}) collective-permute-start(f32[256,256]{1,0:T(8,128)S(1)} %collective-permute-done.15.right_ref.refs_6_), channel_id=1, source_target_pairs={{2,1},{6,5},{10,9},{14,13},{18,17},{22,21},{26,25},{30,29}} | collective-permute-start | bytes 786440 | tf_op jit(solution)/shard_map/ppermute | solution.py:251
  59.5 9.3 %collective-permute-start.21 = (f32[256,256]{1,0:T(8,128)S(1)}, f32[256,256]{1,0:T(8,128)S(1)}, u32[]{:S(2)}, u32[]{:S(2)}) collective-permute-start(f32[256,256]{1,0:T(8,128)S(1)} %shard_map.42), channel_id=1, source_target_pairs={{2,3},{3,2},{6,7},{7,6},{10,11},{11,10},{14,15},{15,14},{18,19},{1... | collective-permute-start | bytes 786440 | tf_op jit(solution)/shard_map/ppermute | solution.py:251
  60.2 8.6 %collective-permute-start.22 = (f32[256,256]{1,0:T(8,128)S(1)}, f32[256,256]{1,0:T(8,128)S(1)}, u32[]{:S(2)}, u32[]{:S(2)}) collective-permute-start(f32[256,256]{1,0:T(8,128)S(1)} %collective-permute-done.19.left_ref.refs_4_), channel_id=1, source_target_pairs={{3,1},{7,5},{11,9},{15,13},{19,17},{23,21},{27,25},{31,29}} | collective-permute-start | bytes 786440 | tf_op jit(solution)/shard_map/ppermute | solution.py:251
  60.9 8.0 %collective-permute-start.23 = (f32[256,256]{1,0:T(8,128)S(1)}, f32[256,256]{1,0:T(8,128)S(1)}, u32[]{:S(2)}, u32[]{:S(2)}) collective-permute-start(f32[256,256]{1,0:T(8,128)S(1)} %collective-permute-done.20.right_ref.refs_6_), channel_id=1, source_target_pairs={{2,1},{6,5},{10,9},{14,13},{18,17},{22,21},{26,25},{30,29}} | collective-permute-start | bytes 786440 | tf_op jit(solution)/shard_map/ppermute | solution.py:251
  64.3 7.2 %collective-permute-start.2 = (f32[128,256]{1,0:T(8,128)S(1)}, f32[128,256]{1,0:T(8,128)S(1)}, u32[]{:S(2)}, u32[]{:S(2)}) collective-permute-start(f32[128,256]{1,0:T(8,128)S(1)} %shard_map.33.left_ref), channel_id=1, source_target_pairs={{0,16},{4,20},{8,24},{12,28},{16,0},{20,4},{24,8},{28,12}} | collective-permute-start | bytes 393224 | tf_op jit(solution)/shard_map/ppermute | solution.py:240
  69.9 4.1 %collective-permute-start.24 = (f32[128,256]{1,0:T(8,128)S(1)}, f32[128,256]{1,0:T(8,128)S(1)}, u32[]{:S(2)}, u32[]{:S(2)}) collective-permute-start(f32[128,256]{1,0:T(8,128)S(1)} %get-tuple-element.51), channel_id=1, source_target_pairs={{0,4},{1,5},{2,6},{3,7},{4,0},{5,1},{6,2},{7,3},{8,12},{9,13},{10,... | collective-permute-start | bytes 393224 | tf_op jit(solution)/shard_map/ppermute | solution.py:240
  72.1 4.1 %collective-permute-start.3 = (f32[128,256]{1,0:T(8,128)S(1)}, f32[128,256]{1,0:T(8,128)S(1)}, u32[]{:S(2)}, u32[]{:S(2)}) collective-permute-start(f32[128,256]{1,0:T(8,128)S(1)} %shard_map.34.mine_ref), channel_id=1, source_target_pairs={{0,4},{4,0},{8,12},{12,8},{16,20},{20,16},{24,28},{28,24}} | collective-permute-start | bytes 393224 | tf_op jit(solution)/shard_map/ppermute | solution.py:240
  74.6 23.6 %collective-permute-start.25 = (f32[128,256]{1,0:T(8,128)S(1)}, f32[128,256]{1,0:T(8,128)S(1)}, u32[]{:S(2)}, u32[]{:S(2)}) collective-permute-start(f32[128,256]{1,0:T(8,128)S(1)} %shard_map.44.left_ref), channel_id=1, source_target_pairs={{0,8},{1,9},{2,10},{3,11},{4,12},{5,13},{6,14},{7,15},{8,0},{9,1},... | collective-permute-start | bytes 393224 | tf_op jit(solution)/shard_map/ppermute | solution.py:240
  91.5 13.2 %collective-permute-start.30 = (f32[256,256]{1,0:T(8,128)S(1)}, f32[256,256]{1,0:T(8,128)S(1)}, u32[]{:S(2)}, u32[]{:S(2)}) collective-permute-start(f32[256,256]{1,0:T(8,128)S(1)} %get-tuple-element.45.own_ref), channel_id=1, source_target_pairs={{0,3},{4,7},{8,11},{12,15},{16,19},{20,23},{24,27},{28,31}} | collective-permute-start | bytes 786440 | tf_op jit(solution)/shard_map/ppermute | solution.py:251
  96.9 12.3 %collective-permute-start.29 = (f32[256,256]{1,0:T(8,128)S(1)}, f32[256,256]{1,0:T(8,128)S(1)}, u32[]{:S(2)}, u32[]{:S(2)}) collective-permute-start(f32[256,256]{1,0:T(8,128)S(1)} %get-tuple-element.45.own_ref), channel_id=1, source_target_pairs={{0,2},{4,6},{8,10},{12,14},{16,18},{20,22},{24,26},{28,30}} | collective-permute-start | bytes 786440 | tf_op jit(solution)/shard_map/ppermute | solution.py:251
  98.8 5.3 %collective-permute-start.26 = (f32[128,256]{1,0:T(8,128)S(1)}, f32[128,256]{1,0:T(8,128)S(1)}, u32[]{:S(2)}, u32[]{:S(2)}) collective-permute-start(f32[128,256]{1,0:T(8,128)S(1)} %shard_map.45.left_ref), channel_id=1, source_target_pairs={{0,16},{1,17},{2,18},{3,19},{4,20},{5,21},{6,22},{7,23},{8,24},{9,... | collective-permute-start | bytes 393224 | tf_op jit(solution)/shard_map/ppermute | solution.py:240
  100.4 13.6 %collective-permute-start.28 = (f32[256,256]{1,0:T(8,128)S(1)}, f32[256,256]{1,0:T(8,128)S(1)}, u32[]{:S(2)}, u32[]{:S(2)}) collective-permute-start(f32[256,256]{1,0:T(8,128)S(1)} %get-tuple-element.45.own_ref), channel_id=1, source_target_pairs={{0,1},{4,5},{8,9},{12,13},{16,17},{20,21},{24,25},{28,29}} | collective-permute-start | bytes 786440 | tf_op jit(solution)/shard_map/ppermute | solution.py:251
  104.7 9.3 %collective-permute-start.27 = (f32[128,256]{1,0:T(8,128)S(1)}, f32[128,256]{1,0:T(8,128)S(1)}, u32[]{:S(2)}, u32[]{:S(2)}) collective-permute-start(f32[128,256]{1,0:T(8,128)S(1)} %shard_map.46.mine_ref), channel_id=1, source_target_pairs={{0,4},{1,5},{2,6},{3,7},{4,0},{5,1},{6,2},{7,3},{8,12},{9,13},{10,... | collective-permute-start | bytes 393224 | tf_op jit(solution)/shard_map/ppermute | solution.py:240

commit v3 on v0

v3 whole, which is shorter than its diff:
```python
import jax
import jax.numpy as jnp
from jax import lax
from jax.experimental import pallas as pl
from jax.experimental.pallas import tpu as pltpu
from jax.sharding import PartitionSpec as P


PAIRS = 5
CHUNKS = 2 * PAIRS + 1
GROUPS = ((0, 1, 2, 3), (4, 5, 6, 7), (8, 9), (10,))
TILE = 64
F32 = jnp.float32
BF16 = jnp.bfloat16
VMEM = pl.BlockSpec(memory_space=pltpu.VMEM)
ANY = pl.BlockSpec(memory_space=pl.ANY)
NN = ((1,), (0,))
TN = ((0,), (0,))


def at_root():
    return lax.axis_index("col") == 0


def is_odd():
    return lax.axis_index("row") % 2 == 1


def kernel_call(body, operands, outputs, scratch=(), hbm_in=0, hbm_out=0, room=8):
    held = [pltpu.with_memory_space_constraint(o, pltpu.HBM) for o in operands[:hbm_in]]
    held += [pltpu.with_memory_space_constraint(o, pltpu.VMEM) for o in operands[hbm_in:]]
    shapes = [jax.ShapeDtypeStruct(s, d) for s, d in outputs[:hbm_out]]
    shapes += [pltpu.VMEM(s, d) for s, d in outputs[hbm_out:]]
    return pl.pallas_call(
        body,
        out_shape=tuple(shapes),
        in_specs=[ANY] * hbm_in + [VMEM] * (len(operands) - hbm_in),
        out_specs=tuple([ANY] * hbm_out + [VMEM] * (len(outputs) - hbm_out)),
        scratch_shapes=scratch,
        compiler_params=pltpu.CompilerParams(vmem_limit_bytes=room << 20),
    )(*held)


def fine(left, right, dims=NN):
    return lax.dot_general(left, right, (dims, ((), ())), precision=lax.Precision.HIGHEST, preferred_element_type=F32)


def split(value):
    high = value.astype(BF16)
    return high, (value - high.astype(F32)).astype(BF16)


def three(left, right, dims=NN):
    one = lambda a, b: lax.dot_general(a, b, (dims, ((), ())), preferred_element_type=F32)
    return one(left[0], right[0]) + (one(left[0], right[1]) + one(left[1], right[0]))


def halves(value, keep_ref, send_ref):
    half = value.shape[0] // 2
    odd = is_odd()
    keep_ref[...] = jnp.where(odd, value[half:], value[:half])
    send_ref[...] = jnp.where(odd, value[:half], value[half:])


def joined(mine, other):
    odd = is_odd()
    return jnp.concatenate([jnp.where(odd, other, mine), jnp.where(odd, mine, other)], axis=0)


def cuts(rows):
    step = -(-rows // (16 * CHUNKS)) * 16
    return [min(c * step, rows) for c in range(CHUNKS + 1)]


def fetch(columns_ref, refs, which, at, sem):
    copies = [
        pltpu.make_async_copy(columns_ref.at[at[c] : at[c + 1], :], ref, sem.at[k])
        for k, (c, ref) in enumerate(zip(which, refs))
    ]
    for copy in copies:
        copy.start()
    for copy in copies:
        copy.wait()


def head(columns):
    rows, width = columns.shape
    at = cuts(rows)

    def body(columns_ref, out_ref, sem):
        fetch(columns_ref, [out_ref], [0], at, sem)

    return kernel_call(body, [columns], [((at[1], width), F32)], [pltpu.SemaphoreType.DMA((1,))], hbm_in=1)[0]


def rest(columns, first):
    rows, width = columns.shape
    at = cuts(rows)
    others = list(range(1, CHUNKS))

    def body(columns_ref, first_ref, *refs):
        outs, (keep_ref, send_ref, sem) = refs[: len(others)], refs[len(others) :]
        fetch(columns_ref, outs, others, at, sem)

        @pl.when(at_root())
        def _():
            total = None
            for ref in (first_ref, *outs):
                pair = split(ref[...])
                part = three(pair, pair, TN)
                total = part if total is None else total + part
            halves(total, keep_ref, send_ref)

    shape = [((at[c + 1] - at[c], width), F32) for c in others] + [((width // 2, width), F32)] * 2
    return kernel_call(body, [columns, first], shape, [pltpu.SemaphoreType.DMA((len(others),))], hbm_in=1)


def eliminate(tile, size):
    lanes = tile.shape[1]
    row = lax.broadcasted_iota(jnp.int32, (size, 1), 0)
    for j in range(0, size, 2):
        low = j // 8 * 8
        tail, at = tile[low:], row[low:]
        k, count = j - low, size - low
        c0 = jnp.broadcast_to(tail[:, j : j + 1], (count, lanes))
        c1 = jnp.broadcast_to(tail[:, j + 1 : j + 2], (count, lanes))
        p00, p01, p11 = c0[k : k + 1], c1[k : k + 1], c1[k + 1 : k + 2]
        r0, r1 = tail[k : k + 1], tail[k + 1 : k + 2]
        scale = 1.0 / (p00 * p11 - p01 * p01)
        q0 = (p11 * r0 - p01 * r1) * scale
        q1 = (p00 * r1 - p01 * r0) * scale
        inner = r0 * (p01 * (1.0 / p00))
        tail = tail - jnp.where(at > j + 1, c0 * q0 + c1 * q1, jnp.where(at == j + 1, inner, 0.0))
        tile = tail if low == 0 else jnp.concatenate([tile[:low], tail], axis=0)
    return tile


def identity(size):
    shape = (size, size)
    same = lax.broadcasted_iota(jnp.int32, shape, 0) == lax.broadcasted_iota(jnp.int32, shape, 1)
    return jnp.where(same, 1.0, 0.0).astype(F32)


def factor(mine, other):
    width = mine.shape[1]

    def body(mine_ref, other_ref, gram_ref, inverse_ref, work_ref):
        @pl.when(at_root())
        def _():
            gram = joined(mine_ref[...], other_ref[...])
            gram_ref[...] = gram
            work_ref[:, :width] = gram
            work_ref[:, width:] = identity(width)
            eye = identity(TILE)
            for start in range(0, width, TILE):
                end = start + TILE
                tile = jnp.concatenate([work_ref[start:end, start:end], eye], axis=1)
                tile = eliminate(tile, TILE)
                pivots = jnp.sum(tile[:, :TILE] * eye, axis=1, keepdims=True)
                block = fine(tile[:, TILE:] * lax.rsqrt(pivots), work_ref[start:end, :])
                work_ref[start:end, :] = block
                if end < width:
                    work_ref[end:, :] = work_ref[end:, :] - fine(block[:, end:width], block, TN)
            inverse_ref[...] = work_ref[:, width:]

    shape = [((width, width), F32)] * 2
    return kernel_call(body, [mine, other], shape, [pltpu.VMEM((width, 2 * width), F32)])


def gather(cols, group, total, chunks, moved, last):
    width = chunks[0].shape[1]
    first = total is None
    flat = [] if first else [total]
    for c, (swapped, parts) in zip(group, moved):
        flat += [chunks[c], *swapped, *parts]

    def body(*refs):
        @pl.when(jnp.logical_not(at_root()))
        def _():
            ins, outs = list(refs[: len(flat)]), list(refs[len(flat) :])
            acc = None if first else ins.pop(0)[...]
            for c, (swapped, parts) in zip(group, moved):
                block = ins.pop(0)[...]
                hub = [ins.pop(0)[...] for _ in swapped]
                parts = [ins.pop(0)[...] for _ in parts]
                got = sum(parts[1:], parts[0])
                if hub:
                    got = jnp.where(lax.axis_index("col") == cols // 2 + 1 - c % 2, hub[0], got)
                pair = split(got)
                outs.pop(0)[...] = pair[0]
                outs.pop(0)[...] = pair[1]
                part = three(pair, split(block), TN)
                acc = part if acc is None else acc + part
            if last:
                halves(acc, *outs)
            else:
                outs[0][...] = acc

    shape = [(chunks[c].shape, BF16) for c in group for _ in range(2)]
    shape += [((width // 2, width), F32)] * 2 if last else [((width, width), F32)]
    return kernel_call(body, flat, shape)


def finish(inverse, gram, mine, other, chunks, sent, pairs):
    width = chunks[0].shape[1]
    rows = sum(c.shape[0] for c in chunks)
    at = cuts(rows)

    def body(own_ref, gram_ref, mine_ref, other_ref, *refs):
        blocks, refs = refs[:CHUNKS], refs[CHUNKS:]
        moved, refs = refs[: len(sent)], refs[len(sent) :]
        held, refs = refs[: 2 * CHUNKS], refs[2 * CHUNKS :]
        out_ref, projected_ref, buffer_ref, small_ref, sem = refs

        def store(value):
            small_ref[...] = value
            pltpu.make_async_copy(small_ref, projected_ref, sem.at[CHUNKS]).start()

        def put(c, value):
            there = pl.ds(at[c], at[c + 1] - at[c])
            buffer_ref[there, :] = value
            pltpu.make_async_copy(buffer_ref.at[there, :], out_ref.at[there, :], sem.at[c]).start()

        @pl.when(at_root())
        def _():
            store(fine(own_ref[...], gram_ref[...]))
            weight = split(own_ref[...].T)
            for c in range(CHUNKS):
                put(c, three(split(blocks[c][...]), weight))

        @pl.when(jnp.logical_not(at_root()))
        def _():
            parts = [ref[...] for ref in moved]
            got = sum(parts[1:], parts[0])
            projected = fine(got, joined(mine_ref[...], other_ref[...]))
            store(projected)
            weight = split(fine(got, projected, TN))
            for c in range(CHUNKS):
                put(c, blocks[c][...] - three((held[2 * c][...], held[2 * c + 1][...]), weight))

        for c in range(CHUNKS):
            there = pl.ds(at[c], at[c + 1] - at[c])
            pltpu.make_async_copy(buffer_ref.at[there, :], out_ref.at[there, :], sem.at[c]).wait()
        pltpu.make_async_copy(small_ref, projected_ref, sem.at[CHUNKS]).wait()

    return kernel_call(
        body,
        [inverse, gram, mine, other, *chunks, *sent, *pairs],
        [((rows, width), F32), ((width, width), F32)],
        [
            pltpu.VMEM((rows, width), F32),
            pltpu.VMEM((width, width), F32),
            pltpu.SemaphoreType.DMA((CHUNKS + 1,)),
        ],
        hbm_out=2,
        room=16,
    )


def added(values):
    def body(*refs):
        total = refs[0][...]
        for ref in refs[1:-1]:
            total = total + ref[...]
        refs[-1][...] = total

    return kernel_call(body, values, [(values[0].shape, F32)])[0]


def exchange(mine, send, rows, cols, members, two):
    def swap(part, bit):
        pairs = [(r * cols + c, (r ^ (bit if c in members else 1)) * cols + c) for r in range(rows) for c in range(cols)]
        return lax.ppermute(part, ("row", "col"), pairs)

    mine = added([mine, swap(send, 1)])
    bit = 2
    while bit < rows:
        bits = [bit, 2 * bit, 3 * bit] if two and 2 * bit < rows else [bit]
        mine = added([mine] + [swap(mine, b) for b in bits])
        bit *= 4 if len(bits) > 1 else 2
    return mine, swap(mine, 1)


def hop(value, pairs):
    return lax.ppermute(value, "col", pairs)


def outward(parts, cols):
    down, up = cols // 2 - 1, cols // 2 + 2
    while down > 1 or up + 1 < cols:
        pairs = ([(down, down - 1)] if down > 1 else []) + ([(up, up + 1)] if up + 1 < cols else [])
        parts.append(hop(parts[-1], pairs))
        down, up = down - 1, up + 1


def spread(chunks, cols):
    lower, upper = cols // 2, cols // 2 + 1
    if cols < 4:
        return [([], [hop(v, [(0, c)]) for c in range(1, cols)]) for v in chunks]
    parts = [[hop(v, [(0, upper if c % 2 else lower)])] for c, v in enumerate(chunks)]
    swaps = [[] for _ in chunks]
    for p in range(PAIRS + 1):
        here = [c for c in (2 * p, 2 * p + 1) if c < len(chunks)]
        for c in here:
            hub = upper if c % 2 else lower
            sides = [hop(parts[c][0], [(hub, lower - 1)])]
            if upper + 1 < cols:
                sides.append(hop(parts[c][0], [(hub, upper + 1)]))
                sides = [sum(sides[1:], sides[0])]
            parts[c] += sides
            outward(parts[c], cols)
        held = [parts[c][0] for c in here]
        pairs = [(lower, upper), (upper, lower)][: len(here)]
        swapped = hop(added(held) if len(held) > 1 else held[0], pairs)
        for c in here:
            swaps[c].append(swapped)
    return list(zip(swaps, parts))


def spread_last(value, cols):
    hub = max(cols // 2, 1)
    held = hop(value, [(0, hub)])
    parts = [held]
    ends = [(hub, hub - 1), (hub, hub + 1)]
    sides = [hop(held, [e]) for e in ends if 0 < e[1] < cols]
    parts += sides
    tail = sum(sides[1:], sides[0]) if sides else None
    down, up = hub - 1, hub + 1
    while down > 1 or up + 1 < cols:
        pairs = ([(down, down - 1)] if down > 1 else []) + ([(up, up + 1)] if up + 1 < cols else [])
        tail = hop(tail, pairs)
        parts.append(tail)
        down, up = down - 1, up + 1
    return parts


def solution(mesh):
    rows, cols = mesh.shape["row"], mesh.shape["col"]

    def per_device(columns):
        first = head(columns)
        *others, keep, send = rest(columns, first)
        chunks = [first, *others]
        moved = spread(chunks, cols)
        gram, inverse = factor(*exchange(keep, send, rows, cols, (0,), False))
        sent = spread_last(inverse, cols)
        total, pairs = None, []
        for group in GROUPS:
            got = gather(cols, group, total, chunks, [moved[c] for c in group], group == GROUPS[-1])
            pairs, total = [*pairs, *got[: 2 * len(group)]], got[2 * len(group)]
        total = exchange(*got[-2:], rows, cols, tuple(range(1, cols)), True)
        return tuple(finish(inverse, gram, *total, chunks, sent, pairs))

    return jax.shard_map(
        per_device, mesh=mesh, in_specs=(P("row", "col"),), out_specs=(P("row", "col"), P(None, "col")), check_vma=False
    )
```

time: 240 us -> 114 us (0.47)
  the two profiles are of different devices: /device:TPU:0 before, /device:TPU:8 now
where the time goes in v3:
time: 114 us
  waiting for transfers between devices  72 us (63%)
  starting transfers between devices  32.6 us (29%)
  Pallas kernels  7.82 us (7%)
  between operations  1.34 us (1%)
    ppermute x31, waiting for transfers between devices, hop(): return lax.ppermute(value, 'col', pairs)  65.5 us
    ppermute x31, starting transfers between devices, hop(): return lax.ppermute(value, 'col', pairs)  28.2 us
    pallas_call x18, Pallas kernels, kernel_call(): pl.pallas_call(body, out_shape=tuple(shapes), in_specs=[ANY] * hbm_in + [...  7.82 us
    ppermute x9, waiting for transfers between devices, swap(): return lax.ppermute(part, ('row', 'col'), pairs)  6.55 us
    ppermute x9, starting transfers between devices, swap(): return lax.ppermute(part, ('row', 'col'), pairs)  4.42 us
  transfers between devices with their start and end apart: 40, of which 16 were waited for; matrix products, arithmetic and copies ran while one was open for 0% of the time, Pallas kernels for 2%

profile of v3, /device:TPU:8, one launch (start us, length us, event | category | flops | bytes accessed | tf_op | source)
XLA Modules:
  0.0 113.8 jit_solution(2270223498549248852)
XLA Ops:
  0.6 0.9 shard_map.30.first_ref.refs_0_
  1.6 1.6 %shard_map.31 = (f32[192,256]{1,0:T(8,128)S(1)}, f32[192,256]{1,0:T(8,128)S(1)}, f32[192,256]{1,0:T(8,128)S(1)}, f32[192,256]{1,0:T(8,128)S(1)}, f32[192,256]{1,...) custom-call(f32[2048,256]{1,0:T(8,128)} %columns_ref.3, ...), custom_call_target="tpu_custom_call" | custom-call | tf_op jit(solution)/shard_map/pallas_call | solution.py:34
  11.4 1.3 %collective-permute-start.7 = (f32[192,256]{1,0:T(8,128)S(1)}, f32[192,256]{1,0:T(8,128)S(1)}, u32[]{:S(2)}, u32[]{:S(2)}) collective-permute-start(f32[192,256]{1,0:T(8,128)S(1)} %collective-permute-done.4.refs_0_.refs_2_), channel_id=1, source_target_pairs={{2,1},{6,5},{10,9},{14,13},{18,17},{22,21},{26,25},{30,29}} | collective-permute-start | bytes 589832 | tf_op jit(solution)/shard_map/ppermute | solution.py:285
  13.6 1.3 %collective-permute-start.8 = (f32[192,256]{1,0:T(8,128)S(1)}, f32[192,256]{1,0:T(8,128)S(1)}, u32[]{:S(2)}, u32[]{:S(2)}) collective-permute-start(f32[192,256]{1,0:T(8,128)S(1)} %collective-permute-done.5.refs_1_.refs_6_), channel_id=1, source_target_pairs={{3,1},{7,5},{11,9},{15,13},{19,17},{23,21},{27,25},{31,29}} | collective-permute-start | bytes 589832 | tf_op jit(solution)/shard_map/ppermute | solution.py:285
  14.9 1.3 %collective-permute-start.12 = (f32[192,256]{1,0:T(8,128)S(1)}, f32[192,256]{1,0:T(8,128)S(1)}, u32[]{:S(2)}, u32[]{:S(2)}) collective-permute-start(f32[192,256]{1,0:T(8,128)S(1)} %collective-permute-done.9.refs_0_.refs_10_), channel_id=1, source_target_pairs={{2,1},{6,5},{10,9},{14,13},{18,17},{22,21},{26,25},{30,29}} | collective-permute-start | bytes 589832 | tf_op jit(solution)/shard_map/ppermute | solution.py:285
  16.9 25.7 %collective-permute-done.7.refs_3_ = f32[192,256]{1,0:T(8,128)S(1)} collective-permute-done((f32[192,256]{1,0:T(8,128)S(1)}, f32[192,256]{1,0:T(8,128)S(1)}, u32[]{:S(2)}, u32[]{:S(2)}) %collective-permute-start.7) | collective-permute-done | bytes 196640 | tf_op jit(solution)/shard_map/ppermute | solution.py:285
  42.6 1.3 %collective-permute-start.13 = (f32[192,256]{1,0:T(8,128)S(1)}, f32[192,256]{1,0:T(8,128)S(1)}, u32[]{:S(2)}, u32[]{:S(2)}) collective-permute-start(f32[192,256]{1,0:T(8,128)S(1)} %collective-permute-done.10.refs_1_.refs_14_), channel_id=1, source_target_pairs={{3,1},{7,5},{11,9},{15,13},{19,17},{23,21},{27,25},{31,29}} | collective-permute-start | bytes 589832 | tf_op jit(solution)/shard_map/ppermute | solution.py:285
  43.9 1.3 %collective-permute-start.17 = (f32[192,256]{1,0:T(8,128)S(1)}, f32[192,256]{1,0:T(8,128)S(1)}, u32[]{:S(2)}, u32[]{:S(2)}) collective-permute-start(f32[192,256]{1,0:T(8,128)S(1)} %collective-permute-done.14.refs_0_.refs_3_), channel_id=1, source_target_pairs={{2,1},{6,5},{10,9},{14,13},{18,17},{22,21},{26,25},{30,29}} | collective-permute-start | bytes 589832 | tf_op jit(solution)/shard_map/ppermute | solution.py:285
  45.2 13.8 %collective-permute-done.8.refs_7_ = f32[192,256]{1,0:T(8,128)S(1)} collective-permute-done((f32[192,256]{1,0:T(8,128)S(1)}, f32[192,256]{1,0:T(8,128)S(1)}, u32[]{:S(2)}, u32[]{:S(2)}) %collective-permute-start.8) | collective-permute-done | bytes 196640 | tf_op jit(solution)/shard_map/ppermute | solution.py:285
  59.7 2.3 %collective-permute-done.12.refs_11_ = f32[192,256]{1,0:T(8,128)S(1)} collective-permute-done((f32[192,256]{1,0:T(8,128)S(1)}, f32[192,256]{1,0:T(8,128)S(1)}, u32[]{:S(2)}, u32[]{:S(2)}) %collective-permute-start.12) | collective-permute-done | bytes 196640 | tf_op jit(solution)/shard_map/ppermute | solution.py:285
  62.0 1.3 %collective-permute-start.18 = (f32[192,256]{1,0:T(8,128)S(1)}, f32[192,256]{1,0:T(8,128)S(1)}, u32[]{:S(2)}, u32[]{:S(2)}) collective-permute-start(f32[192,256]{1,0:T(8,128)S(1)} %collective-permute-done.15.refs_1_.refs_7_), channel_id=1, source_target_pairs={{3,1},{7,5},{11,9},{15,13},{19,17},{23,21},{27,25},{31,29}} | collective-permute-start | bytes 589832 | tf_op jit(solution)/shard_map/ppermute | solution.py:285
  63.3 1.3 %collective-permute-start.22 = (f32[192,256]{1,0:T(8,128)S(1)}, f32[192,256]{1,0:T(8,128)S(1)}, u32[]{:S(2)}, u32[]{:S(2)}) collective-permute-start(f32[192,256]{1,0:T(8,128)S(1)} %collective-permute-done.19.refs_0_.refs_11_), channel_id=1, source_target_pairs={{2,1},{6,5},{10,9},{14,13},{18,17},{22,21},{26,25},{30,29}} | collective-permute-start | bytes 589832 | tf_op jit(solution)/shard_map/ppermute | solution.py:285
  64.6 4.7 %collective-permute-done.13.refs_15_ = f32[192,256]{1,0:T(8,128)S(1)} collective-permute-done((f32[192,256]{1,0:T(8,128)S(1)}, f32[192,256]{1,0:T(8,128)S(1)}, u32[]{:S(2)}, u32[]{:S(2)}) %collective-permute-start.13) | collective-permute-done | bytes 196640 | tf_op jit(solution)/shard_map/ppermute | solution.py:285
  70.0 1.8 %collective-permute-done.17.refs_4_ = f32[192,256]{1,0:T(8,128)S(1)} collective-permute-done((f32[192,256]{1,0:T(8,128)S(1)}, f32[192,256]{1,0:T(8,128)S(1)}, u32[]{:S(2)}, u32[]{:S(2)}) %collective-permute-start.17) | collective-permute-done | bytes 196640 | tf_op jit(solution)/shard_map/ppermute | solution.py:285
  71.8 1.3 %collective-permute-start.23 = (f32[192,256]{1,0:T(8,128)S(1)}, f32[192,256]{1,0:T(8,128)S(1)}, u32[]{:S(2)}, u32[]{:S(2)}) collective-permute-start(f32[192,256]{1,0:T(8,128)S(1)} %collective-permute-done.20.refs_1_.refs_15_), channel_id=1, source_target_pairs={{3,1},{7,5},{11,9},{15,13},{19,17},{23,21},{27,25},{31,29}} | collective-permute-start | bytes 589832 | tf_op jit(solution)/shard_map/ppermute | solution.py:285
  73.1 1.3 %collective-permute-start.27 = (f32[192,256]{1,0:T(8,128)S(1)}, f32[192,256]{1,0:T(8,128)S(1)}, u32[]{:S(2)}, u32[]{:S(2)}) collective-permute-start(f32[192,256]{1,0:T(8,128)S(1)} %collective-permute-done.24.refs_0_.refs_3_), channel_id=1, source_target_pairs={{2,1},{6,5},{10,9},{14,13},{18,17},{22,21},{26,25},{30,29}} | collective-permute-start | bytes 589832 | tf_op jit(solution)/shard_map/ppermute | solution.py:285
  74.4 3.4 %collective-permute-done.18.refs_8_ = f32[192,256]{1,0:T(8,128)S(1)} collective-permute-done((f32[192,256]{1,0:T(8,128)S(1)}, f32[192,256]{1,0:T(8,128)S(1)}, u32[]{:S(2)}, u32[]{:S(2)}) %collective-permute-start.18) | collective-permute-done | bytes 196640 | tf_op jit(solution)/shard_map/ppermute | solution.py:285
  77.8 2.3 %collective-permute-done.22.refs_12_ = f32[192,256]{1,0:T(8,128)S(1)} collective-permute-done((f32[192,256]{1,0:T(8,128)S(1)}, f32[192,256]{1,0:T(8,128)S(1)}, u32[]{:S(2)}, u32[]{:S(2)}) %collective-permute-start.22) | collective-permute-done | bytes 196640 | tf_op jit(solution)/shard_map/ppermute | solution.py:285
  80.8 1.3 %collective-permute-start.28 = (f32[192,256]{1,0:T(8,128)S(1)}, f32[192,256]{1,0:T(8,128)S(1)}, u32[]{:S(2)}, u32[]{:S(2)}) collective-permute-start(f32[192,256]{1,0:T(8,128)S(1)} %collective-permute-done.25.refs_1_.refs_7_), channel_id=1, source_target_pairs={{3,1},{7,5},{11,9},{15,13},{19,17},{23,21},{27,25},{31,29}} | collective-permute-start | bytes 589832 | tf_op jit(solution)/shard_map/ppermute | solution.py:285
  82.1 4.1 %collective-permute-done.23.refs_16_ = f32[192,256]{1,0:T(8,128)S(1)} collective-permute-done((f32[192,256]{1,0:T(8,128)S(1)}, f32[192,256]{1,0:T(8,128)S(1)}, u32[]{:S(2)}, u32[]{:S(2)}) %collective-permute-start.23) | collective-permute-done | bytes 196640 | tf_op jit(solution)/shard_map/ppermute | solution.py:285
  86.3 1.3 %collective-permute-start.31 = (f32[128,256]{1,0:T(8,128)S(1)}, f32[128,256]{1,0:T(8,128)S(1)}, u32[]{:S(2)}, u32[]{:S(2)}) collective-permute-start(f32[128,256]{1,0:T(8,128)S(1)} %collective-permute-done.29.refs_3_), channel_id=1, source_target_pairs={{2,1},{6,5},{10,9},{14,13},{18,17},{22,21},{26,25},{30,29}} | collective-permute-start | bytes 393224 | tf_op jit(solution)/shard_map/ppermute | solution.py:285
  89.0 0.7 shard_map.38
  90.4 3.3 %collective-permute-done.28.refs_8_ = f32[192,256]{1,0:T(8,128)S(1)} collective-permute-done((f32[192,256]{1,0:T(8,128)S(1)}, f32[192,256]{1,0:T(8,128)S(1)}, u32[]{:S(2)}, u32[]{:S(2)}) %collective-permute-start.28) | collective-permute-done | bytes 196640 | tf_op jit(solution)/shard_map/ppermute | solution.py:285
  94.1 1.3 %collective-permute-done.31.refs_4_ = f32[128,256]{1,0:T(8,128)S(1)} collective-permute-done((f32[128,256]{1,0:T(8,128)S(1)}, f32[128,256]{1,0:T(8,128)S(1)}, u32[]{:S(2)}, u32[]{:S(2)}) %collective-permute-start.31) | collective-permute-done | bytes 131104 | tf_op jit(solution)/shard_map/ppermute | solution.py:285
  95.7 1.3 %collective-permute-done.32.refs_1_ = f32[128,256]{1,0:T(8,128)S(1)} collective-permute-done((f32[128,256]{1,0:T(8,128)S(1)}, f32[128,256]{1,0:T(8,128)S(1)}, u32[]{:S(2)}, u32[]{:S(2)}) %collective-permute-start.32) | collective-permute-done | bytes 131104 | tf_op jit(solution)/shard_map/ppermute | solution.py:273
  97.1 2.5 %collective-permute-start.35 = (f32[128,256]{1,0:T(8,128)S(1)}, f32[128,256]{1,0:T(8,128)S(1)}, u32[]{:S(2)}, u32[]{:S(2)}) collective-permute-start(f32[128,256]{1,0:T(8,128)S(1)} %shard_map.45.refs_0_), channel_id=1, source_target_pairs={{0,4},{1,25},{2,26},{3,27},{4,0},{5,29},{6,30},{7,31},{8,12},{9,17... | collective-permute-start | bytes 393224 | tf_op jit(solution)/shard_map/ppermute | solution.py:273
  101.3 1.3 %collective-permute-start.38 = (f32[256,256]{1,0:T(8,128)S(1)}, f32[256,256]{1,0:T(8,128)S(1)}, u32[]{:S(2)}, u32[]{:S(2)}) collective-permute-start(f32[256,256]{1,0:T(8,128)S(1)} %collective-permute-done.37.refs_11_), channel_id=1, source_target_pairs={{2,1},{6,5},{10,9},{14,13},{18,17},{22,21},{26,25},{30,29}} | collective-permute-start | bytes 786440 | tf_op jit(solution)/shard_map/ppermute | solution.py:285
  102.6 1.3 %collective-permute-done.35.refs_3_ = f32[128,256]{1,0:T(8,128)S(1)} collective-permute-done((f32[128,256]{1,0:T(8,128)S(1)}, f32[128,256]{1,0:T(8,128)S(1)}, u32[]{:S(2)}, u32[]{:S(2)}) %collective-permute-start.35) | collective-permute-done | bytes 131104 | tf_op jit(solution)/shard_map/ppermute | solution.py:273
  104.0 2.5 %collective-permute-done.34.refs_2_ = f32[128,256]{1,0:T(8,128)S(1)} collective-permute-done((f32[128,256]{1,0:T(8,128)S(1)}, f32[128,256]{1,0:T(8,128)S(1)}, u32[]{:S(2)}, u32[]{:S(2)}) %collective-permute-start.34) | collective-permute-done | bytes 131104 | tf_op jit(solution)/shard_map/ppermute | solution.py:273
  106.6 1.3 %collective-permute-done.36.other_ref = f32[128,256]{1,0:T(8,128)S(1)} collective-permute-done((f32[128,256]{1,0:T(8,128)S(1)}, f32[128,256]{1,0:T(8,128)S(1)}, u32[]{:S(2)}, u32[]{:S(2)}) %collective-permute-start.36) | collective-permute-done | bytes 131104 | tf_op jit(solution)/shard_map/ppermute | solution.py:273
  108.0 2.8 %collective-permute-done.38.refs_12_ = f32[256,256]{1,0:T(8,128)S(1)} collective-permute-done((f32[256,256]{1,0:T(8,128)S(1)}, f32[256,256]{1,0:T(8,128)S(1)}, u32[]{:S(2)}, u32[]{:S(2)}) %collective-permute-start.38) | collective-permute-done | bytes 262176 | tf_op jit(solution)/shard_map/ppermute | solution.py:285
  110.7 2.9 %shard_map.47 = (f32[2048,256]{1,0:T(8,128)}, f32[256,256]{1,0:T(8,128)}) custom-call(f32[256,256]{1,0:T(8,128)S(1)} %get-tuple-element.45.own_ref, f32[256,256]{1,0:T(8,128)S(1)} %get-tuple-element.46.gram_ref, f32[128,256]{1,0:T(8,128)S(1)} %shard_map.46.mine_ref, f32[128,256]{1,0:T(8,128)S(1)} %collective-permute-done.36.other_ref, ...), custom_call_target="tpu_custom_call" | custom-call | tf_op jit(solution)/shard_map/pallas_call | solution.py:34
  (66 shorter events, 16.4 us)
Async XLA Ops:
  3.3 4.1 %collective-permute-start.4 = (f32[192,256]{1,0:T(8,128)S(1)}, f32[192,256]{1,0:T(8,128)S(1)}, u32[]{:S(2)}, u32[]{:S(2)}) collective-permute-start(f32[192,256]{1,0:T(8,128)S(1)} %shard_map.30.first_ref.refs_0_), channel_id=1, source_target_pairs={{0,2},{4,6},{8,10},{12,14},{16,18},{20,22},{24,26},{28,30}} | collective-permute-start | bytes 589832 | tf_op jit(solution)/shard_map/ppermute | solution.py:285
  4.7 3.5 %collective-permute-start.5 = (f32[192,256]{1,0:T(8,128)S(1)}, f32[192,256]{1,0:T(8,128)S(1)}, u32[]{:S(2)}, u32[]{:S(2)}) collective-permute-start(f32[192,256]{1,0:T(8,128)S(1)} %get-tuple-element.47.refs_4_.refs_1_), channel_id=1, source_target_pairs={{0,3},{4,7},{8,11},{12,15},{16,19},{20,23},{24,27},{28,31}} | collective-permute-start | bytes 589832 | tf_op jit(solution)/shard_map/ppermute | solution.py:285
  5.3 3.5 %collective-permute-start.9 = (f32[192,256]{1,0:T(8,128)S(1)}, f32[192,256]{1,0:T(8,128)S(1)}, u32[]{:S(2)}, u32[]{:S(2)}) collective-permute-start(f32[192,256]{1,0:T(8,128)S(1)} %get-tuple-element.48.refs_8_.refs_2_), channel_id=1, source_target_pairs={{0,2},{4,6},{8,10},{12,14},{16,18},{20,22},{24,26},{28,30}} | collective-permute-start | bytes 589832 | tf_op jit(solution)/shard_map/ppermute | solution.py:285
  8.1 4.6 %collective-permute-start.19 = (f32[192,256]{1,0:T(8,128)S(1)}, f32[192,256]{1,0:T(8,128)S(1)}, u32[]{:S(2)}, u32[]{:S(2)}) collective-permute-start(f32[192,256]{1,0:T(8,128)S(1)} %get-tuple-element.53.refs_9_.refs_6_), channel_id=1, source_target_pairs={{0,2},{4,6},{8,10},{12,14},{16,18},{20,22},{24,26},{28,30}} | collective-permute-start | bytes 589832 | tf_op jit(solution)/shard_map/ppermute | solution.py:285
  9.4 3.5 %collective-permute-start.20 = (f32[192,256]{1,0:T(8,128)S(1)}, f32[192,256]{1,0:T(8,128)S(1)}, u32[]{:S(2)}, u32[]{:S(2)}) collective-permute-start(f32[192,256]{1,0:T(8,128)S(1)} %get-tuple-element.54.refs_13_.refs_7_), channel_id=1, source_target_pairs={{0,3},{4,7},{8,11},{12,15},{16,19},{20,23},{24,27},{28,31}} | collective-permute-start | bytes 589832 | tf_op jit(solution)/shard_map/ppermute | solution.py:285
  10.1 3.5 %collective-permute-start.24 = (f32[192,256]{1,0:T(8,128)S(1)}, f32[192,256]{1,0:T(8,128)S(1)}, u32[]{:S(2)}, u32[]{:S(2)}) collective-permute-start(f32[192,256]{1,0:T(8,128)S(1)} %get-tuple-element.56.refs_1_.refs_8_), channel_id=1, source_target_pairs={{0,2},{4,6},{8,10},{12,14},{16,18},{20,22},{24,26},{28,30}} | collective-permute-start | bytes 589832 | tf_op jit(solution)/shard_map/ppermute | solution.py:285
  10.8 4.2 %collective-permute-start.25 = (f32[192,256]{1,0:T(8,128)S(1)}, f32[192,256]{1,0:T(8,128)S(1)}, u32[]{:S(2)}, u32[]{:S(2)}) collective-permute-start(f32[192,256]{1,0:T(8,128)S(1)} %get-tuple-element.57.refs_5_.refs_9_), channel_id=1, source_target_pairs={{0,3},{4,7},{8,11},{12,15},{16,19},{20,23},{24,27},{28,31}} | collective-permute-start | bytes 589832 | tf_op jit(solution)/shard_map/ppermute | solution.py:285
  11.4 31.1 %collective-permute-start.7 = (f32[192,256]{1,0:T(8,128)S(1)}, f32[192,256]{1,0:T(8,128)S(1)}, u32[]{:S(2)}, u32[]{:S(2)}) collective-permute-start(f32[192,256]{1,0:T(8,128)S(1)} %collective-permute-done.4.refs_0_.refs_2_), channel_id=1, source_target_pairs={{2,1},{6,5},{10,9},{14,13},{18,17},{22,21},{26,25},{30,29}} | collective-permute-start | bytes 589832 | tf_op jit(solution)/shard_map/ppermute | solution.py:285
  12.8 3.5 %collective-permute-start.2 = (f32[128,256]{1,0:T(8,128)S(1)}, f32[128,256]{1,0:T(8,128)S(1)}, u32[]{:S(2)}, u32[]{:S(2)}) collective-permute-start(f32[128,256]{1,0:T(8,128)S(1)} %shard_map.33.refs_0_), channel_id=1, source_target_pairs={{0,16},{1,5},{2,6},{3,7},{4,20},{5,1},{6,2},{7,3},{8,24},{9,13},{1... | collective-permute-start | bytes 393224 | tf_op jit(solution)/shard_map/ppermute | solution.py:273
  12.9 31.0 %collective-permute-start.6 = (f32[192,256]{1,0:T(8,128)S(1)}, f32[192,256]{1,0:T(8,128)S(1)}, u32[]{:S(2)}, u32[]{:S(2)}) collective-permute-start(f32[192,256]{1,0:T(8,128)S(1)} %shard_map.36), channel_id=1, source_target_pairs={{2,3},{3,2},{6,7},{7,6},{10,11},{11,10},{14,15},{15,14},{18,19},{1... | collective-permute-start | bytes 589832 | tf_op jit(solution)/shard_map/ppermute | solution.py:285
  13.6 45.5 %collective-permute-start.8 = (f32[192,256]{1,0:T(8,128)S(1)}, f32[192,256]{1,0:T(8,128)S(1)}, u32[]{:S(2)}, u32[]{:S(2)}) collective-permute-start(f32[192,256]{1,0:T(8,128)S(1)} %collective-permute-done.5.refs_1_.refs_6_), channel_id=1, source_target_pairs={{3,1},{7,5},{11,9},{15,13},{19,17},{23,21},{27,25},{31,29}} | collective-permute-start | bytes 589832 | tf_op jit(solution)/shard_map/ppermute | solution.py:285
  14.9 47.1 %collective-permute-start.12 = (f32[192,256]{1,0:T(8,128)S(1)}, f32[192,256]{1,0:T(8,128)S(1)}, u32[]{:S(2)}, u32[]{:S(2)}) collective-permute-start(f32[192,256]{1,0:T(8,128)S(1)} %collective-permute-done.9.refs_0_.refs_10_), channel_id=1, source_target_pairs={{2,1},{6,5},{10,9},{14,13},{18,17},{22,21},{26,25},{30,29}} | collective-permute-start | bytes 589832 | tf_op jit(solution)/shard_map/ppermute | solution.py:285
  16.3 47.1 %collective-permute-start.11 = (f32[192,256]{1,0:T(8,128)S(1)}, f32[192,256]{1,0:T(8,128)S(1)}, u32[]{:S(2)}, u32[]{:S(2)}) collective-permute-start(f32[192,256]{1,0:T(8,128)S(1)} %shard_map.37), channel_id=1, source_target_pairs={{2,3},{3,2},{6,7},{7,6},{10,11},{11,10},{14,15},{15,14},{18,19},{1... | collective-permute-start | bytes 589832 | tf_op jit(solution)/shard_map/ppermute | solution.py:285
  42.6 26.7 %collective-permute-start.13 = (f32[192,256]{1,0:T(8,128)S(1)}, f32[192,256]{1,0:T(8,128)S(1)}, u32[]{:S(2)}, u32[]{:S(2)}) collective-permute-start(f32[192,256]{1,0:T(8,128)S(1)} %collective-permute-done.10.refs_1_.refs_14_), channel_id=1, source_target_pairs={{3,1},{7,5},{11,9},{15,13},{19,17},{23,21},{27,25},{31,29}} | collective-permute-start | bytes 589832 | tf_op jit(solution)/shard_map/ppermute | solution.py:285
  43.9 27.9 %collective-permute-start.17 = (f32[192,256]{1,0:T(8,128)S(1)}, f32[192,256]{1,0:T(8,128)S(1)}, u32[]{:S(2)}, u32[]{:S(2)}) collective-permute-start(f32[192,256]{1,0:T(8,128)S(1)} %collective-permute-done.14.refs_0_.refs_3_), channel_id=1, source_target_pairs={{2,1},{6,5},{10,9},{14,13},{18,17},{22,21},{26,25},{30,29}} | collective-permute-start | bytes 589832 | tf_op jit(solution)/shard_map/ppermute | solution.py:285
  59.1 14.0 %collective-permute-start.16 = (f32[192,256]{1,0:T(8,128)S(1)}, f32[192,256]{1,0:T(8,128)S(1)}, u32[]{:S(2)}, u32[]{:S(2)}) collective-permute-start(f32[192,256]{1,0:T(8,128)S(1)} %shard_map.39), channel_id=1, source_target_pairs={{2,3},{3,2},{6,7},{7,6},{10,11},{11,10},{14,15},{15,14},{18,19},{1... | collective-permute-start | bytes 589832 | tf_op jit(solution)/shard_map/ppermute | solution.py:285
  62.0 15.8 %collective-permute-start.18 = (f32[192,256]{1,0:T(8,128)S(1)}, f32[192,256]{1,0:T(8,128)S(1)}, u32[]{:S(2)}, u32[]{:S(2)}) collective-permute-start(f32[192,256]{1,0:T(8,128)S(1)} %collective-permute-done.15.refs_1_.refs_7_), channel_id=1, source_target_pairs={{3,1},{7,5},{11,9},{15,13},{19,17},{23,21},{27,25},{31,29}} | collective-permute-start | bytes 589832 | tf_op jit(solution)/shard_map/ppermute | solution.py:285
  63.3 16.8 %collective-permute-start.22 = (f32[192,256]{1,0:T(8,128)S(1)}, f32[192,256]{1,0:T(8,128)S(1)}, u32[]{:S(2)}, u32[]{:S(2)}) collective-permute-start(f32[192,256]{1,0:T(8,128)S(1)} %collective-permute-done.19.refs_0_.refs_11_), channel_id=1, source_target_pairs={{2,1},{6,5},{10,9},{14,13},{18,17},{22,21},{26,25},{30,29}} | collective-permute-start | bytes 589832 | tf_op jit(solution)/shard_map/ppermute | solution.py:285
  69.3 11.5 %collective-permute-start.21 = (f32[192,256]{1,0:T(8,128)S(1)}, f32[192,256]{1,0:T(8,128)S(1)}, u32[]{:S(2)}, u32[]{:S(2)}) collective-permute-start(f32[192,256]{1,0:T(8,128)S(1)} %shard_map.40), channel_id=1, source_target_pairs={{2,3},{3,2},{6,7},{7,6},{10,11},{11,10},{14,15},{15,14},{18,19},{1... | collective-permute-start | bytes 589832 | tf_op jit(solution)/shard_map/ppermute | solution.py:285
  71.8 14.5 %collective-permute-start.23 = (f32[192,256]{1,0:T(8,128)S(1)}, f32[192,256]{1,0:T(8,128)S(1)}, u32[]{:S(2)}, u32[]{:S(2)}) collective-permute-start(f32[192,256]{1,0:T(8,128)S(1)} %collective-permute-done.20.refs_1_.refs_15_), channel_id=1, source_target_pairs={{3,1},{7,5},{11,9},{15,13},{19,17},{23,21},{27,25},{31,29}} | collective-permute-start | bytes 589832 | tf_op jit(solution)/shard_map/ppermute | solution.py:285
  73.1 15.2 %collective-permute-start.27 = (f32[192,256]{1,0:T(8,128)S(1)}, f32[192,256]{1,0:T(8,128)S(1)}, u32[]{:S(2)}, u32[]{:S(2)}) collective-permute-start(f32[192,256]{1,0:T(8,128)S(1)} %collective-permute-done.24.refs_0_.refs_3_), channel_id=1, source_target_pairs={{2,1},{6,5},{10,9},{14,13},{18,17},{22,21},{26,25},{30,29}} | collective-permute-start | bytes 589832 | tf_op jit(solution)/shard_map/ppermute | solution.py:285
  77.8 9.8 %collective-permute-start.3 = (f32[128,256]{1,0:T(8,128)S(1)}, f32[128,256]{1,0:T(8,128)S(1)}, u32[]{:S(2)}, u32[]{:S(2)}) collective-permute-start(f32[128,256]{1,0:T(8,128)S(1)} %shard_map.34.mine_ref), channel_id=1, source_target_pairs={{0,4},{1,5},{2,6},{3,7},{4,0},{5,1},{6,2},{7,3},{8,12},{9,13},{10,... | collective-permute-start | bytes 393224 | tf_op jit(solution)/shard_map/ppermute | solution.py:273
  80.2 10.2 %collective-permute-start.26 = (f32[192,256]{1,0:T(8,128)S(1)}, f32[192,256]{1,0:T(8,128)S(1)}, u32[]{:S(2)}, u32[]{:S(2)}) collective-permute-start(f32[192,256]{1,0:T(8,128)S(1)} %shard_map.42), channel_id=1, source_target_pairs={{2,3},{3,2},{6,7},{7,6},{10,11},{11,10},{14,15},{15,14},{18,19},{1... | collective-permute-start | bytes 589832 | tf_op jit(solution)/shard_map/ppermute | solution.py:285
  80.8 12.8 %collective-permute-start.28 = (f32[192,256]{1,0:T(8,128)S(1)}, f32[192,256]{1,0:T(8,128)S(1)}, u32[]{:S(2)}, u32[]{:S(2)}) collective-permute-start(f32[192,256]{1,0:T(8,128)S(1)} %collective-permute-done.25.refs_1_.refs_7_), channel_id=1, source_target_pairs={{3,1},{7,5},{11,9},{15,13},{19,17},{23,21},{27,25},{31,29}} | collective-permute-start | bytes 589832 | tf_op jit(solution)/shard_map/ppermute | solution.py:285
  86.3 9.1 %collective-permute-start.31 = (f32[128,256]{1,0:T(8,128)S(1)}, f32[128,256]{1,0:T(8,128)S(1)}, u32[]{:S(2)}, u32[]{:S(2)}) collective-permute-start(f32[128,256]{1,0:T(8,128)S(1)} %collective-permute-done.29.refs_3_), channel_id=1, source_target_pairs={{2,1},{6,5},{10,9},{14,13},{18,17},{22,21},{26,25},{30,29}} | collective-permute-start | bytes 393224 | tf_op jit(solution)/shard_map/ppermute | solution.py:285
  87.6 7.8 %collective-permute-start.30 = (f32[128,256]{1,0:T(8,128)S(1)}, f32[128,256]{1,0:T(8,128)S(1)}, u32[]{:S(2)}, u32[]{:S(2)}) collective-permute-start(f32[128,256]{1,0:T(8,128)S(1)} %collective-permute-done.29.refs_3_), channel_id=1, source_target_pairs={{2,3},{6,7},{10,11},{14,15},{18,19},{22,23},{26,27},{30,31}} | collective-permute-start | bytes 393224 | tf_op jit(solution)/shard_map/ppermute | solution.py:285
  88.3 12.4 %collective-permute-start.37 = (f32[256,256]{1,0:T(8,128)S(1)}, f32[256,256]{1,0:T(8,128)S(1)}, u32[]{:S(2)}, u32[]{:S(2)}) collective-permute-start(f32[256,256]{1,0:T(8,128)S(1)} %get-tuple-element.45.own_ref), channel_id=1, source_target_pairs={{0,2},{4,6},{8,10},{12,14},{16,18},{20,22},{24,26},{28,30}} | collective-permute-start | bytes 786440 | tf_op jit(solution)/shard_map/ppermute | solution.py:285
  97.1 6.9 %collective-permute-start.35 = (f32[128,256]{1,0:T(8,128)S(1)}, f32[128,256]{1,0:T(8,128)S(1)}, u32[]{:S(2)}, u32[]{:S(2)}) collective-permute-start(f32[128,256]{1,0:T(8,128)S(1)} %shard_map.45.refs_0_), channel_id=1, source_target_pairs={{0,4},{1,25},{2,26},{3,27},{4,0},{5,29},{6,30},{7,31},{8,12},{9,17... | collective-permute-start | bytes 393224 | tf_op jit(solution)/shard_map/ppermute | solution.py:273
  99.6 6.8 %collective-permute-start.34 = (f32[128,256]{1,0:T(8,128)S(1)}, f32[128,256]{1,0:T(8,128)S(1)}, u32[]{:S(2)}, u32[]{:S(2)}) collective-permute-start(f32[128,256]{1,0:T(8,128)S(1)} %shard_map.45.refs_0_), channel_id=1, source_target_pairs={{0,4},{1,17},{2,18},{3,19},{4,0},{5,21},{6,22},{7,23},{8,12},{9,25... | collective-permute-start | bytes 393224 | tf_op jit(solution)/shard_map/ppermute | solution.py:273
  100.1 6.4 %collective-permute-start.33 = (f32[128,256]{1,0:T(8,128)S(1)}, f32[128,256]{1,0:T(8,128)S(1)}, u32[]{:S(2)}, u32[]{:S(2)}) collective-permute-start(f32[128,256]{1,0:T(8,128)S(1)} %shard_map.45.refs_0_), channel_id=1, source_target_pairs={{0,4},{1,9},{2,10},{3,11},{4,0},{5,13},{6,14},{7,15},{8,12},{9,1},... | collective-permute-start | bytes 393224 | tf_op jit(solution)/shard_map/ppermute | solution.py:273
  100.7 7.3 %collective-permute-start.39 = (f32[256,256]{1,0:T(8,128)S(1)}, f32[256,256]{1,0:T(8,128)S(1)}, u32[]{:S(2)}, u32[]{:S(2)}) collective-permute-start(f32[256,256]{1,0:T(8,128)S(1)} %collective-permute-done.37.refs_11_), channel_id=1, source_target_pairs={{2,3},{6,7},{10,11},{14,15},{18,19},{22,23},{26,27},{30,31}} | collective-permute-start | bytes 786440 | tf_op jit(solution)/shard_map/ppermute | solution.py:285
  101.3 9.4 %collective-permute-start.38 = (f32[256,256]{1,0:T(8,128)S(1)}, f32[256,256]{1,0:T(8,128)S(1)}, u32[]{:S(2)}, u32[]{:S(2)}) collective-permute-start(f32[256,256]{1,0:T(8,128)S(1)} %collective-permute-done.37.refs_11_), channel_id=1, source_target_pairs={{2,1},{6,5},{10,9},{14,13},{18,17},{22,21},{26,25},{30,29}} | collective-permute-start | bytes 786440 | tf_op jit(solution)/shard_map/ppermute | solution.py:285
  (8 other events, 21.0 us)

commit v4 on v3

--- a/solution.py
+++ b/solution.py
@@ -6,9 +6,8 @@
 from jax.sharding import PartitionSpec as P
 
 
-PAIRS = 5
-CHUNKS = 2 * PAIRS + 1
-GROUPS = ((0, 1, 2, 3), (4, 5, 6, 7), (8, 9), (10,))
+CHUNKS = 11
+GROUPS = ((0, 1, 2, 3), (4, 5, 6), (7, 8), (9,), (10,))
 TILE = 64
 F32 = jnp.float32
 BF16 = jnp.bfloat16
@@ -87,32 +86,34 @@
     rows, width = columns.shape
     at = cuts(rows)
 
-    def body(columns_ref, out_ref, sem):
-        fetch(columns_ref, [out_ref], [0], at, sem)
-
-    return kernel_call(body, [columns], [((at[1], width), F32)], [pltpu.SemaphoreType.DMA((1,))], hbm_in=1)[0]
-
-
-def rest(columns, first):
+    def body(columns_ref, first_ref, second_ref, sem):
+        @pl.when(at_root())
+        def _():
+            fetch(columns_ref, [first_ref, second_ref], [0, 1], at, sem)
+
+    shape = [((at[c + 1] - at[c], width), F32) for c in (0, 1)]
+    return kernel_call(body, [columns], shape, [pltpu.SemaphoreType.DMA((2,))], hbm_in=1)
+
+
+def rest(columns):
     rows, width = columns.shape
     at = cuts(rows)
-    others = list(range(1, CHUNKS))
-
-    def body(columns_ref, first_ref, *refs):
-        outs, (keep_ref, send_ref, sem) = refs[: len(others)], refs[len(others) :]
-        fetch(columns_ref, outs, others, at, sem)
+
+    def body(columns_ref, *refs):
+        outs, (keep_ref, send_ref, sem) = refs[:CHUNKS], refs[CHUNKS:]
+        fetch(columns_ref, outs, range(CHUNKS), at, sem)
 
         @pl.when(at_root())
         def _():
             total = None
-            for ref in (first_ref, *outs):
+            for ref in outs:
                 pair = split(ref[...])
                 part = three(pair, pair, TN)
                 total = part if total is None else total + part
             halves(total, keep_ref, send_ref)
 
-    shape = [((at[c + 1] - at[c], width), F32) for c in others] + [((width // 2, width), F32)] * 2
-    return kernel_call(body, [columns, first], shape, [pltpu.SemaphoreType.DMA((len(others),))], hbm_in=1)
+    shape = [((at[c + 1] - at[c], width), F32) for c in range(CHUNKS)] + [((width // 2, width), F32)] * 2
+    return kernel_call(body, [columns], shape, [pltpu.SemaphoreType.DMA((CHUNKS,))], hbm_in=1)
 
 
 def eliminate(tile, size):
@@ -144,7 +145,7 @@
 def factor(mine, other):
     width = mine.shape[1]
 
-    def body(mine_ref, other_ref, gram_ref, inverse_ref, work_ref):
+    def body(mine_ref, other_ref, gram_ref, inverse_ref, half_ref, work_ref):
         @pl.when(at_root())
         def _():
             gram = joined(mine_ref[...], other_ref[...])
@@ -162,30 +163,32 @@
                 if end < width:
                     work_ref[end:, :] = work_ref[end:, :] - fine(block[:, end:width], block, TN)
             inverse_ref[...] = work_ref[:, width:]
-
-    shape = [((width, width), F32)] * 2
+            half = width // 2
+            half_ref[...] = jnp.where(is_odd(), work_ref[half:, width:], work_ref[:half, width:])
+
+    shape = [((width, width), F32)] * 2 + [((width // 2, width), F32)]
     return kernel_call(body, [mine, other], shape, [pltpu.VMEM((width, 2 * width), F32)])
 
 
-def gather(cols, group, total, chunks, moved, last):
+def gather(group, total, chunks, moved, last):
     width = chunks[0].shape[1]
     first = total is None
     flat = [] if first else [total]
-    for c, (swapped, parts) in zip(group, moved):
-        flat += [chunks[c], *swapped, *parts]
+    for c, (chosen, parts) in zip(group, moved):
+        flat += [chunks[c], *chosen.values(), *parts]
 
     def body(*refs):
         @pl.when(jnp.logical_not(at_root()))
         def _():
             ins, outs = list(refs[: len(flat)]), list(refs[len(flat) :])
             acc = None if first else ins.pop(0)[...]
-            for c, (swapped, parts) in zip(group, moved):
+            for chosen, parts in moved:
                 block = ins.pop(0)[...]
-                hub = [ins.pop(0)[...] for _ in swapped]
+                hubs = [(where, ins.pop(0)[...]) for where in chosen]
                 parts = [ins.pop(0)[...] for _ in parts]
                 got = sum(parts[1:], parts[0])
-                if hub:
-                    got = jnp.where(lax.axis_index("col") == cols // 2 + 1 - c % 2, hub[0], got)
+                for where, value in hubs:
+                    got = jnp.where(lax.axis_index("col") == where, value, got)
                 pair = split(got)
                 outs.pop(0)[...] = pair[0]
                 outs.pop(0)[...] = pair[1]
@@ -201,14 +204,30 @@
     return kernel_call(body, flat, shape)
 
 
-def finish(inverse, gram, mine, other, chunks, sent, pairs):
+def prepare(inverse, mine, other):
+    shape = inverse.shape
+
+    def body(own_ref, mine_ref, other_ref, factor_ref, square_ref):
+        @pl.when(jnp.logical_not(at_root()))
+        def _():
+            got = joined(mine_ref[...], other_ref[...])
+            factor_ref[...] = got
+            square_ref[...] = fine(got, got, TN)
+
+        @pl.when(at_root())
+        def _():
+            factor_ref[...] = own_ref[...]
+
+    return kernel_call(body, [inverse, mine, other], [(shape, F32)] * 2)
+
+
+def finish(factored, square, gram, mine, other, chunks, pairs):
     width = chunks[0].shape[1]
     rows = sum(c.shape[0] for c in chunks)
     at = cuts(rows)
 
-    def body(own_ref, gram_ref, mine_ref, other_ref, *refs):
+    def body(factor_ref, square_ref, gram_ref, mine_ref, other_ref, *refs):
         blocks, refs = refs[:CHUNKS], refs[CHUNKS:]
-        moved, refs = refs[: len(sent)], refs[len(sent) :]
         held, refs = refs[: 2 * CHUNKS], refs[2 * CHUNKS :]
         out_ref, projected_ref, buffer_ref, small_ref, sem = refs
 
@@ -223,20 +242,18 @@
 
         @pl.when(at_root())
         def _():
-            store(fine(own_ref[...], gram_ref[...]))
-            weight = split(own_ref[...].T)
+            weight = split(factor_ref[...].T)
             for c in range(CHUNKS):
                 put(c, three(split(blocks[c][...]), weight))
+            store(fine(factor_ref[...], gram_ref[...]))
 
         @pl.when(jnp.logical_not(at_root()))
         def _():
-            parts = [ref[...] for ref in moved]
-            got = sum(parts[1:], parts[0])
-            projected = fine(got, joined(mine_ref[...], other_ref[...]))
-            store(projected)
-            weight = split(fine(got, projected, TN))
+            total = joined(mine_ref[...], other_ref[...])
+            weight = split(fine(square_ref[...], total))
             for c in range(CHUNKS):
                 put(c, blocks[c][...] - three((held[2 * c][...], held[2 * c + 1][...]), weight))
+            store(fine(factor_ref[...], total))
 
         for c in range(CHUNKS):
             there = pl.ds(at[c], at[c + 1] - at[c])
@@ -245,7 +262,7 @@
 
     return kernel_call(
         body,
-        [inverse, gram, mine, other, *chunks, *sent, *pairs],
+        [factored, square, gram, mine, other, *chunks, *pairs],
         [((rows, width), F32), ((width, width), F32)],
         [
             pltpu.VMEM((rows, width), F32),
@@ -267,18 +284,24 @@
     return kernel_call(body, values, [(values[0].shape, F32)])[0]
 
 
+def swap(value, across, rows, cols, bit=0, members=()):
+    pairs = []
+    for r in range(rows):
+        for c in range(cols):
+            there = r * cols + across[c] if c in across else (r ^ (bit if c in members else 1)) * cols + c
+            pairs.append((r * cols + c, there))
+    return lax.ppermute(value, ("row", "col"), pairs)
+
+
 def exchange(mine, send, rows, cols, members, two):
-    def swap(part, bit):
-        pairs = [(r * cols + c, (r ^ (bit if c in members else 1)) * cols + c) for r in range(rows) for c in range(cols)]
-        return lax.ppermute(part, ("row", "col"), pairs)
-
-    mine = added([mine, swap(send, 1)])
+    get = lambda value, bit: swap(value, {}, rows, cols, bit, members)
+    mine = added([mine, get(send, 1)])
     bit = 2
     while bit < rows:
         bits = [bit, 2 * bit, 3 * bit] if two and 2 * bit < rows else [bit]
-        mine = added([mine] + [swap(mine, b) for b in bits])
+        mine = added([mine] + [get(mine, b) for b in bits])
         bit *= 4 if len(bits) > 1 else 2
-    return mine, swap(mine, 1)
+    return mine, get(mine, 1)
 
 
 def hop(value, pairs):
@@ -286,39 +309,43 @@
 
 
 def outward(parts, cols):
-    down, up = cols // 2 - 1, cols // 2 + 2
+    down, up = cols // 2 - 1, cols // 2 + 1
     while down > 1 or up + 1 < cols:
         pairs = ([(down, down - 1)] if down > 1 else []) + ([(up, up + 1)] if up + 1 < cols else [])
         parts.append(hop(parts[-1], pairs))
         down, up = down - 1, up + 1
 
 
-def spread(chunks, cols):
-    lower, upper = cols // 2, cols // 2 + 1
+def direct(value, cols):
+    middle = sorted(range(1, cols), key=lambda c: abs(c - cols // 2))
+    return [hop(value, [(0, c)]) for c in middle]
+
+
+def spread(chunks, rows, cols):
+    hub = cols // 2
     if cols < 4:
-        return [([], [hop(v, [(0, c)]) for c in range(1, cols)]) for v in chunks]
-    parts = [[hop(v, [(0, upper if c % 2 else lower)])] for c, v in enumerate(chunks)]
-    swaps = [[] for _ in chunks]
-    for p in range(PAIRS + 1):
-        here = [c for c in (2 * p, 2 * p + 1) if c < len(chunks)]
-        for c in here:
-            hub = upper if c % 2 else lower
-            sides = [hop(parts[c][0], [(hub, lower - 1)])]
-            if upper + 1 < cols:
-                sides.append(hop(parts[c][0], [(hub, upper + 1)]))
-                sides = [sum(sides[1:], sides[0])]
-            parts[c] += sides
-            outward(parts[c], cols)
-        held = [parts[c][0] for c in here]
-        pairs = [(lower, upper), (upper, lower)][: len(here)]
-        swapped = hop(added(held) if len(held) > 1 else held[0], pairs)
-        for c in here:
-            swaps[c].append(swapped)
-    return list(zip(swaps, parts))
+        return [({}, [hop(v, [(0, c)]) for c in range(1, cols)]) for v in chunks]
+    cycle = [(0, hub), *[(k, k + 1) for k in range(hub, cols - 1)], (cols - 1, hub - 1)]
+    cycle += [(k, k - 1) for k in range(hub - 1, 0, -1)]
+    moved = []
+    for c, value in enumerate(chunks):
+        got = hop(value, cycle if c < 2 else [(0, hub)])
+        near = cols == 4 and c == len(chunks) - 1
+        low = hop(value, [(0, hub - 1)]) if near else hop(got, [(hub, hub - 1)])
+        high = swap(got, {hub: hub + 1, hub + 1: hub}, rows, cols)
+        if cols == 4:
+            moved.append(({hub: got, hub + 1: high}, [low]))
+            continue
+        parts = [jnp.where(lax.axis_index("col") == hub + 1, high, low)]
+        outward(parts, cols)
+        moved.append(({hub: got}, parts))
+    return moved
 
 
 def spread_last(value, cols):
     hub = max(cols // 2, 1)
+    if cols <= 4:
+        return direct(value, cols)
     held = hop(value, [(0, hub)])
     parts = [held]
     ends = [(hub, hub - 1), (hub, hub + 1)]
@@ -338,18 +365,17 @@
     rows, cols = mesh.shape["row"], mesh.shape["col"]
 
     def per_device(columns):
-        first = head(columns)
-        *others, keep, send = rest(columns, first)
-        chunks = [first, *others]
-        moved = spread(chunks, cols)
-        gram, inverse = factor(*exchange(keep, send, rows, cols, (0,), False))
-        sent = spread_last(inverse, cols)
+        *chunks, keep, send = rest(columns)
+        moved = spread([*head(columns), *chunks[2:]], rows, cols)
+        gram, inverse, half = factor(*exchange(keep, send, rows, cols, (0,), False))
+        sent = added(spread_last(half, cols))
+        sent = (sent, swap(sent, {}, rows, cols))
         total, pairs = None, []
         for group in GROUPS:
-            got = gather(cols, group, total, chunks, [moved[c] for c in group], group == GROUPS[-1])
+            got = gather(group, total, chunks, [moved[c] for c in group], group == GROUPS[-1])
             pairs, total = [*pairs, *got[: 2 * len(group)]], got[2 * len(group)]
         total = exchange(*got[-2:], rows, cols, tuple(range(1, cols)), True)
-        return tuple(finish(inverse, gram, *total, chunks, sent, pairs))
+        return tuple(finish(*prepare(inverse, *sent), gram, *total, chunks, pairs))
 
     return jax.shard_map(
         per_device, mesh=mesh, in_specs=(P("row", "col"),), out_specs=(P("row", "col"), P(None, "col")), check_vma=False

time: 114 us -> 122 us (1.070)
  the two profiles are of different devices: /device:TPU:8 before, /device:TPU:0 now
where the time goes in v4:
time: 122 us; the launch traced here: 121 us
  starting transfers between devices  75.9 us (62%)
  waiting for transfers between devices  22.3 us (18%)
  Pallas kernels  21.3 us (17%)
  between operations  1.27 us (1%)
    ppermute x25, starting transfers between devices, hop(): return lax.ppermute(value, 'col', pairs)  67.7 us
    ppermute x25, waiting for transfers between devices, hop(): return lax.ppermute(value, 'col', pairs)  21.3 us
    pallas_call x16, Pallas kernels, kernel_call(): pl.pallas_call(body, out_shape=tuple(shapes), in_specs=[ANY] * hbm_in + [...  21.3 us
    ppermute x21, starting transfers between devices, swap(): return lax.ppermute(value, ('row', 'col'), pairs)  8.19 us
  transfers between devices with their start and end apart: 46, of which 11 were waited for; matrix products, arithmetic and copies ran while one was open for 0% of the time, Pallas kernels for 13%

profile of v4, /device:TPU:0, one launch (start us, length us, event | category | flops | bytes accessed | tf_op | source)
XLA Modules:
  0.0 120.8 jit_solution(11533192041636098370)
XLA Ops:
  0.6 3.1 %shard_map.30 = (f32[192,256]{1,0:T(8,128)S(1)}, f32[192,256]{1,0:T(8,128)S(1)}, f32[192,256]{1,0:T(8,128)S(1)}, f32[192,256]{1,0:T(8,128)S(1)}, f32[192,256]{1,...) custom-call(f32[2048,256]{1,0:T(8,128)} %columns_ref.3), custom_call_target="tpu_custom_call" | custom-call | tf_op jit(solution)/shard_map/pallas_call | solution.py:33
  4.3 4.1 %collective-permute-start.38 = (f32[128,256]{1,0:T(8,128)S(1)}, f32[128,256]{1,0:T(8,128)S(1)}, u32[]{:S(2)}, u32[]{:S(2)}) collective-permute-start(f32[128,256]{1,0:T(8,128)S(1)} %get-tuple-element.73.refs_1_.refs_10_), channel_id=1, source_target_pairs={{0,2},{4,6},{8,10},{12,14},{16,18},{20,22},{24,26},{28,30}} | collective-permute-start | bytes 393224 | tf_op jit(solution)/shard_map/ppermute | solution.py:308
  8.4 1.0 shard_map.37
  9.6 1.5 %collective-permute-start.14 = (f32[192,256]{1,0:T(8,128)S(1)}, f32[192,256]{1,0:T(8,128)S(1)}, u32[]{:S(2)}, u32[]{:S(2)}) collective-permute-start(f32[192,256]{1,0:T(8,128)S(1)} %get-tuple-element.61.refs_8_.refs_2_), channel_id=1, source_target_pairs={{0,2},{4,6},{8,10},{12,14},{16,18},{20,22},{24,26},{28,30}} | collective-permute-start | bytes 589832 | tf_op jit(solution)/shard_map/ppermute | solution.py:308
  11.1 1.3 %collective-permute-start.17 = (f32[192,256]{1,0:T(8,128)S(1)}, f32[192,256]{1,0:T(8,128)S(1)}, u32[]{:S(2)}, u32[]{:S(2)}) collective-permute-start(f32[192,256]{1,0:T(8,128)S(1)} %get-tuple-element.62.refs_12_.refs_3_), channel_id=1, source_target_pairs={{0,2},{4,6},{8,10},{12,14},{16,18},{20,22},{24,26},{28,30}} | collective-permute-start | bytes 589832 | tf_op jit(solution)/shard_map/ppermute | solution.py:308
  12.4 5.1 %collective-permute-start.20 = (f32[192,256]{1,0:T(8,128)S(1)}, f32[192,256]{1,0:T(8,128)S(1)}, u32[]{:S(2)}, u32[]{:S(2)}) collective-permute-start(f32[192,256]{1,0:T(8,128)S(1)} %get-tuple-element.64.refs_1_.refs_4_), channel_id=1, source_target_pairs={{0,2},{4,6},{8,10},{12,14},{16,18},{20,22},{24,26},{28,30}} | collective-permute-start | bytes 589832 | tf_op jit(solution)/shard_map/ppermute | solution.py:308
  17.6 1.6 %collective-permute-start.1 = (f32[128,256]{1,0:T(8,128)S(1)}, f32[128,256]{1,0:T(8,128)S(1)}, u32[]{:S(2)}, u32[]{:S(2)}) collective-permute-start(f32[128,256]{1,0:T(8,128)S(1)} %shard_map.31.refs_0_), channel_id=1, source_target_pairs={{0,8},{1,5},{2,6},{3,7},{4,12},{5,1},{6,2},{7,3},{8,0},{9,13},{10,... | collective-permute-start | bytes 393224 | tf_op jit(solution)/shard_map/ppermute | solution.py:293
  19.2 1.6 %collective-permute-done.11.refs_5_ = f32[192,256]{1,0:T(8,128)S(1)} collective-permute-done((f32[192,256]{1,0:T(8,128)S(1)}, f32[192,256]{1,0:T(8,128)S(1)}, u32[]{:S(2)}, u32[]{:S(2)}) %collective-permute-start.11) | collective-permute-done | bytes 196640 | tf_op jit(solution)/shard_map/ppermute | solution.py:308
  20.7 5.2 %collective-permute-start.23 = (f32[192,256]{1,0:T(8,128)S(1)}, f32[192,256]{1,0:T(8,128)S(1)}, u32[]{:S(2)}, u32[]{:S(2)}) collective-permute-start(f32[192,256]{1,0:T(8,128)S(1)} %get-tuple-element.65.refs_5_), channel_id=1, source_target_pairs={{0,2},{4,6},{8,10},{12,14},{16,18},{20,22},{24,26},{28,30}} | collective-permute-start | bytes 589832 | tf_op jit(solution)/shard_map/ppermute | solution.py:308
  26.0 4.2 %collective-permute-start.26 = (f32[192,256]{1,0:T(8,128)S(1)}, f32[192,256]{1,0:T(8,128)S(1)}, u32[]{:S(2)}, u32[]{:S(2)}) collective-permute-start(f32[192,256]{1,0:T(8,128)S(1)} %get-tuple-element.66.refs_9_.refs_6_), channel_id=1, source_target_pairs={{0,2},{4,6},{8,10},{12,14},{16,18},{20,22},{24,26},{28,30}} | collective-permute-start | bytes 589832 | tf_op jit(solution)/shard_map/ppermute | solution.py:308
  30.2 4.2 %collective-permute-start.29 = (f32[192,256]{1,0:T(8,128)S(1)}, f32[192,256]{1,0:T(8,128)S(1)}, u32[]{:S(2)}, u32[]{:S(2)}) collective-permute-start(f32[192,256]{1,0:T(8,128)S(1)} %get-tuple-element.68.refs_1_.refs_7_), channel_id=1, source_target_pairs={{0,2},{4,6},{8,10},{12,14},{16,18},{20,22},{24,26},{28,30}} | collective-permute-start | bytes 589832 | tf_op jit(solution)/shard_map/ppermute | solution.py:308
  34.4 4.2 %collective-permute-start.32 = (f32[192,256]{1,0:T(8,128)S(1)}, f32[192,256]{1,0:T(8,128)S(1)}, u32[]{:S(2)}, u32[]{:S(2)}) collective-permute-start(f32[192,256]{1,0:T(8,128)S(1)} %get-tuple-element.69.refs_5_.refs_8_), channel_id=1, source_target_pairs={{0,2},{4,6},{8,10},{12,14},{16,18},{20,22},{24,26},{28,30}} | collective-permute-start | bytes 589832 | tf_op jit(solution)/shard_map/ppermute | solution.py:308
  38.6 1.3 %collective-permute-start.35 = (f32[192,256]{1,0:T(8,128)S(1)}, f32[192,256]{1,0:T(8,128)S(1)}, u32[]{:S(2)}, u32[]{:S(2)}) collective-permute-start(f32[192,256]{1,0:T(8,128)S(1)} %get-tuple-element.71.refs_1_.refs_9_), channel_id=1, source_target_pairs={{0,2},{4,6},{8,10},{12,14},{16,18},{20,22},{24,26},{28,30}} | collective-permute-start | bytes 589832 | tf_op jit(solution)/shard_map/ppermute | solution.py:308
  40.0 1.6 %collective-permute-start.2 = (f32[128,256]{1,0:T(8,128)S(1)}, f32[128,256]{1,0:T(8,128)S(1)}, u32[]{:S(2)}, u32[]{:S(2)}) collective-permute-start(f32[128,256]{1,0:T(8,128)S(1)} %shard_map.32.refs_0_), channel_id=1, source_target_pairs={{0,16},{1,5},{2,6},{3,7},{4,20},{5,1},{6,2},{7,3},{8,24},{9,13},{1... | collective-permute-start | bytes 393224 | tf_op jit(solution)/shard_map/ppermute | solution.py:293
  42.4 3.5 %collective-permute-done.29.refs_2_ = f32[192,256]{1,0:T(8,128)S(1)} collective-permute-done((f32[192,256]{1,0:T(8,128)S(1)}, f32[192,256]{1,0:T(8,128)S(1)}, u32[]{:S(2)}, u32[]{:S(2)}) %collective-permute-start.29) | collective-permute-done | bytes 196640 | tf_op jit(solution)/shard_map/ppermute | solution.py:308
  46.0 4.2 %collective-permute-done.32.refs_6_ = f32[192,256]{1,0:T(8,128)S(1)} collective-permute-done((f32[192,256]{1,0:T(8,128)S(1)}, f32[192,256]{1,0:T(8,128)S(1)}, u32[]{:S(2)}, u32[]{:S(2)}) %collective-permute-start.32) | collective-permute-done | bytes 196640 | tf_op jit(solution)/shard_map/ppermute | solution.py:308
  50.9 3.1 %collective-permute-done.35.refs_2_ = f32[192,256]{1,0:T(8,128)S(1)} collective-permute-done((f32[192,256]{1,0:T(8,128)S(1)}, f32[192,256]{1,0:T(8,128)S(1)}, u32[]{:S(2)}, u32[]{:S(2)}) %collective-permute-start.35) | collective-permute-done | bytes 196640 | tf_op jit(solution)/shard_map/ppermute | solution.py:308
  53.9 0.7 collective-permute-start.16
  55.2 0.7 collective-permute-start.19
  56.0 0.7 collective-permute-start.22
  57.2 0.7 collective-permute-start.25
  58.0 0.7 collective-permute-start.28
  62.0 25.9 %collective-permute-start.40 = (f32[128,256]{1,0:T(8,128)S(1)}, f32[128,256]{1,0:T(8,128)S(1)}, u32[]{:S(2)}, u32[]{:S(2)}) collective-permute-start(f32[128,256]{1,0:T(8,128)S(1)} %get-tuple-element.73.refs_1_.refs_10_), channel_id=1, source_target_pairs={{0,1},{4,5},{8,9},{12,13},{16,17},{20,21},{24,25},{28,29}} | collective-permute-start | bytes 393224 | tf_op jit(solution)/shard_map/ppermute | solution.py:308
  88.6 2.7 %collective-permute-done.40.refs_4_ = f32[128,256]{1,0:T(8,128)S(1)} collective-permute-done((f32[128,256]{1,0:T(8,128)S(1)}, f32[128,256]{1,0:T(8,128)S(1)}, u32[]{:S(2)}, u32[]{:S(2)}) %collective-permute-start.40) | collective-permute-done | bytes 131104 | tf_op jit(solution)/shard_map/ppermute | solution.py:308
  91.3 14.8 %shard_map.34 = (f32[256,256]{1,0:T(8,128)S(1)}, f32[256,256]{1,0:T(8,128)S(1)}, f32[128,256]{1,0:T(8,128)S(1)}) custom-call(f32[128,256]{1,0:T(8,128)S(1)} %shard_map.33.mine_ref, f32[128,256]{1,0:T(8,128)S(1)} %collective-permute-done.3.other_ref), custom_call_target="tpu_custom_call" | custom-call | tf_op jit(solution)/shard_map/pallas_call | solution.py:33
  106.1 1.3 %collective-permute-start.6 = (f32[128,256]{1,0:T(8,128)S(1)}, f32[128,256]{1,0:T(8,128)S(1)}, u32[]{:S(2)}, u32[]{:S(2)}) collective-permute-start(f32[128,256]{1,0:T(8,128)S(1)} %get-tuple-element.53), channel_id=1, source_target_pairs={{0,3},{4,7},{8,11},{12,15},{16,19},{20,23},{24,27},{28,31}} | collective-permute-start | bytes 393224 | tf_op jit(solution)/shard_map/ppermute | solution.py:308
  107.4 1.3 %collective-permute-start.5 = (f32[128,256]{1,0:T(8,128)S(1)}, f32[128,256]{1,0:T(8,128)S(1)}, u32[]{:S(2)}, u32[]{:S(2)}) collective-permute-start(f32[128,256]{1,0:T(8,128)S(1)} %get-tuple-element.53), channel_id=1, source_target_pairs={{0,1},{4,5},{8,9},{12,13},{16,17},{20,21},{24,25},{28,29}} | collective-permute-start | bytes 393224 | tf_op jit(solution)/shard_map/ppermute | solution.py:308
  108.8 1.3 %collective-permute-start.4 = (f32[128,256]{1,0:T(8,128)S(1)}, f32[128,256]{1,0:T(8,128)S(1)}, u32[]{:S(2)}, u32[]{:S(2)}) collective-permute-start(f32[128,256]{1,0:T(8,128)S(1)} %get-tuple-element.53), channel_id=1, source_target_pairs={{0,2},{4,6},{8,10},{12,14},{16,18},{20,22},{24,26},{28,30}} | collective-permute-start | bytes 393224 | tf_op jit(solution)/shard_map/ppermute | solution.py:308
  111.3 2.8 %collective-permute-done.5.refs_1_ = f32[128,256]{1,0:T(8,128)S(1)} collective-permute-done((f32[128,256]{1,0:T(8,128)S(1)}, f32[128,256]{1,0:T(8,128)S(1)}, u32[]{:S(2)}, u32[]{:S(2)}) %collective-permute-start.5) | collective-permute-done | bytes 131104 | tf_op jit(solution)/shard_map/ppermute | solution.py:308
  114.1 2.6 %collective-permute-done.4.refs_0_ = f32[128,256]{1,0:T(8,128)S(1)} collective-permute-done((f32[128,256]{1,0:T(8,128)S(1)}, f32[128,256]{1,0:T(8,128)S(1)}, u32[]{:S(2)}, u32[]{:S(2)}) %collective-permute-start.4) | collective-permute-done | bytes 131104 | tf_op jit(solution)/shard_map/ppermute | solution.py:308
  117.5 0.7 collective-permute-done.7.other_ref
  118.4 2.2 %shard_map.45 = (f32[2048,256]{1,0:T(8,128)}, f32[256,256]{1,0:T(8,128)}) custom-call(f32[256,256]{1,0:T(8,128)S(1)} %get-tuple-element.54.factor_ref, f32[256,256]{1,0:T(8,128)S(1)} %get-tuple-element.55.square_ref, f32[256,256]{1,0:T(8,128)S(1)} %get-tuple-element.56.gram_ref, f32[128,256]{1,0:T(8,128)S(1)} %shard_map.44.mine_ref, ...), custom_call_target="tpu_custom_call" | custom-call | tf_op jit(solution)/shard_map/pallas_call | solution.py:33
  (76 shorter events, 9.7 us)
Async XLA Ops:
  3.7 7.4 %collective-permute-start = (f32[128,256]{1,0:T(8,128)S(1)}, f32[128,256]{1,0:T(8,128)S(1)}, u32[]{:S(2)}, u32[]{:S(2)}) collective-permute-start(f32[128,256]{1,0:T(8,128)S(1)} %get-tuple-element.51), channel_id=1, source_target_pairs={{0,4},{1,5},{2,6},{3,7},{4,0},{5,1},{6,2},{7,3},{8,12},{9,13},{10,... | collective-permute-start | bytes 393224 | tf_op jit(solution)/shard_map/ppermute | solution.py:293
  4.3 8.1 %collective-permute-start.38 = (f32[128,256]{1,0:T(8,128)S(1)}, f32[128,256]{1,0:T(8,128)S(1)}, u32[]{:S(2)}, u32[]{:S(2)}) collective-permute-start(f32[128,256]{1,0:T(8,128)S(1)} %get-tuple-element.73.refs_1_.refs_10_), channel_id=1, source_target_pairs={{0,2},{4,6},{8,10},{12,14},{16,18},{20,22},{24,26},{28,30}} | collective-permute-start | bytes 393224 | tf_op jit(solution)/shard_map/ppermute | solution.py:308
  9.5 8.1 %collective-permute-start.8 = (f32[192,256]{1,0:T(8,128)S(1)}, f32[192,256]{1,0:T(8,128)S(1)}, u32[]{:S(2)}, u32[]{:S(2)}) collective-permute-start(f32[192,256]{1,0:T(8,128)S(1)} %get-tuple-element.58), channel_id=1, source_target_pairs={{0,2},{2,3},{3,1},{1,0},{4,6},{6,7},{7,5},{5,4},{8,10},{10,11},{11... | collective-permute-start | bytes 589832 | tf_op jit(solution)/shard_map/ppermute | solution.py:308
  9.5 11.2 %collective-permute-start.11 = (f32[192,256]{1,0:T(8,128)S(1)}, f32[192,256]{1,0:T(8,128)S(1)}, u32[]{:S(2)}, u32[]{:S(2)}) collective-permute-start(f32[192,256]{1,0:T(8,128)S(1)} %get-tuple-element.60), channel_id=1, source_target_pairs={{0,2},{2,3},{3,1},{1,0},{4,6},{6,7},{7,5},{5,4},{8,10},{10,11},{11... | collective-permute-start | bytes 589832 | tf_op jit(solution)/shard_map/ppermute | solution.py:308
  9.6 16.4 %collective-permute-start.14 = (f32[192,256]{1,0:T(8,128)S(1)}, f32[192,256]{1,0:T(8,128)S(1)}, u32[]{:S(2)}, u32[]{:S(2)}) collective-permute-start(f32[192,256]{1,0:T(8,128)S(1)} %get-tuple-element.61.refs_8_.refs_2_), channel_id=1, source_target_pairs={{0,2},{4,6},{8,10},{12,14},{16,18},{20,22},{24,26},{28,30}} | collective-permute-start | bytes 589832 | tf_op jit(solution)/shard_map/ppermute | solution.py:308
  11.1 19.1 %collective-permute-start.17 = (f32[192,256]{1,0:T(8,128)S(1)}, f32[192,256]{1,0:T(8,128)S(1)}, u32[]{:S(2)}, u32[]{:S(2)}) collective-permute-start(f32[192,256]{1,0:T(8,128)S(1)} %get-tuple-element.62.refs_12_.refs_3_), channel_id=1, source_target_pairs={{0,2},{4,6},{8,10},{12,14},{16,18},{20,22},{24,26},{28,30}} | collective-permute-start | bytes 589832 | tf_op jit(solution)/shard_map/ppermute | solution.py:308
  12.4 22.0 %collective-permute-start.20 = (f32[192,256]{1,0:T(8,128)S(1)}, f32[192,256]{1,0:T(8,128)S(1)}, u32[]{:S(2)}, u32[]{:S(2)}) collective-permute-start(f32[192,256]{1,0:T(8,128)S(1)} %get-tuple-element.64.refs_1_.refs_4_), channel_id=1, source_target_pairs={{0,2},{4,6},{8,10},{12,14},{16,18},{20,22},{24,26},{28,30}} | collective-permute-start | bytes 589832 | tf_op jit(solution)/shard_map/ppermute | solution.py:308
  17.6 21.0 %collective-permute-start.1 = (f32[128,256]{1,0:T(8,128)S(1)}, f32[128,256]{1,0:T(8,128)S(1)}, u32[]{:S(2)}, u32[]{:S(2)}) collective-permute-start(f32[128,256]{1,0:T(8,128)S(1)} %shard_map.31.refs_0_), channel_id=1, source_target_pairs={{0,8},{1,5},{2,6},{3,7},{4,12},{5,1},{6,2},{7,3},{8,0},{9,13},{10,... | collective-permute-start | bytes 393224 | tf_op jit(solution)/shard_map/ppermute | solution.py:293
  20.7 19.2 %collective-permute-start.23 = (f32[192,256]{1,0:T(8,128)S(1)}, f32[192,256]{1,0:T(8,128)S(1)}, u32[]{:S(2)}, u32[]{:S(2)}) collective-permute-start(f32[192,256]{1,0:T(8,128)S(1)} %get-tuple-element.65.refs_5_), channel_id=1, source_target_pairs={{0,2},{4,6},{8,10},{12,14},{16,18},{20,22},{24,26},{28,30}} | collective-permute-start | bytes 589832 | tf_op jit(solution)/shard_map/ppermute | solution.py:308
  26.0 15.8 %collective-permute-start.26 = (f32[192,256]{1,0:T(8,128)S(1)}, f32[192,256]{1,0:T(8,128)S(1)}, u32[]{:S(2)}, u32[]{:S(2)}) collective-permute-start(f32[192,256]{1,0:T(8,128)S(1)} %get-tuple-element.66.refs_9_.refs_6_), channel_id=1, source_target_pairs={{0,2},{4,6},{8,10},{12,14},{16,18},{20,22},{24,26},{28,30}} | collective-permute-start | bytes 589832 | tf_op jit(solution)/shard_map/ppermute | solution.py:308
  30.2 15.8 %collective-permute-start.29 = (f32[192,256]{1,0:T(8,128)S(1)}, f32[192,256]{1,0:T(8,128)S(1)}, u32[]{:S(2)}, u32[]{:S(2)}) collective-permute-start(f32[192,256]{1,0:T(8,128)S(1)} %get-tuple-element.68.refs_1_.refs_7_), channel_id=1, source_target_pairs={{0,2},{4,6},{8,10},{12,14},{16,18},{20,22},{24,26},{28,30}} | collective-permute-start | bytes 589832 | tf_op jit(solution)/shard_map/ppermute | solution.py:308
  34.4 15.8 %collective-permute-start.32 = (f32[192,256]{1,0:T(8,128)S(1)}, f32[192,256]{1,0:T(8,128)S(1)}, u32[]{:S(2)}, u32[]{:S(2)}) collective-permute-start(f32[192,256]{1,0:T(8,128)S(1)} %get-tuple-element.69.refs_5_.refs_8_), channel_id=1, source_target_pairs={{0,2},{4,6},{8,10},{12,14},{16,18},{20,22},{24,26},{28,30}} | collective-permute-start | bytes 589832 | tf_op jit(solution)/shard_map/ppermute | solution.py:308
  38.6 15.3 %collective-permute-start.35 = (f32[192,256]{1,0:T(8,128)S(1)}, f32[192,256]{1,0:T(8,128)S(1)}, u32[]{:S(2)}, u32[]{:S(2)}) collective-permute-start(f32[192,256]{1,0:T(8,128)S(1)} %get-tuple-element.71.refs_1_.refs_9_), channel_id=1, source_target_pairs={{0,2},{4,6},{8,10},{12,14},{16,18},{20,22},{24,26},{28,30}} | collective-permute-start | bytes 589832 | tf_op jit(solution)/shard_map/ppermute | solution.py:308
  40.0 13.9 %collective-permute-start.2 = (f32[128,256]{1,0:T(8,128)S(1)}, f32[128,256]{1,0:T(8,128)S(1)}, u32[]{:S(2)}, u32[]{:S(2)}) collective-permute-start(f32[128,256]{1,0:T(8,128)S(1)} %shard_map.32.refs_0_), channel_id=1, source_target_pairs={{0,16},{1,5},{2,6},{3,7},{4,20},{5,1},{6,2},{7,3},{8,24},{9,13},{1... | collective-permute-start | bytes 393224 | tf_op jit(solution)/shard_map/ppermute | solution.py:293
  41.8 12.8 %collective-permute-start.10 = (f32[192,256]{1,0:T(8,128)S(1)}, f32[192,256]{1,0:T(8,128)S(1)}, u32[]{:S(2)}, u32[]{:S(2)}) collective-permute-start(f32[192,256]{1,0:T(8,128)S(1)} %collective-permute-done.8.refs_1_), channel_id=1, source_target_pairs={{2,1},{6,5},{10,9},{14,13},{18,17},{22,21},{26,25},{30,29}} | collective-permute-start | bytes 589832 | tf_op jit(solution)/shard_map/ppermute | solution.py:308
  46.0 9.2 %collective-permute-start.9 = (f32[192,256]{1,0:T(8,128)S(1)}, f32[192,256]{1,0:T(8,128)S(1)}, u32[]{:S(2)}, u32[]{:S(2)}) collective-permute-start(f32[192,256]{1,0:T(8,128)S(1)} %collective-permute-done.8.refs_1_), channel_id=1, source_target_pairs={{0,4},{1,5},{2,3},{3,2},{4,0},{5,1},{6,7},{7,6},{8,12},{9,13},{10,... | collective-permute-start | bytes 589832 | tf_op jit(solution)/shard_map/ppermute | solution.py:293
  50.2 5.7 %collective-permute-start.13 = (f32[192,256]{1,0:T(8,128)S(1)}, f32[192,256]{1,0:T(8,128)S(1)}, u32[]{:S(2)}, u32[]{:S(2)}) collective-permute-start(f32[192,256]{1,0:T(8,128)S(1)} %collective-permute-done.11.refs_5_), channel_id=1, source_target_pairs={{2,1},{6,5},{10,9},{14,13},{18,17},{22,21},{26,25},{30,29}} | collective-permute-start | bytes 589832 | tf_op jit(solution)/shard_map/ppermute | solution.py:308
  53.9 2.7 %collective-permute-start.16 = (f32[192,256]{1,0:T(8,128)S(1)}, f32[192,256]{1,0:T(8,128)S(1)}, u32[]{:S(2)}, u32[]{:S(2)}) collective-permute-start(f32[192,256]{1,0:T(8,128)S(1)} %collective-permute-done.14.refs_9_), channel_id=1, source_target_pairs={{2,1},{6,5},{10,9},{14,13},{18,17},{22,21},{26,25},{30,29}} | collective-permute-start | bytes 589832 | tf_op jit(solution)/shard_map/ppermute | solution.py:308
  60.0 27.9 %collective-permute-start.34 = (f32[192,256]{1,0:T(8,128)S(1)}, f32[192,256]{1,0:T(8,128)S(1)}, u32[]{:S(2)}, u32[]{:S(2)}) collective-permute-start(f32[192,256]{1,0:T(8,128)S(1)} %collective-permute-done.32.refs_6_), channel_id=1, source_target_pairs={{2,1},{6,5},{10,9},{14,13},{18,17},{22,21},{26,25},{30,29}} | collective-permute-start | bytes 589832 | tf_op jit(solution)/shard_map/ppermute | solution.py:308
  60.7 27.5 %collective-permute-start.33 = (f32[192,256]{1,0:T(8,128)S(1)}, f32[192,256]{1,0:T(8,128)S(1)}, u32[]{:S(2)}, u32[]{:S(2)}) collective-permute-start(f32[192,256]{1,0:T(8,128)S(1)} %collective-permute-done.32.refs_6_), channel_id=1, source_target_pairs={{0,4},{1,5},{2,3},{3,2},{4,0},{5,1},{6,7},{7,6},{8,12},{9,13},{10,... | collective-permute-start | bytes 589832 | tf_op jit(solution)/shard_map/ppermute | solution.py:293
  61.2 27.3 %collective-permute-start.37 = (f32[192,256]{1,0:T(8,128)S(1)}, f32[192,256]{1,0:T(8,128)S(1)}, u32[]{:S(2)}, u32[]{:S(2)}) collective-permute-start(f32[192,256]{1,0:T(8,128)S(1)} %collective-permute-done.35.refs_2_), channel_id=1, source_target_pairs={{2,1},{6,5},{10,9},{14,13},{18,17},{22,21},{26,25},{30,29}} | collective-permute-start | bytes 589832 | tf_op jit(solution)/shard_map/ppermute | solution.py:308
  61.9 26.7 %collective-permute-start.36 = (f32[192,256]{1,0:T(8,128)S(1)}, f32[192,256]{1,0:T(8,128)S(1)}, u32[]{:S(2)}, u32[]{:S(2)}) collective-permute-start(f32[192,256]{1,0:T(8,128)S(1)} %collective-permute-done.35.refs_2_), channel_id=1, source_target_pairs={{0,4},{1,5},{2,3},{3,2},{4,0},{5,1},{6,7},{7,6},{8,12},{9,13},{10,... | collective-permute-start | bytes 589832 | tf_op jit(solution)/shard_map/ppermute | solution.py:293
  62.0 29.3 %collective-permute-start.40 = (f32[128,256]{1,0:T(8,128)S(1)}, f32[128,256]{1,0:T(8,128)S(1)}, u32[]{:S(2)}, u32[]{:S(2)}) collective-permute-start(f32[128,256]{1,0:T(8,128)S(1)} %get-tuple-element.73.refs_1_.refs_10_), channel_id=1, source_target_pairs={{0,1},{4,5},{8,9},{12,13},{16,17},{20,21},{24,25},{28,29}} | collective-permute-start | bytes 393224 | tf_op jit(solution)/shard_map/ppermute | solution.py:308
  87.9 3.4 %collective-permute-start.39 = (f32[128,256]{1,0:T(8,128)S(1)}, f32[128,256]{1,0:T(8,128)S(1)}, u32[]{:S(2)}, u32[]{:S(2)}) collective-permute-start(f32[128,256]{1,0:T(8,128)S(1)} %collective-permute-done.38.refs_2_), channel_id=1, source_target_pairs={{0,4},{1,5},{2,3},{3,2},{4,0},{5,1},{6,7},{7,6},{8,12},{9,13},{10,... | collective-permute-start | bytes 393224 | tf_op jit(solution)/shard_map/ppermute | solution.py:293
  88.2 3.1 %collective-permute-start.3 = (f32[128,256]{1,0:T(8,128)S(1)}, f32[128,256]{1,0:T(8,128)S(1)}, u32[]{:S(2)}, u32[]{:S(2)}) collective-permute-start(f32[128,256]{1,0:T(8,128)S(1)} %shard_map.33.mine_ref), channel_id=1, source_target_pairs={{0,4},{1,5},{2,6},{3,7},{4,0},{5,1},{6,2},{7,3},{8,12},{9,13},{10,... | collective-permute-start | bytes 393224 | tf_op jit(solution)/shard_map/ppermute | solution.py:293
  91.3 18.8 %collective-permute-start.41 = (f32[128,256]{1,0:T(8,128)S(1)}, f32[128,256]{1,0:T(8,128)S(1)}, u32[]{:S(2)}, u32[]{:S(2)}) collective-permute-start(f32[128,256]{1,0:T(8,128)S(1)} %get-tuple-element.75), channel_id=1, source_target_pairs={{0,4},{1,5},{2,6},{3,7},{4,0},{5,1},{6,2},{7,3},{8,12},{9,13},{10,... | collective-permute-start | bytes 393224 | tf_op jit(solution)/shard_map/ppermute | solution.py:293
  106.1 5.2 %collective-permute-start.6 = (f32[128,256]{1,0:T(8,128)S(1)}, f32[128,256]{1,0:T(8,128)S(1)}, u32[]{:S(2)}, u32[]{:S(2)}) collective-permute-start(f32[128,256]{1,0:T(8,128)S(1)} %get-tuple-element.53), channel_id=1, source_target_pairs={{0,3},{4,7},{8,11},{12,15},{16,19},{20,23},{24,27},{28,31}} | collective-permute-start | bytes 393224 | tf_op jit(solution)/shard_map/ppermute | solution.py:308
  107.4 6.7 %collective-permute-start.5 = (f32[128,256]{1,0:T(8,128)S(1)}, f32[128,256]{1,0:T(8,128)S(1)}, u32[]{:S(2)}, u32[]{:S(2)}) collective-permute-start(f32[128,256]{1,0:T(8,128)S(1)} %get-tuple-element.53), channel_id=1, source_target_pairs={{0,1},{4,5},{8,9},{12,13},{16,17},{20,21},{24,25},{28,29}} | collective-permute-start | bytes 393224 | tf_op jit(solution)/shard_map/ppermute | solution.py:308
  108.8 8.0 %collective-permute-start.4 = (f32[128,256]{1,0:T(8,128)S(1)}, f32[128,256]{1,0:T(8,128)S(1)}, u32[]{:S(2)}, u32[]{:S(2)}) collective-permute-start(f32[128,256]{1,0:T(8,128)S(1)} %get-tuple-element.53), channel_id=1, source_target_pairs={{0,2},{4,6},{8,10},{12,14},{16,18},{20,22},{24,26},{28,30}} | collective-permute-start | bytes 393224 | tf_op jit(solution)/shard_map/ppermute | solution.py:308
  110.1 6.8 %collective-permute-start.44 = (f32[128,256]{1,0:T(8,128)S(1)}, f32[128,256]{1,0:T(8,128)S(1)}, u32[]{:S(2)}, u32[]{:S(2)}) collective-permute-start(f32[128,256]{1,0:T(8,128)S(1)} %shard_map.43.refs_0_), channel_id=1, source_target_pairs={{0,4},{1,25},{2,26},{3,27},{4,0},{5,29},{6,30},{7,31},{8,12},{9,17... | collective-permute-start | bytes 393224 | tf_op jit(solution)/shard_map/ppermute | solution.py:293
  110.7 6.2 %collective-permute-start.43 = (f32[128,256]{1,0:T(8,128)S(1)}, f32[128,256]{1,0:T(8,128)S(1)}, u32[]{:S(2)}, u32[]{:S(2)}) collective-permute-start(f32[128,256]{1,0:T(8,128)S(1)} %shard_map.43.refs_0_), channel_id=1, source_target_pairs={{0,4},{1,17},{2,18},{3,19},{4,0},{5,21},{6,22},{7,23},{8,12},{9,25... | collective-permute-start | bytes 393224 | tf_op jit(solution)/shard_map/ppermute | solution.py:293
  111.3 5.6 %collective-permute-start.42 = (f32[128,256]{1,0:T(8,128)S(1)}, f32[128,256]{1,0:T(8,128)S(1)}, u32[]{:S(2)}, u32[]{:S(2)}) collective-permute-start(f32[128,256]{1,0:T(8,128)S(1)} %shard_map.43.refs_0_), channel_id=1, source_target_pairs={{0,4},{1,9},{2,10},{3,11},{4,0},{5,13},{6,14},{7,15},{8,12},{9,1},... | collective-permute-start | bytes 393224 | tf_op jit(solution)/shard_map/ppermute | solution.py:293
  (14 other events, 32.4 us)

commit v5 on v4

--- a/solution.py
+++ b/solution.py
@@ -6,7 +6,8 @@
 from jax.sharding import PartitionSpec as P
 
 
-CHUNKS = 11
+WEIGHTS = (12,) * 10 + (8,)
+CHUNKS = len(WEIGHTS)
 GROUPS = ((0, 1, 2, 3), (4, 5, 6), (7, 8), (9,), (10,))
 TILE = 64
 F32 = jnp.float32
@@ -67,8 +68,8 @@
 
 
 def cuts(rows):
-    step = -(-rows // (16 * CHUNKS)) * 16
-    return [min(c * step, rows) for c in range(CHUNKS + 1)]
+    whole = sum(WEIGHTS)
+    return [sum(WEIGHTS[:c]) * rows // whole // 16 * 16 for c in range(CHUNKS)] + [rows]
 
 
 def fetch(columns_ref, refs, which, at, sem):
@@ -325,11 +326,10 @@
     hub = cols // 2
     if cols < 4:
         return [({}, [hop(v, [(0, c)]) for c in range(1, cols)]) for v in chunks]
-    cycle = [(0, hub), *[(k, k + 1) for k in range(hub, cols - 1)], (cols - 1, hub - 1)]
-    cycle += [(k, k - 1) for k in range(hub - 1, 0, -1)]
+    cycle = {0: hub, **{k: k - 1 for k in range(1, hub + 1)}}
     moved = []
     for c, value in enumerate(chunks):
-        got = hop(value, cycle if c < 2 else [(0, hub)])
+        got = swap(value, cycle, rows, cols) if c < 2 else hop(value, [(0, hub)])
         near = cols == 4 and c == len(chunks) - 1
         low = hop(value, [(0, hub - 1)]) if near else hop(got, [(hub, hub - 1)])
         high = swap(got, {hub: hub + 1, hub + 1: hub}, rows, cols)

time: 122 us -> 122 us (level)
    ppermute x21 -> x23, waiting for transfers between devices: 1.01 us -> 2.6 us  [swap(): return lax.ppermute(value, ('row', 'col'), pairs)]
    ppermute x25 -> x23, waiting for transfers between devices: 21.3 us -> 19.7 us  [hop(): return lax.ppermute(value, 'col', pairs)]
    ppermute x25 -> x23, starting transfers between devices: 67.7 us -> 67.6 us  [hop(): return lax.ppermute(value, 'col', pairs)]
    ppermute x21 -> x23, starting transfers between devices: 8.19 us -> 8.31 us  [swap(): return lax.ppermute(value, ('row', 'col'), pairs)]
where the time goes in v5:
time: 122 us; the launch traced here: 121 us
  starting transfers between devices  75.9 us (62%)
  waiting for transfers between devices  22.3 us (18%)
  Pallas kernels  21.3 us (17%)
  between operations  1.27 us (1%)
    ppermute x23, starting transfers between devices, hop(): return lax.ppermute(value, 'col', pairs)  67.6 us
    pallas_call x16, Pallas kernels, kernel_call(): pl.pallas_call(body, out_shape=tuple(shapes), in_specs=[ANY] * hbm_in + [...  21.3 us
    ppermute x23, waiting for transfers between devices, hop(): return lax.ppermute(value, 'col', pairs)  19.7 us
    ppermute x23, starting transfers between devices, swap(): return lax.ppermute(value, ('row', 'col'), pairs)  8.31 us
    ppermute x23, waiting for transfers between devices, swap(): return lax.ppermute(value, ('row', 'col'), pairs)  2.6 us
  transfers between devices with their start and end apart: 46, of which 11 were waited for; matrix products, arithmetic and copies ran while one was open for 0% of the time, Pallas kernels for 13%

profile of v5, /device:TPU:0, one launch (start us, length us, event | category | flops | bytes accessed | tf_op | source)
XLA Modules:
  0.0 120.8 jit_solution(5464553543284824506)
XLA Ops:
  0.6 3.1 %shard_map.30 = (f32[192,256]{1,0:T(8,128)S(1)}, f32[192,256]{1,0:T(8,128)S(1)}, f32[192,256]{1,0:T(8,128)S(1)}, f32[192,256]{1,0:T(8,128)S(1)}, f32[192,256]{1,...) custom-call(f32[2048,256]{1,0:T(8,128)} %columns_ref.3), custom_call_target="tpu_custom_call" | custom-call | tf_op jit(solution)/shard_map/pallas_call | solution.py:34
  4.3 4.1 %collective-permute-start.38 = (f32[128,256]{1,0:T(8,128)S(1)}, f32[128,256]{1,0:T(8,128)S(1)}, u32[]{:S(2)}, u32[]{:S(2)}) collective-permute-start(f32[128,256]{1,0:T(8,128)S(1)} %get-tuple-element.73.refs_1_.refs_10_), channel_id=1, source_target_pairs={{0,2},{4,6},{8,10},{12,14},{16,18},{20,22},{24,26},{28,30}} | collective-permute-start | bytes 393224 | tf_op jit(solution)/shard_map/ppermute | solution.py:309
  8.4 1.0 shard_map.37
  9.6 5.3 %collective-permute-start.14 = (f32[192,256]{1,0:T(8,128)S(1)}, f32[192,256]{1,0:T(8,128)S(1)}, u32[]{:S(2)}, u32[]{:S(2)}) collective-permute-start(f32[192,256]{1,0:T(8,128)S(1)} %get-tuple-element.61.refs_8_.refs_2_), channel_id=1, source_target_pairs={{0,2},{4,6},{8,10},{12,14},{16,18},{20,22},{24,26},{28,30}} | collective-permute-start | bytes 589832 | tf_op jit(solution)/shard_map/ppermute | solution.py:309
  14.9 1.3 %collective-permute-start.17 = (f32[192,256]{1,0:T(8,128)S(1)}, f32[192,256]{1,0:T(8,128)S(1)}, u32[]{:S(2)}, u32[]{:S(2)}) collective-permute-start(f32[192,256]{1,0:T(8,128)S(1)} %get-tuple-element.62.refs_12_.refs_3_), channel_id=1, source_target_pairs={{0,2},{4,6},{8,10},{12,14},{16,18},{20,22},{24,26},{28,30}} | collective-permute-start | bytes 589832 | tf_op jit(solution)/shard_map/ppermute | solution.py:309
  16.3 1.3 %collective-permute-start.20 = (f32[192,256]{1,0:T(8,128)S(1)}, f32[192,256]{1,0:T(8,128)S(1)}, u32[]{:S(2)}, u32[]{:S(2)}) collective-permute-start(f32[192,256]{1,0:T(8,128)S(1)} %get-tuple-element.64.refs_1_.refs_4_), channel_id=1, source_target_pairs={{0,2},{4,6},{8,10},{12,14},{16,18},{20,22},{24,26},{28,30}} | collective-permute-start | bytes 589832 | tf_op jit(solution)/shard_map/ppermute | solution.py:309
  17.6 1.6 %collective-permute-start.1 = (f32[128,256]{1,0:T(8,128)S(1)}, f32[128,256]{1,0:T(8,128)S(1)}, u32[]{:S(2)}, u32[]{:S(2)}) collective-permute-start(f32[128,256]{1,0:T(8,128)S(1)} %shard_map.31.refs_0_), channel_id=1, source_target_pairs={{0,8},{1,5},{2,6},{3,7},{4,12},{5,1},{6,2},{7,3},{8,0},{9,13},{10,... | collective-permute-start | bytes 393224 | tf_op jit(solution)/shard_map/ppermute | solution.py:294
  19.2 1.6 %collective-permute-done.11.refs_5_ = f32[192,256]{1,0:T(8,128)S(1)} collective-permute-done((f32[192,256]{1,0:T(8,128)S(1)}, f32[192,256]{1,0:T(8,128)S(1)}, u32[]{:S(2)}, u32[]{:S(2)}) %collective-permute-start.11) | collective-permute-done | bytes 196640 | tf_op jit(solution)/shard_map/ppermute | solution.py:294
  20.7 5.2 %collective-permute-start.23 = (f32[192,256]{1,0:T(8,128)S(1)}, f32[192,256]{1,0:T(8,128)S(1)}, u32[]{:S(2)}, u32[]{:S(2)}) collective-permute-start(f32[192,256]{1,0:T(8,128)S(1)} %get-tuple-element.65.refs_5_), channel_id=1, source_target_pairs={{0,2},{4,6},{8,10},{12,14},{16,18},{20,22},{24,26},{28,30}} | collective-permute-start | bytes 589832 | tf_op jit(solution)/shard_map/ppermute | solution.py:309
  26.0 4.2 %collective-permute-start.26 = (f32[192,256]{1,0:T(8,128)S(1)}, f32[192,256]{1,0:T(8,128)S(1)}, u32[]{:S(2)}, u32[]{:S(2)}) collective-permute-start(f32[192,256]{1,0:T(8,128)S(1)} %get-tuple-element.66.refs_9_.refs_6_), channel_id=1, source_target_pairs={{0,2},{4,6},{8,10},{12,14},{16,18},{20,22},{24,26},{28,30}} | collective-permute-start | bytes 589832 | tf_op jit(solution)/shard_map/ppermute | solution.py:309
  30.2 4.2 %collective-permute-start.29 = (f32[192,256]{1,0:T(8,128)S(1)}, f32[192,256]{1,0:T(8,128)S(1)}, u32[]{:S(2)}, u32[]{:S(2)}) collective-permute-start(f32[192,256]{1,0:T(8,128)S(1)} %get-tuple-element.68.refs_1_.refs_7_), channel_id=1, source_target_pairs={{0,2},{4,6},{8,10},{12,14},{16,18},{20,22},{24,26},{28,30}} | collective-permute-start | bytes 589832 | tf_op jit(solution)/shard_map/ppermute | solution.py:309
  34.4 4.2 %collective-permute-start.32 = (f32[192,256]{1,0:T(8,128)S(1)}, f32[192,256]{1,0:T(8,128)S(1)}, u32[]{:S(2)}, u32[]{:S(2)}) collective-permute-start(f32[192,256]{1,0:T(8,128)S(1)} %get-tuple-element.69.refs_5_.refs_8_), channel_id=1, source_target_pairs={{0,2},{4,6},{8,10},{12,14},{16,18},{20,22},{24,26},{28,30}} | collective-permute-start | bytes 589832 | tf_op jit(solution)/shard_map/ppermute | solution.py:309
  38.6 1.3 %collective-permute-start.35 = (f32[192,256]{1,0:T(8,128)S(1)}, f32[192,256]{1,0:T(8,128)S(1)}, u32[]{:S(2)}, u32[]{:S(2)}) collective-permute-start(f32[192,256]{1,0:T(8,128)S(1)} %get-tuple-element.71.refs_1_.refs_9_), channel_id=1, source_target_pairs={{0,2},{4,6},{8,10},{12,14},{16,18},{20,22},{24,26},{28,30}} | collective-permute-start | bytes 589832 | tf_op jit(solution)/shard_map/ppermute | solution.py:309
  40.0 1.6 %collective-permute-start.2 = (f32[128,256]{1,0:T(8,128)S(1)}, f32[128,256]{1,0:T(8,128)S(1)}, u32[]{:S(2)}, u32[]{:S(2)}) collective-permute-start(f32[128,256]{1,0:T(8,128)S(1)} %shard_map.32.refs_0_), channel_id=1, source_target_pairs={{0,16},{1,5},{2,6},{3,7},{4,20},{5,1},{6,2},{7,3},{8,24},{9,13},{1... | collective-permute-start | bytes 393224 | tf_op jit(solution)/shard_map/ppermute | solution.py:294
  42.4 3.5 %collective-permute-done.29.refs_2_ = f32[192,256]{1,0:T(8,128)S(1)} collective-permute-done((f32[192,256]{1,0:T(8,128)S(1)}, f32[192,256]{1,0:T(8,128)S(1)}, u32[]{:S(2)}, u32[]{:S(2)}) %collective-permute-start.29) | collective-permute-done | bytes 196640 | tf_op jit(solution)/shard_map/ppermute | solution.py:309
  46.0 4.2 %collective-permute-done.32.refs_6_ = f32[192,256]{1,0:T(8,128)S(1)} collective-permute-done((f32[192,256]{1,0:T(8,128)S(1)}, f32[192,256]{1,0:T(8,128)S(1)}, u32[]{:S(2)}, u32[]{:S(2)}) %collective-permute-start.32) | collective-permute-done | bytes 196640 | tf_op jit(solution)/shard_map/ppermute | solution.py:309
  50.9 3.1 %collective-permute-done.35.refs_2_ = f32[192,256]{1,0:T(8,128)S(1)} collective-permute-done((f32[192,256]{1,0:T(8,128)S(1)}, f32[192,256]{1,0:T(8,128)S(1)}, u32[]{:S(2)}, u32[]{:S(2)}) %collective-permute-start.35) | collective-permute-done | bytes 196640 | tf_op jit(solution)/shard_map/ppermute | solution.py:309
  53.9 0.7 collective-permute-start.16
  55.2 0.7 collective-permute-start.19
  56.0 0.7 collective-permute-start.22
  57.2 0.7 collective-permute-start.25
  58.0 0.7 collective-permute-start.28
  62.0 25.9 %collective-permute-start.40 = (f32[128,256]{1,0:T(8,128)S(1)}, f32[128,256]{1,0:T(8,128)S(1)}, u32[]{:S(2)}, u32[]{:S(2)}) collective-permute-start(f32[128,256]{1,0:T(8,128)S(1)} %get-tuple-element.73.refs_1_.refs_10_), channel_id=1, source_target_pairs={{0,1},{4,5},{8,9},{12,13},{16,17},{20,21},{24,25},{28,29}} | collective-permute-start | bytes 393224 | tf_op jit(solution)/shard_map/ppermute | solution.py:309
  88.6 2.7 %collective-permute-done.40.refs_4_ = f32[128,256]{1,0:T(8,128)S(1)} collective-permute-done((f32[128,256]{1,0:T(8,128)S(1)}, f32[128,256]{1,0:T(8,128)S(1)}, u32[]{:S(2)}, u32[]{:S(2)}) %collective-permute-start.40) | collective-permute-done | bytes 131104 | tf_op jit(solution)/shard_map/ppermute | solution.py:309
  91.3 14.8 %shard_map.34 = (f32[256,256]{1,0:T(8,128)S(1)}, f32[256,256]{1,0:T(8,128)S(1)}, f32[128,256]{1,0:T(8,128)S(1)}) custom-call(f32[128,256]{1,0:T(8,128)S(1)} %shard_map.33.mine_ref, f32[128,256]{1,0:T(8,128)S(1)} %collective-permute-done.3.other_ref), custom_call_target="tpu_custom_call" | custom-call | tf_op jit(solution)/shard_map/pallas_call | solution.py:34
  106.1 1.3 %collective-permute-start.6 = (f32[128,256]{1,0:T(8,128)S(1)}, f32[128,256]{1,0:T(8,128)S(1)}, u32[]{:S(2)}, u32[]{:S(2)}) collective-permute-start(f32[128,256]{1,0:T(8,128)S(1)} %get-tuple-element.53), channel_id=1, source_target_pairs={{0,3},{4,7},{8,11},{12,15},{16,19},{20,23},{24,27},{28,31}} | collective-permute-start | bytes 393224 | tf_op jit(solution)/shard_map/ppermute | solution.py:309
  107.4 1.3 %collective-permute-start.5 = (f32[128,256]{1,0:T(8,128)S(1)}, f32[128,256]{1,0:T(8,128)S(1)}, u32[]{:S(2)}, u32[]{:S(2)}) collective-permute-start(f32[128,256]{1,0:T(8,128)S(1)} %get-tuple-element.53), channel_id=1, source_target_pairs={{0,1},{4,5},{8,9},{12,13},{16,17},{20,21},{24,25},{28,29}} | collective-permute-start | bytes 393224 | tf_op jit(solution)/shard_map/ppermute | solution.py:309
  108.8 1.3 %collective-permute-start.4 = (f32[128,256]{1,0:T(8,128)S(1)}, f32[128,256]{1,0:T(8,128)S(1)}, u32[]{:S(2)}, u32[]{:S(2)}) collective-permute-start(f32[128,256]{1,0:T(8,128)S(1)} %get-tuple-element.53), channel_id=1, source_target_pairs={{0,2},{4,6},{8,10},{12,14},{16,18},{20,22},{24,26},{28,30}} | collective-permute-start | bytes 393224 | tf_op jit(solution)/shard_map/ppermute | solution.py:309
  111.3 2.8 %collective-permute-done.5.refs_1_ = f32[128,256]{1,0:T(8,128)S(1)} collective-permute-done((f32[128,256]{1,0:T(8,128)S(1)}, f32[128,256]{1,0:T(8,128)S(1)}, u32[]{:S(2)}, u32[]{:S(2)}) %collective-permute-start.5) | collective-permute-done | bytes 131104 | tf_op jit(solution)/shard_map/ppermute | solution.py:309
  114.1 2.6 %collective-permute-done.4.refs_0_ = f32[128,256]{1,0:T(8,128)S(1)} collective-permute-done((f32[128,256]{1,0:T(8,128)S(1)}, f32[128,256]{1,0:T(8,128)S(1)}, u32[]{:S(2)}, u32[]{:S(2)}) %collective-permute-start.4) | collective-permute-done | bytes 131104 | tf_op jit(solution)/shard_map/ppermute | solution.py:309
  117.5 0.7 collective-permute-done.7.other_ref
  118.4 2.2 %shard_map.45 = (f32[2048,256]{1,0:T(8,128)}, f32[256,256]{1,0:T(8,128)}) custom-call(f32[256,256]{1,0:T(8,128)S(1)} %get-tuple-element.54.factor_ref, f32[256,256]{1,0:T(8,128)S(1)} %get-tuple-element.55.square_ref, f32[256,256]{1,0:T(8,128)S(1)} %get-tuple-element.56.gram_ref, f32[128,256]{1,0:T(8,128)S(1)} %shard_map.44.mine_ref, ...), custom_call_target="tpu_custom_call" | custom-call | tf_op jit(solution)/shard_map/pallas_call | solution.py:34
  (76 shorter events, 9.7 us)
Async XLA Ops:
  3.7 11.2 %collective-permute-start = (f32[128,256]{1,0:T(8,128)S(1)}, f32[128,256]{1,0:T(8,128)S(1)}, u32[]{:S(2)}, u32[]{:S(2)}) collective-permute-start(f32[128,256]{1,0:T(8,128)S(1)} %get-tuple-element.51), channel_id=1, source_target_pairs={{0,4},{1,5},{2,6},{3,7},{4,0},{5,1},{6,2},{7,3},{8,12},{9,13},{10,... | collective-permute-start | bytes 393224 | tf_op jit(solution)/shard_map/ppermute | solution.py:294
  4.3 12.0 %collective-permute-start.38 = (f32[128,256]{1,0:T(8,128)S(1)}, f32[128,256]{1,0:T(8,128)S(1)}, u32[]{:S(2)}, u32[]{:S(2)}) collective-permute-start(f32[128,256]{1,0:T(8,128)S(1)} %get-tuple-element.73.refs_1_.refs_10_), channel_id=1, source_target_pairs={{0,2},{4,6},{8,10},{12,14},{16,18},{20,22},{24,26},{28,30}} | collective-permute-start | bytes 393224 | tf_op jit(solution)/shard_map/ppermute | solution.py:309
  9.5 8.1 %collective-permute-start.8 = (f32[192,256]{1,0:T(8,128)S(1)}, f32[192,256]{1,0:T(8,128)S(1)}, u32[]{:S(2)}, u32[]{:S(2)}) collective-permute-start(f32[192,256]{1,0:T(8,128)S(1)} %get-tuple-element.58), channel_id=1, source_target_pairs={{0,2},{1,0},{2,1},{3,7},{4,6},{5,4},{6,5},{7,3},{8,10},{9,8},{10,9... | collective-permute-start | bytes 589832 | tf_op jit(solution)/shard_map/ppermute | solution.py:294
  9.5 11.2 %collective-permute-start.11 = (f32[192,256]{1,0:T(8,128)S(1)}, f32[192,256]{1,0:T(8,128)S(1)}, u32[]{:S(2)}, u32[]{:S(2)}) collective-permute-start(f32[192,256]{1,0:T(8,128)S(1)} %get-tuple-element.60), channel_id=1, source_target_pairs={{0,2},{1,0},{2,1},{3,7},{4,6},{5,4},{6,5},{7,3},{8,10},{9,8},{10,9... | collective-permute-start | bytes 589832 | tf_op jit(solution)/shard_map/ppermute | solution.py:294
  9.6 16.4 %collective-permute-start.14 = (f32[192,256]{1,0:T(8,128)S(1)}, f32[192,256]{1,0:T(8,128)S(1)}, u32[]{:S(2)}, u32[]{:S(2)}) collective-permute-start(f32[192,256]{1,0:T(8,128)S(1)} %get-tuple-element.61.refs_8_.refs_2_), channel_id=1, source_target_pairs={{0,2},{4,6},{8,10},{12,14},{16,18},{20,22},{24,26},{28,30}} | collective-permute-start | bytes 589832 | tf_op jit(solution)/shard_map/ppermute | solution.py:309
  14.9 15.3 %collective-permute-start.17 = (f32[192,256]{1,0:T(8,128)S(1)}, f32[192,256]{1,0:T(8,128)S(1)}, u32[]{:S(2)}, u32[]{:S(2)}) collective-permute-start(f32[192,256]{1,0:T(8,128)S(1)} %get-tuple-element.62.refs_12_.refs_3_), channel_id=1, source_target_pairs={{0,2},{4,6},{8,10},{12,14},{16,18},{20,22},{24,26},{28,30}} | collective-permute-start | bytes 589832 | tf_op jit(solution)/shard_map/ppermute | solution.py:309
  16.3 18.2 %collective-permute-start.20 = (f32[192,256]{1,0:T(8,128)S(1)}, f32[192,256]{1,0:T(8,128)S(1)}, u32[]{:S(2)}, u32[]{:S(2)}) collective-permute-start(f32[192,256]{1,0:T(8,128)S(1)} %get-tuple-element.64.refs_1_.refs_4_), channel_id=1, source_target_pairs={{0,2},{4,6},{8,10},{12,14},{16,18},{20,22},{24,26},{28,30}} | collective-permute-start | bytes 589832 | tf_op jit(solution)/shard_map/ppermute | solution.py:309
  17.6 21.0 %collective-permute-start.1 = (f32[128,256]{1,0:T(8,128)S(1)}, f32[128,256]{1,0:T(8,128)S(1)}, u32[]{:S(2)}, u32[]{:S(2)}) collective-permute-start(f32[128,256]{1,0:T(8,128)S(1)} %shard_map.31.refs_0_), channel_id=1, source_target_pairs={{0,8},{1,5},{2,6},{3,7},{4,12},{5,1},{6,2},{7,3},{8,0},{9,13},{10,... | collective-permute-start | bytes 393224 | tf_op jit(solution)/shard_map/ppermute | solution.py:294
  20.7 19.2 %collective-permute-start.23 = (f32[192,256]{1,0:T(8,128)S(1)}, f32[192,256]{1,0:T(8,128)S(1)}, u32[]{:S(2)}, u32[]{:S(2)}) collective-permute-start(f32[192,256]{1,0:T(8,128)S(1)} %get-tuple-element.65.refs_5_), channel_id=1, source_target_pairs={{0,2},{4,6},{8,10},{12,14},{16,18},{20,22},{24,26},{28,30}} | collective-permute-start | bytes 589832 | tf_op jit(solution)/shard_map/ppermute | solution.py:309
  26.0 15.8 %collective-permute-start.26 = (f32[192,256]{1,0:T(8,128)S(1)}, f32[192,256]{1,0:T(8,128)S(1)}, u32[]{:S(2)}, u32[]{:S(2)}) collective-permute-start(f32[192,256]{1,0:T(8,128)S(1)} %get-tuple-element.66.refs_9_.refs_6_), channel_id=1, source_target_pairs={{0,2},{4,6},{8,10},{12,14},{16,18},{20,22},{24,26},{28,30}} | collective-permute-start | bytes 589832 | tf_op jit(solution)/shard_map/ppermute | solution.py:309
  30.2 15.8 %collective-permute-start.29 = (f32[192,256]{1,0:T(8,128)S(1)}, f32[192,256]{1,0:T(8,128)S(1)}, u32[]{:S(2)}, u32[]{:S(2)}) collective-permute-start(f32[192,256]{1,0:T(8,128)S(1)} %get-tuple-element.68.refs_1_.refs_7_), channel_id=1, source_target_pairs={{0,2},{4,6},{8,10},{12,14},{16,18},{20,22},{24,26},{28,30}} | collective-permute-start | bytes 589832 | tf_op jit(solution)/shard_map/ppermute | solution.py:309
  34.4 15.8 %collective-permute-start.32 = (f32[192,256]{1,0:T(8,128)S(1)}, f32[192,256]{1,0:T(8,128)S(1)}, u32[]{:S(2)}, u32[]{:S(2)}) collective-permute-start(f32[192,256]{1,0:T(8,128)S(1)} %get-tuple-element.69.refs_5_.refs_8_), channel_id=1, source_target_pairs={{0,2},{4,6},{8,10},{12,14},{16,18},{20,22},{24,26},{28,30}} | collective-permute-start | bytes 589832 | tf_op jit(solution)/shard_map/ppermute | solution.py:309
  38.6 15.3 %collective-permute-start.35 = (f32[192,256]{1,0:T(8,128)S(1)}, f32[192,256]{1,0:T(8,128)S(1)}, u32[]{:S(2)}, u32[]{:S(2)}) collective-permute-start(f32[192,256]{1,0:T(8,128)S(1)} %get-tuple-element.71.refs_1_.refs_9_), channel_id=1, source_target_pairs={{0,2},{4,6},{8,10},{12,14},{16,18},{20,22},{24,26},{28,30}} | collective-permute-start | bytes 589832 | tf_op jit(solution)/shard_map/ppermute | solution.py:309
  40.0 13.9 %collective-permute-start.2 = (f32[128,256]{1,0:T(8,128)S(1)}, f32[128,256]{1,0:T(8,128)S(1)}, u32[]{:S(2)}, u32[]{:S(2)}) collective-permute-start(f32[128,256]{1,0:T(8,128)S(1)} %shard_map.32.refs_0_), channel_id=1, source_target_pairs={{0,16},{1,5},{2,6},{3,7},{4,20},{5,1},{6,2},{7,3},{8,24},{9,13},{1... | collective-permute-start | bytes 393224 | tf_op jit(solution)/shard_map/ppermute | solution.py:294
  41.8 12.8 %collective-permute-start.10 = (f32[192,256]{1,0:T(8,128)S(1)}, f32[192,256]{1,0:T(8,128)S(1)}, u32[]{:S(2)}, u32[]{:S(2)}) collective-permute-start(f32[192,256]{1,0:T(8,128)S(1)} %collective-permute-done.8.refs_1_), channel_id=1, source_target_pairs={{2,1},{6,5},{10,9},{14,13},{18,17},{22,21},{26,25},{30,29}} | collective-permute-start | bytes 589832 | tf_op jit(solution)/shard_map/ppermute | solution.py:309
  46.0 9.2 %collective-permute-start.9 = (f32[192,256]{1,0:T(8,128)S(1)}, f32[192,256]{1,0:T(8,128)S(1)}, u32[]{:S(2)}, u32[]{:S(2)}) collective-permute-start(f32[192,256]{1,0:T(8,128)S(1)} %collective-permute-done.8.refs_1_), channel_id=1, source_target_pairs={{0,4},{1,5},{2,3},{3,2},{4,0},{5,1},{6,7},{7,6},{8,12},{9,13},{10,... | collective-permute-start | bytes 589832 | tf_op jit(solution)/shard_map/ppermute | solution.py:294
  50.2 5.7 %collective-permute-start.13 = (f32[192,256]{1,0:T(8,128)S(1)}, f32[192,256]{1,0:T(8,128)S(1)}, u32[]{:S(2)}, u32[]{:S(2)}) collective-permute-start(f32[192,256]{1,0:T(8,128)S(1)} %collective-permute-done.11.refs_5_), channel_id=1, source_target_pairs={{2,1},{6,5},{10,9},{14,13},{18,17},{22,21},{26,25},{30,29}} | collective-permute-start | bytes 589832 | tf_op jit(solution)/shard_map/ppermute | solution.py:309
  53.9 2.7 %collective-permute-start.16 = (f32[192,256]{1,0:T(8,128)S(1)}, f32[192,256]{1,0:T(8,128)S(1)}, u32[]{:S(2)}, u32[]{:S(2)}) collective-permute-start(f32[192,256]{1,0:T(8,128)S(1)} %collective-permute-done.14.refs_9_), channel_id=1, source_target_pairs={{2,1},{6,5},{10,9},{14,13},{18,17},{22,21},{26,25},{30,29}} | collective-permute-start | bytes 589832 | tf_op jit(solution)/shard_map/ppermute | solution.py:309
  60.0 27.9 %collective-permute-start.34 = (f32[192,256]{1,0:T(8,128)S(1)}, f32[192,256]{1,0:T(8,128)S(1)}, u32[]{:S(2)}, u32[]{:S(2)}) collective-permute-start(f32[192,256]{1,0:T(8,128)S(1)} %collective-permute-done.32.refs_6_), channel_id=1, source_target_pairs={{2,1},{6,5},{10,9},{14,13},{18,17},{22,21},{26,25},{30,29}} | collective-permute-start | bytes 589832 | tf_op jit(solution)/shard_map/ppermute | solution.py:309
  60.7 27.5 %collective-permute-start.33 = (f32[192,256]{1,0:T(8,128)S(1)}, f32[192,256]{1,0:T(8,128)S(1)}, u32[]{:S(2)}, u32[]{:S(2)}) collective-permute-start(f32[192,256]{1,0:T(8,128)S(1)} %collective-permute-done.32.refs_6_), channel_id=1, source_target_pairs={{0,4},{1,5},{2,3},{3,2},{4,0},{5,1},{6,7},{7,6},{8,12},{9,13},{10,... | collective-permute-start | bytes 589832 | tf_op jit(solution)/shard_map/ppermute | solution.py:294
  61.2 27.3 %collective-permute-start.37 = (f32[192,256]{1,0:T(8,128)S(1)}, f32[192,256]{1,0:T(8,128)S(1)}, u32[]{:S(2)}, u32[]{:S(2)}) collective-permute-start(f32[192,256]{1,0:T(8,128)S(1)} %collective-permute-done.35.refs_2_), channel_id=1, source_target_pairs={{2,1},{6,5},{10,9},{14,13},{18,17},{22,21},{26,25},{30,29}} | collective-permute-start | bytes 589832 | tf_op jit(solution)/shard_map/ppermute | solution.py:309
  61.9 26.7 %collective-permute-start.36 = (f32[192,256]{1,0:T(8,128)S(1)}, f32[192,256]{1,0:T(8,128)S(1)}, u32[]{:S(2)}, u32[]{:S(2)}) collective-permute-start(f32[192,256]{1,0:T(8,128)S(1)} %collective-permute-done.35.refs_2_), channel_id=1, source_target_pairs={{0,4},{1,5},{2,3},{3,2},{4,0},{5,1},{6,7},{7,6},{8,12},{9,13},{10,... | collective-permute-start | bytes 589832 | tf_op jit(solution)/shard_map/ppermute | solution.py:294
  62.0 29.3 %collective-permute-start.40 = (f32[128,256]{1,0:T(8,128)S(1)}, f32[128,256]{1,0:T(8,128)S(1)}, u32[]{:S(2)}, u32[]{:S(2)}) collective-permute-start(f32[128,256]{1,0:T(8,128)S(1)} %get-tuple-element.73.refs_1_.refs_10_), channel_id=1, source_target_pairs={{0,1},{4,5},{8,9},{12,13},{16,17},{20,21},{24,25},{28,29}} | collective-permute-start | bytes 393224 | tf_op jit(solution)/shard_map/ppermute | solution.py:309
  87.9 3.4 %collective-permute-start.39 = (f32[128,256]{1,0:T(8,128)S(1)}, f32[128,256]{1,0:T(8,128)S(1)}, u32[]{:S(2)}, u32[]{:S(2)}) collective-permute-start(f32[128,256]{1,0:T(8,128)S(1)} %collective-permute-done.38.refs_2_), channel_id=1, source_target_pairs={{0,4},{1,5},{2,3},{3,2},{4,0},{5,1},{6,7},{7,6},{8,12},{9,13},{10,... | collective-permute-start | bytes 393224 | tf_op jit(solution)/shard_map/ppermute | solution.py:294
  88.2 3.1 %collective-permute-start.3 = (f32[128,256]{1,0:T(8,128)S(1)}, f32[128,256]{1,0:T(8,128)S(1)}, u32[]{:S(2)}, u32[]{:S(2)}) collective-permute-start(f32[128,256]{1,0:T(8,128)S(1)} %shard_map.33.mine_ref), channel_id=1, source_target_pairs={{0,4},{1,5},{2,6},{3,7},{4,0},{5,1},{6,2},{7,3},{8,12},{9,13},{10,... | collective-permute-start | bytes 393224 | tf_op jit(solution)/shard_map/ppermute | solution.py:294
  91.3 18.8 %collective-permute-start.41 = (f32[128,256]{1,0:T(8,128)S(1)}, f32[128,256]{1,0:T(8,128)S(1)}, u32[]{:S(2)}, u32[]{:S(2)}) collective-permute-start(f32[128,256]{1,0:T(8,128)S(1)} %get-tuple-element.75), channel_id=1, source_target_pairs={{0,4},{1,5},{2,6},{3,7},{4,0},{5,1},{6,2},{7,3},{8,12},{9,13},{10,... | collective-permute-start | bytes 393224 | tf_op jit(solution)/shard_map/ppermute | solution.py:294
  106.1 5.2 %collective-permute-start.6 = (f32[128,256]{1,0:T(8,128)S(1)}, f32[128,256]{1,0:T(8,128)S(1)}, u32[]{:S(2)}, u32[]{:S(2)}) collective-permute-start(f32[128,256]{1,0:T(8,128)S(1)} %get-tuple-element.53), channel_id=1, source_target_pairs={{0,3},{4,7},{8,11},{12,15},{16,19},{20,23},{24,27},{28,31}} | collective-permute-start | bytes 393224 | tf_op jit(solution)/shard_map/ppermute | solution.py:309
  107.4 6.7 %collective-permute-start.5 = (f32[128,256]{1,0:T(8,128)S(1)}, f32[128,256]{1,0:T(8,128)S(1)}, u32[]{:S(2)}, u32[]{:S(2)}) collective-permute-start(f32[128,256]{1,0:T(8,128)S(1)} %get-tuple-element.53), channel_id=1, source_target_pairs={{0,1},{4,5},{8,9},{12,13},{16,17},{20,21},{24,25},{28,29}} | collective-permute-start | bytes 393224 | tf_op jit(solution)/shard_map/ppermute | solution.py:309
  108.8 8.0 %collective-permute-start.4 = (f32[128,256]{1,0:T(8,128)S(1)}, f32[128,256]{1,0:T(8,128)S(1)}, u32[]{:S(2)}, u32[]{:S(2)}) collective-permute-start(f32[128,256]{1,0:T(8,128)S(1)} %get-tuple-element.53), channel_id=1, source_target_pairs={{0,2},{4,6},{8,10},{12,14},{16,18},{20,22},{24,26},{28,30}} | collective-permute-start | bytes 393224 | tf_op jit(solution)/shard_map/ppermute | solution.py:309
  110.1 6.8 %collective-permute-start.44 = (f32[128,256]{1,0:T(8,128)S(1)}, f32[128,256]{1,0:T(8,128)S(1)}, u32[]{:S(2)}, u32[]{:S(2)}) collective-permute-start(f32[128,256]{1,0:T(8,128)S(1)} %shard_map.43.refs_0_), channel_id=1, source_target_pairs={{0,4},{1,25},{2,26},{3,27},{4,0},{5,29},{6,30},{7,31},{8,12},{9,17... | collective-permute-start | bytes 393224 | tf_op jit(solution)/shard_map/ppermute | solution.py:294
  110.7 6.2 %collective-permute-start.43 = (f32[128,256]{1,0:T(8,128)S(1)}, f32[128,256]{1,0:T(8,128)S(1)}, u32[]{:S(2)}, u32[]{:S(2)}) collective-permute-start(f32[128,256]{1,0:T(8,128)S(1)} %shard_map.43.refs_0_), channel_id=1, source_target_pairs={{0,4},{1,17},{2,18},{3,19},{4,0},{5,21},{6,22},{7,23},{8,12},{9,25... | collective-permute-start | bytes 393224 | tf_op jit(solution)/shard_map/ppermute | solution.py:294
  111.3 5.6 %collective-permute-start.42 = (f32[128,256]{1,0:T(8,128)S(1)}, f32[128,256]{1,0:T(8,128)S(1)}, u32[]{:S(2)}, u32[]{:S(2)}) collective-permute-start(f32[128,256]{1,0:T(8,128)S(1)} %shard_map.43.refs_0_), channel_id=1, source_target_pairs={{0,4},{1,9},{2,10},{3,11},{4,0},{5,13},{6,14},{7,15},{8,12},{9,1},... | collective-permute-start | bytes 393224 | tf_op jit(solution)/shard_map/ppermute | solution.py:294
  (14 other events, 32.4 us)
